TPU v7x, 32 devices: a whole 2x2x4 slice. The times are simulated.
32 devices in a mesh: gx: 8 (over z, x), gy: 4 (over y, core).
Axes of the slice: x: 2, y: 2, z: 4, core: 2. Of those that a mesh axis runs over, the one named last changes fastest.
Arguments:
- features: bfloat16 [128, 256, 512], P('gx', 'gy'), may hold values from -6 to 6
- cotangent: bfloat16 [128, 256, 512], P('gx', 'gy'), may hold values from -6 to 6
- low: int32 [128, 256], P('gx', 'gy'), may hold values from 0 to 7, as said below
- high: int32 [128, 256], P('gx', 'gy'), may hold values from 0 to 8, as said below
- weight_one: bfloat16 [27, 64, 64], replicated, may hold values from -0.4375 to 0.4375
- weight_two: bfloat16 [27, 64, 64], replicated, may hold values from -0.4375 to 0.4375
- scale_one: float32 [64], replicated, may hold values from 0.5 to 2
- shift_one: float32 [64], replicated, may hold values from -1.5 to 1.5
- scale_two: float32 [64], replicated, may hold values from 0.5 to 2
- shift_two: float32 [64], replicated, may hold values from -1.5 to 1.5
Outputs:
- output: bfloat16 [128, 256, 512], P('gx', 'gy')
- grad_features: bfloat16 [128, 256, 512], P('gx', 'gy')
- grad_weight_one: float32 [27, 64, 64], replicated
- grad_weight_two: float32 [27, 64, 64], replicated
Inputs may be any that keep to these rules, and one draw needn't show every extreme that they name: An empty column has low = high = 0; an occupied one has low < high. One device holds at most 4 filled bricks and some device holds exactly that many; the devices that share a gy index hold at most 2 filled bricks a device together, and some such group holds exactly that many. `high`: see low.
All inputs are finite; a program needn't handle non-finite values.
Results may differ from a plain program's by a relative error of at most 0.0071.
Values may be sent and summed in bfloat16 or wider, within the bound.
No kernel may reach another device: no remote copies, remote signals or barrier semaphores. Data moves between devices by JAX's collectives and lax.ppermute only.
A program may use at most 256 MiB of HBM per device.

v0:
```python
import functools

import jax
import jax.numpy as jnp
from jax import lax
from jax.experimental import pallas as pl
from jax.experimental.pallas import tpu as pltpu
from jax.sharding import PartitionSpec as P

BRICK = 8
ACT_MAX = 4
SHARE = 2
F32 = jnp.float32
BF16 = jnp.bfloat16


def shifted_in(array, axis, by):
    devices = lax.axis_size(axis)
    pairs = [(i, i + by) for i in range(devices) if 0 <= i + by < devices]
    return lax.ppermute(array, axis, pairs)


def flat_permute(array, move):
    nx, ny = lax.axis_size("gx"), lax.axis_size("gy")
    pairs = []
    for x in range(nx):
        for y in range(ny):
            to = move(x, y)
            if to is not None:
                pairs.append((x * ny + y, to[0] * ny + to[1]))
    return lax.ppermute(array, ("gx", "gy"), pairs)


def low_lanes(shape):
    return lax.broadcasted_iota(jnp.int32, shape, len(shape) - 1) < 64


def turn(value):
    return pltpu.roll(value, 64, value.ndim - 1)


def to_shifted(pairs):
    turned = [turn(v) for v in pairs]
    low = low_lanes(pairs[0].shape)
    zero = jnp.zeros_like(pairs[0])
    before = [zero] + turned
    after = turned + [zero]
    return [jnp.where(low, b, a) for b, a in zip(before, after)]


def to_aligned(shifted):
    turned = [turn(v) for v in shifted]
    low = low_lanes(shifted[0].shape)
    return [jnp.where(low, turned[m], turned[m + 1]) for m in range(len(shifted) - 1)]


VMEM = pl.BlockSpec(memory_space=pltpu.VMEM)
SMEM = pl.BlockSpec(memory_space=pltpu.SMEM)
shape = jax.ShapeDtypeStruct


def decoded(code):
    floor = jnp.floor(code * (1.0 / 16.0))
    return floor, code - 16.0 * floor


def mask_of(bounds, z_low):
    z = jnp.where(low_lanes((1, 128)), 1.0 * z_low, z_low + 1.0)
    return (z >= bounds[0]) & (z < bounds[1])


def edge_kernel(features, low, high, packed, top, bottom, first, last):
    lx, ly = low.shape
    code = (low[...] * 16 + high[...]).astype(F32)
    same = lax.broadcasted_iota(jnp.int32, (ly, ly), 0) == lax.broadcasted_iota(
        jnp.int32, (ly, ly), 1
    )
    ones = jnp.ones((ly, 128), BF16)
    low_row = low_lanes((1, 128))
    for x in range(lx):
        spread = jnp.where(same, code[x : x + 1, :], 0.0).astype(BF16)
        column = jnp.dot(spread, ones, preferred_element_type=F32)
        bounds = decoded(column)
        pieces = []
        for m in range(4):
            v = features[x, :, 128 * m : 128 * m + 128].astype(F32)
            pieces.append(jnp.where(mask_of(bounds, 2 * m), v, 0.0))
        for p, v in enumerate(to_shifted(pieces)):
            if p == 0:
                v = jnp.where(low_row, column, v)
            lanes = slice(128 * p, 128 * p + 128)
            v16 = v.astype(BF16)
            packed[x, :, lanes] = v16
            if x < 2:
                top[x, :, lanes] = v16
            if x >= lx - 2:
                bottom[x - (lx - 2), :, lanes] = v16
            first[x, :, lanes] = v[0:2].astype(BF16)
            last[x, :, lanes] = v[ly - 2 : ly].astype(BF16)


def edge_call(features, low, high):
    lx, ly, width = features.shape
    wide = width + 128
    return pl.pallas_call(
        edge_kernel,
        out_shape=(
            shape((lx, ly, wide), BF16),
            shape((2, ly, wide), BF16),
            shape((2, ly, wide), BF16),
            shape((lx, 2, wide), BF16),
            shape((lx, 2, wide), BF16),
        ),
        in_specs=[VMEM] * 3,
        out_specs=(VMEM,) * 5,
        name="edges",
    )(features, low, high)


def side_kernel(above, below, first, last, to_left, to_right):
    lx = first.shape[0]
    ly = above.shape[1]
    for strip, base in ((above, 0), (below, lx + 2)):
        for x in range(2):
            v = strip[x].astype(F32)
            to_left[base + x] = v[0:2].astype(BF16)
            to_right[base + x] = v[ly - 2 : ly].astype(BF16)
    to_left[2 : lx + 2] = first[...]
    to_right[2 : lx + 2] = last[...]


def side_call(above, below, first, last):
    tall = (first.shape[0] + 4,) + first.shape[1:]
    return pl.pallas_call(
        side_kernel,
        out_shape=(shape(tall, BF16), shape(tall, BF16)),
        in_specs=[VMEM] * 4,
        out_specs=(VMEM, VMEM),
        name="sides",
    )(above, below, first, last)


def tile_kernel(low, high, weight_one, weight_two, slots, tiles, tiles_last):
    lx, ly = low.shape
    filled = jnp.where(high[...] > low[...], 1.0, 0.0)
    rows = [
        jnp.sum(filled[8 * i : 8 * i + 8], axis=0, keepdims=True) for i in range(lx // BRICK)
    ]
    rows = jnp.concatenate(rows + [jnp.zeros((8 - len(rows), ly), F32)], axis=0)
    among = lax.broadcasted_iota(jnp.int32, (ly, 128), 0) // BRICK
    among = among == lax.broadcasted_iota(jnp.int32, (ly, 128), 1)
    counts = jnp.dot(
        rows.astype(BF16), jnp.where(among, 1.0, 0.0).astype(BF16), preferred_element_type=F32
    )
    for i in range(3 * ACT_MAX):
        slots[i] = 0
    r = lax.broadcasted_iota(jnp.int32, (8, 128), 0)
    c = lax.broadcasted_iota(jnp.int32, (8, 128), 1)
    flags = [
        jnp.sum(jnp.where((r == i) & (c == j), counts, 0.0))
        for i in range(lx // BRICK)
        for j in range(ly // BRICK)
    ]
    seat = jnp.int32(0)
    for n, flag in enumerate(flags):
        i, j = n // (ly // BRICK), n % (ly // BRICK)
        has = (flag > 0.5) & (seat < ACT_MAX)

        @pl.when(has)
        def _(seat=seat, i=i, j=j):
            slots[seat] = i
            slots[ACT_MAX + seat] = j
            slots[2 * ACT_MAX + seat] = 1

        seat = seat + has.astype(jnp.int32)

    zero = jnp.zeros((64, 64), BF16)
    for conv, weight in enumerate((weight_one, weight_two, weight_two, weight_one)):
        for tap in range(9):
            taps = []
            for oz in range(3):
                if conv < 2:
                    taps.append(weight[3 * tap + oz])
                else:
                    taps.append(weight[26 - 3 * tap - oz].astype(F32).T.astype(BF16))
            taps = [zero] + taps + [zero]
            for d in range(4):
                tile = jnp.concatenate([taps[d + 1], taps[d]], axis=1)
                if conv < 3:
                    tiles[conv, tap, d] = tile
                else:
                    tiles_last[tap, d] = tile


def tile_call(low, high, weight_one, weight_two):
    return pl.pallas_call(
        tile_kernel,
        out_shape=(
            shape((3 * ACT_MAX,), jnp.int32),
            shape((3, 9, 4, 64, 128), BF16),
            shape((9, 4, 64, 128), BF16),
        ),
        in_specs=[VMEM] * 4,
        out_specs=(SMEM, VMEM, VMEM),
        name="tiles",
    )(low, high, weight_one, weight_two)


def build_bands(bands, tile_at):
    bands[...] = jnp.zeros(bands.shape, BF16)
    for ox in range(3):
        for oy in range(3):
            for r in range(6):
                for q in range(2):
                    d = r - 2 * q
                    if 0 <= d < 4:
                        row = ((r // 2) * 3 + oy) * 128 + (r % 2) * 64
                        bands[ox, row : row + 64, 128 * q : 128 * q + 128] = tile_at(
                            ox * 3 + oy, d
                        )


def convolve(source, bands, acc, xs):
    rows = source.shape[0] * xs * 16
    for half in range(2):
        total = None
        for ox in range(3):
            part = source[:, ox : ox + xs, :, 768 * half : 768 * half + 1152]
            part = jnp.dot(part.reshape(rows, 1152), bands[ox], preferred_element_type=F32)
            total = part if total is None else total + part
        acc[0:rows, 256 * half : 256 * half + 256] = total


def place(slots, s):
    x0 = pl.multiple_of(slots[s] * 8, 8)
    y0 = pl.multiple_of(slots[ACT_MAX + s] * 8, 8)
    return x0, y0, slots[2 * ACT_MAX + s]


def twice(row):
    return jnp.concatenate([row, row], axis=1)


def brick_kernel(
    slots, core, packed, above, below, left, right, cotangent, tiles, s_one, t_one, s_two, t_two,
    out, errors_out, grads_out, keep, send,
    fx, ms, bands_a, bands_b, bands_c, c1, c2, c3, acc, slope, h, e2, er2, ets, et1, folded, total,
):
    lx, ly = out.shape[0], out.shape[1]
    low_row = low_lanes((1, 128))
    scale_one, shift_one = twice(s_one[...]), twice(t_one[...])
    scale_two, shift_two = twice(s_two[...]), twice(t_two[...])

    build_bands(bands_a, lambda t, d: tiles[0, t, d])

    def put(x, strip, start, stop):
        for p in range(5):
            v = strip(p).astype(F32)
            if p == 0:
                bounds = decoded(jnp.where(low_row, v, turn(v)))
                v = jnp.where(low_row, 0.0, v)
                for m in range(4):
                    ms[m, x, start:stop, :] = jnp.where(mask_of(bounds, 2 * m), 1.0, 0.0)
            fx[p, x, start:stop, :] = v

    def own_row(i, _):
        for k in range(2):
            x = 2 * i + k
            put(x + 2, lambda p: packed[x, :, 128 * p : 128 * p + 128], 8, 8 + ly)
            out[x] = jnp.zeros(out.shape[1:], BF16)
        return 0

    lax.fori_loop(0, lx // 2, own_row, 0)
    for x in range(2):
        put(x, lambda p: above[x, :, 128 * p : 128 * p + 128], 8, 8 + ly)
        put(lx + 2 + x, lambda p: below[x, :, 128 * p : 128 * p + 128], 8, 8 + ly)

    def side_row(i, _):
        for k in range(4):
            x = 4 * i + k
            for base in (0, 8 + ly):
                for m in range(4):
                    ms[m, x, base : base + 8, :] = jnp.zeros((8, 128), F32)
                for p in range(5):
                    fx[p, x, base : base + 8, :] = jnp.zeros((8, 128), F32)
            put(x, lambda p: left[x, :, 128 * p : 128 * p + 128], 6, 8)
            put(x, lambda p: right[x, :, 128 * p : 128 * p + 128], 8 + ly, 10 + ly)
        return 0

    lax.fori_loop(0, (lx + 4) // 4, side_row, 0)

    def gather_one(s, _):
        x0, y0, live = place(slots, s)
        for p in range(5):
            view = fx.at[p, pl.ds(x0, 12), pl.ds(y0, 24), :]
            for oy in range(3):
                lane = (p * 3 + oy) * 128
                c1[s, :, :, lane : lane + 128] = view[:, 6 + oy : 22 + oy, :].astype(BF16)
        return 0

    lax.fori_loop(0, ACT_MAX, gather_one, 0)
    build_bands(bands_b, lambda t, d: tiles[1, t, d])
    convolve(c1, bands_a, acc, 10)

    def hidden_of(i, _):
        s = i // 2
        x0, y0, live = place(slots, s)
        keep_rows = lax.broadcasted_iota(jnp.int32, (16, 128), 0) < jnp.where(live > 0, 10, 0)
        for k in range(5):
            x = (i % 2) * 5 + k
            at = pl.multiple_of((s * 10 + x) * 16, 16)
            pieces = []
            for m in range(4):
                lanes = slice(128 * m, 128 * m + 128)
                mask = ms.at[m, x0 + x + 1, pl.ds(y0, 24), :][7:23, :]
                mask = jnp.where(keep_rows, mask, 0.0)
                pre = acc[pl.ds(at, 16), lanes] * scale_one + shift_one
                sig = 1.0 / (1.0 + jnp.exp(-pre))
                pieces.append(pre * sig * mask)
                slope[pl.ds(at, 16), lanes] = (
                    scale_one * mask * (sig * (1.0 + pre * (1.0 - sig)))
                )
            for p, v in enumerate(to_shifted(pieces)):
                h[s, p, x] = v
        return 0

    lax.fori_loop(0, 2 * ACT_MAX, hidden_of, 0)

    def gather_two(q, _):
        for p in range(5):
            for oy in range(3):
                lane = (p * 3 + oy) * 128
                one = h[2 * q, p, :, oy : oy + 8, :]
                two = h[2 * q + 1, p, :, oy : oy + 8, :]
                c2[q, :, :, lane : lane + 128] = jnp.concatenate([one, two], axis=1).astype(BF16)
        return 0

    lax.fori_loop(0, ACT_MAX // 2, gather_two, 0)
    build_bands(bands_c, lambda t, d: tiles[2, t, d])
    convolve(c2, bands_b, acc, 8)

    def finish_two(s, _):
        x0, y0, live = place(slots, s)
        odd = lax.rem(slots[ACT_MAX + s], 2) == 1
        y16 = pl.multiple_of(slots[ACT_MAX + s] // 2 * 16, 16)
        alive = jnp.where(live > 0, 1.0, 0.0)
        zero = jnp.zeros((8, 128), F32)
        for p in range(5):
            for x in (0, 1, 10, 11):
                e2[s, p, x] = jnp.zeros((24, 128), F32)
        for x in range(8):
            at = pl.multiple_of(((s // 2) * 8 + x) * 16 + (s % 2) * 8, 8)
            centre = to_aligned([fx[p, x0 + 2 + x, pl.ds(y0 + 8, 8), :] for p in range(5)])
            errors = []
            for m in range(4):
                lanes = slice(128 * m, 128 * m + 128)
                mask = ms[m, x0 + 2 + x, pl.ds(y0 + 8, 8), :] * alive
                pre = acc[pl.ds(at, 8), lanes] * scale_two + shift_two + centre[m]
                sig = 1.0 / (1.0 + jnp.exp(-pre))
                result = pre * sig * mask
                both = cotangent[x0 + x, pl.ds(y16, 16), lanes].astype(F32)
                target = jnp.where(odd, both[8:16], both[0:8])
                grad = target * mask * (sig * (1.0 + pre * (1.0 - sig)))
                error = grad * scale_two
                errors.append(error)
                er2[pl.ds(at, 8), lanes] = error
                grads_out[s, x, :, lanes] = grad
                result = jnp.where(
                    odd,
                    jnp.concatenate([zero, result], axis=0),
                    jnp.concatenate([result, zero], axis=0),
                )
                now = out[x0 + x, pl.ds(y16, 16), lanes].astype(F32)
                out[x0 + x, pl.ds(y16, 16), lanes] = (now + result).astype(BF16)
            for p, v in enumerate(to_shifted(errors)):
                e2[s, p, x + 2, 0:8, :] = zero
                e2[s, p, x + 2, 8:16, :] = v
                e2[s, p, x + 2, 16:24, :] = zero
        return 0

    lax.fori_loop(0, ACT_MAX, finish_two, 0)

    def gather_three(s, _):
        for p in range(5):
            for oy in range(3):
                lane = (p * 3 + oy) * 128
                c3[s, :, :, lane : lane + 128] = e2[s, p, :, 6 + oy : 22 + oy, :].astype(BF16)
        return 0

    lax.fori_loop(0, ACT_MAX, gather_three, 0)
    ets[0:128] = jnp.zeros((128, ets.shape[1]), BF16)
    ets[640:768] = jnp.zeros((128, ets.shape[1]), BF16)
    ets[128:640] = er2[...].astype(BF16).T
    convolve(c3, bands_c, acc, 10)

    def finish_three(i, _):
        for k in range(4):
            at = pl.multiple_of((i * 4 + k) * 16, 16)
            for m in range(4):
                lanes = slice(128 * m, 128 * m + 128)
                error = acc[pl.ds(at, 16), lanes] * slope[pl.ds(at, 16), lanes]
                errors_out[pl.ds(at, 16), lanes] = error.astype(BF16)
        return 0

    lax.fori_loop(0, ACT_MAX * 10 // 4, finish_three, 0)

    def weight_sums(source, errors_t, xs, which):
        rows = source.shape[0] * xs * 16
        for ox in range(3):
            sums = None
            for p in range(5):
                part = source[:, ox : ox + xs, :, 384 * p : 384 * p + 384].reshape(rows, 384)
                part = jnp.dot(
                    errors_t[128 * p : 128 * p + 256, :], part, preferred_element_type=F32
                )
                sums = part if sums is None else sums + part
            for oy in range(3):
                block = sums[:, 128 * oy : 128 * oy + 128]
                turned = turn(block)
                for oz in range(3):
                    one, two = 64 * (2 - oz), 64 * (3 - oz)
                    n = ox * 9 + oy * 3 + oz
                    if which == 0:
                        folded[n] = block[one : one + 64] + turned[two : two + 64]
                    else:
                        v = turned[one : one + 64] + block[two : two + 64]
                        total[n] = jnp.where(low_row, folded[n], v).astype(BF16)

    et1[0:128] = jnp.zeros((128, et1.shape[1]), BF16)
    et1[640:768] = jnp.zeros((128, et1.shape[1]), BF16)
    et1[128:640] = errors_out[...].T
    weight_sums(c1, et1, 10, 0)
    weight_sums(c2, ets, 8, 1)
    total[27] = jnp.zeros((64, 128), BF16)
    mine = core[0] * 14
    keep[...] = total[pl.ds(mine, 14)]
    send[...] = total[pl.ds(14 - mine, 14)]


def brick_call(slots, core, packed, above, below, left, right, cotangent, tiles, *vectors):
    lx, ly, width = cotangent.shape
    n = ACT_MAX
    wide = ly + 16
    return pl.pallas_call(
        brick_kernel,
        out_shape=(
            shape((lx, ly, width), BF16),
            shape((n * 160, width), BF16),
            shape((n, 8, 8, width), F32),
            shape((14, 64, 128), BF16),
            shape((14, 64, 128), BF16),
        ),
        in_specs=[SMEM, SMEM] + [VMEM] * 11,
        out_specs=(VMEM,) * 5,
        scratch_shapes=[
            pltpu.VMEM((5, lx + 4, wide, 128), F32),
            pltpu.VMEM((4, lx + 4, wide, 128), F32),
            pltpu.VMEM((3, 1152, 256), BF16),
            pltpu.VMEM((3, 1152, 256), BF16),
            pltpu.VMEM((3, 1152, 256), BF16),
            pltpu.VMEM((n, 12, 16, 1920), BF16),
            pltpu.VMEM((n // 2, 10, 16, 1920), BF16),
            pltpu.VMEM((n, 12, 16, 1920), BF16),
            pltpu.VMEM((n * 160, width), F32),
            pltpu.VMEM((n * 160, width), F32),
            pltpu.VMEM((n, 5, 10, 16, 128), F32),
            pltpu.VMEM((n, 5, 12, 24, 128), F32),
            pltpu.VMEM((n * 64, width), F32),
            pltpu.VMEM((768, n * 64), BF16),
            pltpu.VMEM((768, n * 160), BF16),
            pltpu.VMEM((27, 64, 128), F32),
            pltpu.VMEM((28, 64, 128), BF16),
        ],
        name="bricks",
    )(slots, core, packed, above, below, left, right, cotangent, tiles, *vectors)


def input_kernel(
    slots, errors, grads, codes, tiles, grad_own, grad_left, grad_right, e1, c4, bands, acc, grid
):
    lx, ly = grad_own.shape[0] - 4, grad_own.shape[1]
    wide = grid.shape[2]
    build_bands(bands, lambda t, d: tiles[t, d])

    def clear_row(i, _):
        for k in range(2):
            for m in range(4):
                grid[m, 2 * i + k] = jnp.zeros((wide, 128), F32)
        return 0

    lax.fori_loop(0, (lx + 4) // 2, clear_row, 0)

    def spread(s, _):
        for p in range(5):
            for x in (0, 1, 12, 13):
                e1[p, x] = jnp.zeros((24, 128), F32)
        for x in range(10):
            at = pl.multiple_of((s * 10 + x) * 16, 16)
            rows = [
                errors[pl.ds(at, 16), 128 * m : 128 * m + 128].astype(F32) for m in range(4)
            ]
            for p, v in enumerate(to_shifted(rows)):
                e1[p, x + 2, 0:8, :] = jnp.zeros((8, 128), F32)
                e1[p, x + 2, 8:24, :] = v
        for p in range(5):
            for oy in range(3):
                lane = (p * 3 + oy) * 128
                c4[s, :, :, lane : lane + 128] = e1[p, :, 6 + oy : 22 + oy, :].astype(BF16)
        return 0

    lax.fori_loop(0, ACT_MAX, spread, 0)
    convolve(c4, bands, acc, 12)

    def finish(s, _):
        x0, y0, live = place(slots, s)
        for x in range(12):
            at = pl.multiple_of((s * 12 + x) * 16, 16)
            for m in range(4):
                lanes = slice(128 * m, 128 * m + 128)
                view = grid.at[m, x0 + x, pl.ds(y0, 24), :]
                view[6:22, :] = view[6:22, :] + acc[pl.ds(at, 16), lanes]
        for x in range(8):
            for m in range(4):
                lanes = slice(128 * m, 128 * m + 128)
                view = grid.at[m, x0 + 2 + x, pl.ds(y0 + 8, 8), :]
                view[...] = view[...] + grads[s, x, :, lanes]
        return 0

    lax.fori_loop(0, ACT_MAX, finish, 0)

    def write_row(x, inside):
        low_row = low_lanes((1, 128))
        if inside:
            v = codes[x - 2].astype(F32)
            bounds = decoded(jnp.where(low_row, v, turn(v)))
        for m in range(4):
            lanes = slice(128 * m, 128 * m + 128)
            v = grid[m, x, 8 : 8 + ly, :]
            if inside:
                v = jnp.where(mask_of(bounds, 2 * m), v, 0.0)
            grad_own[x, :, lanes] = v.astype(BF16)
            grad_left[x, :, lanes] = grid[m, x, 6:8, :].astype(BF16)
            grad_right[x, :, lanes] = grid[m, x, 8 + ly : 10 + ly, :].astype(BF16)

    def own_rows(i, _):
        for k in range(2):
            write_row(2 + 2 * i + k, True)
        return 0

    lax.fori_loop(0, lx // 2, own_rows, 0)
    for x in (0, 1, lx + 2, lx + 3):
        write_row(x, False)


def input_call(slots, errors, grads, packed, tiles):
    lx, ly, wide = packed.shape
    width = wide - 128
    n = ACT_MAX
    return pl.pallas_call(
        input_kernel,
        out_shape=(
            shape((lx + 4, ly, width), BF16),
            shape((lx + 4, 2, width), BF16),
            shape((lx + 4, 2, width), BF16),
        ),
        grid=(1,),
        in_specs=[
            SMEM,
            VMEM,
            VMEM,
            pl.BlockSpec((lx, ly, 128), lambda i: (0, 0, 0)),
            VMEM,
        ],
        out_specs=(VMEM,) * 3,
        scratch_shapes=[
            pltpu.VMEM((5, 14, 24, 128), F32),
            pltpu.VMEM((n, 14, 16, 1920), BF16),
            pltpu.VMEM((3, 1152, 256), BF16),
            pltpu.VMEM((n * 192, width), F32),
            pltpu.VMEM((4, lx + 4, ly + 16, 128), F32),
        ],
        name="inputs",
    )(slots, errors, grads, packed, tiles)


def ends_kernel(above, below, from_left, from_right, top, bottom):
    ly = above.shape[1]
    lx = from_left.shape[0] - 4
    for source, base, target in ((above, 0, top), (below, lx + 2, bottom)):
        for x in range(2):
            v = source[x].astype(F32)
            one = jnp.concatenate(
                [from_left[base + x].astype(F32), jnp.zeros((6, v.shape[1]), F32)], axis=0
            )
            two = jnp.concatenate(
                [jnp.zeros((6, v.shape[1]), F32), from_right[base + x].astype(F32)], axis=0
            )
            v = jnp.concatenate([v[0:8] + one, v[8 : ly - 8], v[ly - 8 : ly] + two], axis=0)
            target[x] = v.astype(BF16)


def ends_call(grads, from_left, from_right):
    lx4, ly, width = grads.shape
    half = lx4 // 2 - 1
    return pl.pallas_call(
        ends_kernel,
        out_shape=(shape((2, ly, width), BF16), shape((2, ly, width), BF16)),
        grid=(1,),
        in_specs=[
            pl.BlockSpec((2, ly, width), lambda i: (0, 0, 0)),
            pl.BlockSpec((2, ly, width), lambda i: (half, 0, 0)),
            VMEM,
            VMEM,
        ],
        out_specs=(VMEM, VMEM),
        name="ends",
    )(grads, grads, from_left, from_right)


def join_kernel(grads, codes, from_left, from_right, from_above, from_below, grad_features):
    lx, ly = grad_features.shape[0], grad_features.shape[1]
    low_row = low_lanes((1, 128))

    def row(x, extra):
        code = codes[x].astype(F32)
        bounds = decoded(jnp.where(low_row, code, turn(code)))
        for m in range(4):
            lanes = slice(128 * m, 128 * m + 128)
            v = grads[x + 2, :, lanes].astype(F32)
            zero = jnp.zeros((6, 128), F32)
            one = jnp.concatenate([from_left[x + 2, :, lanes].astype(F32), zero], axis=0)
            two = jnp.concatenate([zero, from_right[x + 2, :, lanes].astype(F32)], axis=0)
            v = jnp.concatenate([v[0:8] + one, v[8 : ly - 8], v[ly - 8 : ly] + two], axis=0)
            if extra is not None:
                v = v + extra[0][extra[1], :, lanes].astype(F32)
            grad_features[x, :, lanes] = jnp.where(mask_of(bounds, 2 * m), v, 0.0).astype(BF16)

    def inner(i, _):
        for k in range(2):
            row(2 + 2 * i + k, None)
        return 0

    lax.fori_loop(0, (lx - 4) // 2, inner, 0)
    for x in range(2):
        row(x, (from_above, x))
        row(lx - 2 + x, (from_below, x))


def join_call(grads, packed, from_left, from_right, from_above, from_below):
    lx4, ly, width = grads.shape
    lx = lx4 - 4
    return pl.pallas_call(
        join_kernel,
        out_shape=shape((lx, ly, width), BF16),
        grid=(1,),
        in_specs=[VMEM, pl.BlockSpec((lx, ly, 128), lambda i: (0, 0, 0))] + [VMEM] * 4,
        out_specs=VMEM,
        name="join",
    )(grads, packed, from_left, from_right, from_above, from_below)


def pair_kernel(member, keep, got, *parts):
    for o, part in enumerate(parts):
        at = member[0] ^ o
        part[...] = (keep[at].astype(F32) + got[at].astype(F32)).astype(BF16)


def pair_call(member, keep, got, count):
    rows = keep.shape[0] * keep.shape[1] // count
    keep, got = keep.reshape(count, rows, 128), got.reshape(count, rows, 128)
    return pl.pallas_call(
        pair_kernel,
        out_shape=tuple(shape((rows, 128), BF16) for _ in range(count)),
        in_specs=[SMEM, VMEM, VMEM],
        out_specs=(VMEM,) * count,
        name="pair",
    )(member, keep, got)


def seat_kernel(member, *refs):
    parts, whole = refs[:-1], refs[-1]
    for o, part in enumerate(parts):
        whole[member[0] ^ o] = part[...]


def seat_call(member, parts):
    rows = parts[0].shape[0]
    return pl.pallas_call(
        seat_kernel,
        out_shape=shape((len(parts), rows, 128), BF16),
        in_specs=[SMEM] + [VMEM] * len(parts),
        out_specs=VMEM,
        name="seat",
    )(member, *parts)


def sums_kernel(core, mine, other, grad_one, grad_two, both, *, scale):
    both[core[0]] = mine[...]
    both[1 - core[0]] = other[...]
    for n in range(27):
        v = both[n // 14, n % 14].astype(F32).T * scale
        grad_one[n] = v[0:64]
        grad_two[n] = v[64:128]


def sums_call(core, mine, other, scale):
    return pl.pallas_call(
        functools.partial(sums_kernel, scale=scale),
        out_shape=(shape((27, 64, 64), F32), shape((27, 64, 64), F32)),
        in_specs=[SMEM, VMEM, VMEM],
        out_specs=(VMEM, VMEM),
        scratch_shapes=[pltpu.VMEM((2, 14, 64, 128), BF16)],
        name="sums",
    )(core, mine, other)


def reduce_sums(keep, send):
    nx, ny = lax.axis_size("gx"), lax.axis_size("gy")
    gx, gy = lax.axis_index("gx"), lax.axis_index("gy")
    core = (gy % 2).reshape(1)
    lines = ny // 2
    near = max(nx // 4, 1)
    far = nx // near

    got = flat_permute(send, lambda x, y: (x, y ^ 1))
    count = lines * near
    member = ((gy // 2) * near + gx % near).reshape(1)

    def in_plane(o):
        def move(x, y):
            to = ((y // 2) * near + x % near) ^ o
            return (x // near * near + to % near, to // near * 2 + y % 2)

        return move

    def along(o):
        return lambda x, y: (((x // near) ^ o) * near + x % near, y)

    parts = pair_call(member, keep, got, count)
    own = parts[0].astype(F32)
    for o in range(1, count):
        own = own + flat_permute(parts[o], in_plane(o)).astype(F32)
    own = own.astype(BF16)
    values = [own.astype(F32)] + [flat_permute(own, along(o)).astype(F32) for o in range(1, far)]
    while len(values) > 1:
        values = [values[i] + values[i + 1] for i in range(0, len(values), 2)]
    own = values[0].astype(BF16)
    others = [flat_permute(own, in_plane(o)) for o in range(1, count)]
    half = seat_call(member, [own] + others).reshape(keep.shape)
    other = flat_permute(half, lambda x, y: (x, y ^ 1))
    return core, half, other


def shards(
    features, cotangent, low, high, weight_one, weight_two, scale_one, shift_one, scale_two,
    shift_two,
):
    packed, top, bottom, first, last = edge_call(features, low, high)
    above = shifted_in(bottom, "gx", 1)
    below = shifted_in(top, "gx", -1)
    slots, tiles, tiles_last = tile_call(low, high, weight_one, weight_two)
    to_left, to_right = side_call(above, below, first, last)
    left = shifted_in(to_right, "gy", 1)
    right = shifted_in(to_left, "gy", -1)
    core = (lax.axis_index("gy") % 2).reshape(1)
    vectors = [v.reshape(1, -1) for v in (scale_one, shift_one, scale_two, shift_two)]
    out, errors, grads, keep, send = brick_call(
        slots, core, packed, above, below, left, right, cotangent, tiles, *vectors
    )
    core, half, other = reduce_sums(keep, send)
    grads, grad_left, grad_right = input_call(slots, errors, grads, packed, tiles_last)
    from_right = shifted_in(grad_left, "gy", -1)
    from_left = shifted_in(grad_right, "gy", 1)
    top, bottom = ends_call(grads, from_left, from_right)
    from_below = shifted_in(top, "gx", -1)
    from_above = shifted_in(bottom, "gx", 1)
    grad_features = join_call(grads, packed, from_left, from_right, from_above, from_below)
    capacity = lax.axis_size("gx") * lax.axis_size("gy") * SHARE
    grad_one, grad_two = sums_call(core, half, other, 1.0 / capacity)
    return (out, grad_features, grad_one, grad_two)


def solution(mesh):
    whole = P("gx", "gy", None)
    columns = P("gx", "gy")
    return jax.shard_map(
        shards,
        mesh=mesh,
        in_specs=(whole, whole, columns, columns) + (P(),) * 6,
        out_specs=(whole, whole, P(), P()),
        check_vma=False,
    )
```

profile of v0, /device:TPU:17, one launch (start us, length us, event | category | flops | bytes accessed | tf_op | source)
XLA Modules:
  0.0 115.0 jit_solution(511258601114425896)
XLA Ops:
  0.6 3.3 %edges.1 = (bf16[16,64,640]{2,1,0:T(8,128)(2,1)}, bf16[2,64,640]{2,1,0:T(8,128)(2,1)}, bf16[2,64,640]{2,1,0:T(8,128)(2,1)}, bf16[16,2,640]{2,1,0:T(2,128)(2,1)}, bf16[16,2,640]{2,1,0:T(2,128)(2,1)}) custom-call(bf16[16,64,512]{2,1,0:T(8,128)(2,1)} %features.1, s32[16,64]{1,0:T(8,128)} %low.3, s32[16,64]{1,0:T(8,128)} %high.3), custom_call_target="tpu_custom_call" | custom-call | tf_op jit(solution)/shard_map/edges/pallas_call | solution.py:105
  3.9 3.1 %collective-permute-start = (bf16[2,64,640]{2,1,0:T(8,128)(2,1)}, bf16[2,64,640]{2,1,0:T(8,128)(2,1)S(1)}, u32[]{:S(2)}, u32[]{:S(2)}) collective-permute-start(bf16[2,64,640]{2,1,0:T(8,128)(2,1)} %get-tuple-element.32), channel_id=1, source_target_pairs={{0,4},{4,8},{8,12},{12,16},{16,20},{20,24},{24,28},{1,5},{5,9},{9,... | collective-permute-start | bytes 491528 | tf_op jit(solution)/shard_map/ppermute | solution.py:20
  7.0 3.1 %collective-permute-start.1 = (bf16[2,64,640]{2,1,0:T(8,128)(2,1)}, bf16[2,64,640]{2,1,0:T(8,128)(2,1)S(1)}, u32[]{:S(2)}, u32[]{:S(2)}) collective-permute-start(bf16[2,64,640]{2,1,0:T(8,128)(2,1)} %get-tuple-element.33), channel_id=1, source_target_pairs={{4,0},{8,4},{12,8},{16,12},{20,16},{24,20},{28,24},{5,1},{9,5},{13... | collective-permute-start | bytes 491528 | tf_op jit(solution)/shard_map/ppermute | solution.py:20
  10.1 1.9 %collective-permute-done.above = bf16[2,64,640]{2,1,0:T(8,128)(2,1)S(1)} collective-permute-done((bf16[2,64,640]{2,1,0:T(8,128)(2,1)}, bf16[2,64,640]{2,1,0:T(8,128)(2,1)S(1)}, u32[]{:S(2)}, u32[]{:S(2)}) %collective-permute-start) | collective-permute-done | bytes 163872 | tf_op jit(solution)/shard_map/ppermute | solution.py:20
  12.0 4.5 %collective-permute-done.1.below = bf16[2,64,640]{2,1,0:T(8,128)(2,1)S(1)} collective-permute-done((bf16[2,64,640]{2,1,0:T(8,128)(2,1)}, bf16[2,64,640]{2,1,0:T(8,128)(2,1)S(1)}, u32[]{:S(2)}, u32[]{:S(2)}) %collective-permute-start.1) | collective-permute-done | bytes 163872 | tf_op jit(solution)/shard_map/ppermute | solution.py:20
  16.5 0.7 copy-done.1
  17.2 1.7 %sides.1 = (bf16[20,2,640]{2,1,0:T(2,128)(2,1)}, bf16[20,2,640]{2,1,0:T(2,128)(2,1)}) custom-call(bf16[2,64,640]{2,1,0:T(8,128)(2,1)} %copy-done, bf16[2,64,640]{2,1,0:T(8,128)(2,1)} %copy-done.1, bf16[16,2,640]{2,1,0:T(2,128)(2,1)} %get-tuple-element.34.first, bf16[16,2,640]{2,1,0:T(2,128)(2,1)} %get-tuple-element.35.last), custom_call_target="tpu_custom_call" | custom-call | tf_op jit(solution)/shard_map/sides/pallas_call | solution.py:134
  18.8 3.5 %collective-permute-start.2 = (bf16[20,2,640]{2,1,0:T(2,128)(2,1)}, bf16[20,2,640]{2,1,0:T(2,128)(2,1)S(1)}, u32[]{:S(2)}, u32[]{:S(2)}) collective-permute-start(bf16[20,2,640]{2,1,0:T(2,128)(2,1)} %get-tuple-element.36), channel_id=1, source_target_pairs={{0,1},{1,2},{2,3},{4,5},{5,6},{6,7},{8,9},{9,10},{10,11},{12,13},{... | collective-permute-start | bytes 153608 | tf_op jit(solution)/shard_map/ppermute | solution.py:20
  22.4 1.9 %collective-permute-start.3 = (bf16[20,2,640]{2,1,0:T(2,128)(2,1)}, bf16[20,2,640]{2,1,0:T(2,128)(2,1)S(1)}, u32[]{:S(2)}, u32[]{:S(2)}) collective-permute-start(bf16[20,2,640]{2,1,0:T(2,128)(2,1)} %get-tuple-element.37), channel_id=1, source_target_pairs={{1,0},{2,1},{3,2},{5,4},{6,5},{7,6},{9,8},{10,9},{11,10},{13,12},{... | collective-permute-start | bytes 153608 | tf_op jit(solution)/shard_map/ppermute | solution.py:20
  24.3 3.3 %tiles.1 = (s32[12]{0:T(128)}, bf16[3,9,4,64,128]{4,3,2,1,0:T(8,128)(2,1)}, bf16[9,4,64,128]{3,2,1,0:T(8,128)(2,1)}) custom-call(s32[16,64]{1,0:T(8,128)} %low.3, s32[16,64]{1,0:T(8,128)} %high.3, bf16[27,64,64]{2,1,0:T(8,128)(2,1)} %weight_one.1, bf16[27,64,64]{2,1,0:T(8,128)(2,1)} %weight_two.1), custom_call_target="tpu_custom_call" | custom-call | tf_op jit(solution)/shard_map/tiles/pallas_call | solution.py:196
  28.3 0.4 copy-done.13
  28.6 20.3 %bricks.1 = (bf16[16,64,512]{2,1,0:T(8,128)(2,1)}, bf16[640,512]{1,0:T(8,128)(2,1)}, f32[4,8,8,512]{3,2,1,0:T(8,128)}, bf16[14,64,128]{2,1,0:T(8,128)(2,1)}, bf16[14,64,128]{2,1,0:T(8,128)(2,1)}) custom-call(s32[12]{0:T(128)} %get-tuple-element.30.slots, s32[1]{0:T(128)} %bitcast.core, bf16[16,64,640]{2,1,0:T(8,128)(2,1)} %get-tuple-element.31.packed.codes, ...), custom_call_target="tpu_custom_call" | custom-call | tf_op jit(solution)/shard_map/bricks/pallas_call | solution.py:444
  48.9 1.7 %collective-permute-done.8 = bf16[14,64,128]{2,1,0:T(8,128)(2,1)S(1)} collective-permute-done((bf16[14,64,128]{2,1,0:T(8,128)(2,1)}, bf16[14,64,128]{2,1,0:T(8,128)(2,1)S(1)}, u32[]{:S(2)}, u32[]{:S(2)}) %collective-permute-start.8) | collective-permute-done | bytes 229408 | tf_op jit(solution)/shard_map/ppermute | solution.py:31
  50.6 0.7 copy-done.2
  51.3 1.8 %pair.1 = (bf16[224,128]{1,0:T(8,128)(2,1)}, bf16[224,128]{1,0:T(8,128)(2,1)}, bf16[224,128]{1,0:T(8,128)(2,1)}, bf16[224,128]{1,0:T(8,128)(2,1)}) custom-call(s32[1]{0:T(128)} %bitcast.5.member, bf16[4,224,128]{2,1,0:T(8,128)(2,1)} %bitcast.11, bf16[4,224,128]{2,1,0:T(8,128)(2,1)} %bitcast.12), custom_call_target="tpu_custom_call" | custom-call | tf_op jit(solution)/shard_map/pair/pallas_call | solution.py:671
  53.1 0.9 collective-permute-start.9
  54.0 1.2 %collective-permute-start.10 = (bf16[224,128]{1,0:T(8,128)(2,1)}, bf16[224,128]{1,0:T(8,128)(2,1)S(1)}, u32[]{:S(2)}, u32[]{:S(2)}) collective-permute-start(bf16[224,128]{1,0:T(8,128)(2,1)} %get-tuple-element.52), channel_id=1, source_target_pairs={{0,2},{1,3},{2,0},{3,1},{4,6},{5,7},{6,4},{7,5},{8,10},{9,11},{10,... | collective-permute-start | bytes 172040 | tf_op jit(solution)/shard_map/ppermute | solution.py:31
  55.1 0.6 collective-permute-start.11
  55.7 0.9 collective-permute-done.9
  56.6 0.6 collective-permute-done.10
  57.2 2.0 %collective-permute-done.11 = bf16[224,128]{1,0:T(8,128)(2,1)S(1)} collective-permute-done((bf16[224,128]{1,0:T(8,128)(2,1)}, bf16[224,128]{1,0:T(8,128)(2,1)S(1)}, u32[]{:S(2)}, u32[]{:S(2)}) %collective-permute-start.11) | collective-permute-done | bytes 57376 | tf_op jit(solution)/shard_map/ppermute | solution.py:31
  59.3 0.9 add_convert_fusion.1
  60.3 2.6 %collective-permute-start.13 = (bf16[224,128]{1,0:T(8,128)(2,1)S(1)}, bf16[224,128]{1,0:T(8,128)(2,1)S(1)}, u32[]{:S(2)}, u32[]{:S(2)}) collective-permute-start(bf16[224,128]{1,0:T(8,128)(2,1)S(1)} %add_convert_fusion.1), channel_id=1, source_target_pairs={{0,16},{1,17},{2,18},{3,19},{4,20},{5,21},{6,22},{7,23},{8,24},{9,... | collective-permute-start | bytes 172040 | tf_op jit(solution)/shard_map/ppermute | solution.py:31
  63.2 2.3 %collective-permute-done.13 = bf16[224,128]{1,0:T(8,128)(2,1)S(1)} collective-permute-done((bf16[224,128]{1,0:T(8,128)(2,1)S(1)}, bf16[224,128]{1,0:T(8,128)(2,1)S(1)}, u32[]{:S(2)}, u32[]{:S(2)}) %collective-permute-start.13) | collective-permute-done | bytes 57376 | tf_op jit(solution)/shard_map/ppermute | solution.py:31
  65.5 0.9 collective-permute-done.12
  66.5 1.3 %collective-permute-start.17 = (bf16[224,128]{1,0:T(8,128)(2,1)S(1)}, bf16[224,128]{1,0:T(8,128)(2,1)S(1)}, u32[]{:S(2)}, u32[]{:S(2)}) collective-permute-start(bf16[224,128]{1,0:T(8,128)(2,1)S(1)} %add_convert_fusion.refs_0_), channel_id=1, source_target_pairs={{0,6},{1,7},{2,4},{3,5},{4,2},{5,3},{6,0},{7,1},{8,14},{9,15},{10,... | collective-permute-start | bytes 172040 | tf_op jit(solution)/shard_map/ppermute | solution.py:31
  67.7 0.8 collective-permute-start.16
  68.5 0.7 collective-permute-start.15
  69.2 1.3 %collective-permute-done.17.refs_3_ = bf16[224,128]{1,0:T(8,128)(2,1)S(1)} collective-permute-done((bf16[224,128]{1,0:T(8,128)(2,1)S(1)}, bf16[224,128]{1,0:T(8,128)(2,1)S(1)}, u32[]{:S(2)}, u32[]{:S(2)}) %collective-permute-start.17) | collective-permute-done | bytes 57376 | tf_op jit(solution)/shard_map/ppermute | solution.py:31
  70.5 0.6 collective-permute-done.16.refs_2_
  71.1 0.4 collective-permute-done.15.refs_1_
  71.7 0.6 copy-done.11
  72.3 1.6 %seat.1 = bf16[4,224,128]{2,1,0:T(8,128)(2,1)} custom-call(s32[1]{0:T(128)} %bitcast.5.member, bf16[224,128]{1,0:T(8,128)(2,1)} %copy-done.4, bf16[224,128]{1,0:T(8,128)(2,1)} %copy-done.11, bf16[224,128]{1,0:T(8,128)(2,1)} %copy-done.10, bf16[224,128]{1,0:T(8,128)(2,1)} %copy-done.9), custom_call_target="tpu_custom_call" | custom-call | tf_op jit(solution)/shard_map/seat/pallas_call | solution.py:688
  74.0 5.3 %collective-permute-start.18 = (bf16[14,64,128]{2,1,0:T(8,128)(2,1)}, bf16[14,64,128]{2,1,0:T(8,128)(2,1)S(1)}, u32[]{:S(2)}, u32[]{:S(2)}) collective-permute-start(bf16[14,64,128]{2,1,0:T(8,128)(2,1)} %bitcast.9), channel_id=1, source_target_pairs={{0,1},{1,0},{2,3},{3,2},{4,5},{5,4},{6,7},{7,6},{8,9},{9,8},{10,11... | collective-permute-start | bytes 688136 | tf_op jit(solution)/shard_map/ppermute | solution.py:31
  79.2 8.6 %inputs.1 = (bf16[20,64,512]{2,1,0:T(8,128)(2,1)}, bf16[20,2,512]{2,1,0:T(2,128)(2,1)}, bf16[20,2,512]{2,1,0:T(2,128)(2,1)}) custom-call(s32[12]{0:T(128)} %get-tuple-element.30.slots, bf16[640,512]{1,0:T(8,128)(2,1)} %get-tuple-element.40.errors, f32[4,8,8,512]{3,2,1,0:T(8,128)} %get-tuple-element.41.grads, ...), custom_call_target="tpu_custom_call" | custom-call | tf_op jit(solution)/shard_map/inputs/pallas_call | solution.py:559
  87.9 2.0 %collective-permute-start.4 = (bf16[20,2,512]{2,1,0:T(2,128)(2,1)}, bf16[20,2,512]{2,1,0:T(2,128)(2,1)S(1)}, u32[]{:S(2)}, u32[]{:S(2)}) collective-permute-start(bf16[20,2,512]{2,1,0:T(2,128)(2,1)} %get-tuple-element.44), channel_id=1, source_target_pairs={{0,1},{1,2},{2,3},{4,5},{5,6},{6,7},{8,9},{9,10},{10,11},{12,13},{... | collective-permute-start | bytes 122888 | tf_op jit(solution)/shard_map/ppermute | solution.py:20
  89.9 2.3 %collective-permute-start.5 = (bf16[20,2,512]{2,1,0:T(2,128)(2,1)}, bf16[20,2,512]{2,1,0:T(2,128)(2,1)S(1)}, u32[]{:S(2)}, u32[]{:S(2)}) collective-permute-start(bf16[20,2,512]{2,1,0:T(2,128)(2,1)} %get-tuple-element.45), channel_id=1, source_target_pairs={{1,0},{2,1},{3,2},{5,4},{6,5},{7,6},{9,8},{10,9},{11,10},{13,12},{... | collective-permute-start | bytes 122888 | tf_op jit(solution)/shard_map/ppermute | solution.py:20
  92.2 3.2 %collective-permute-done.5.from_right = bf16[20,2,512]{2,1,0:T(2,128)(2,1)S(1)} collective-permute-done((bf16[20,2,512]{2,1,0:T(2,128)(2,1)}, bf16[20,2,512]{2,1,0:T(2,128)(2,1)S(1)}, u32[]{:S(2)}, u32[]{:S(2)}) %collective-permute-start.5) | collective-permute-done | bytes 40992 | tf_op jit(solution)/shard_map/ppermute | solution.py:20
  95.5 0.6 copy-done.6
  96.1 1.7 %ends.1 = (bf16[2,64,512]{2,1,0:T(8,128)(2,1)}, bf16[2,64,512]{2,1,0:T(8,128)(2,1)}) custom-call(bf16[20,64,512]{2,1,0:T(8,128)(2,1)} %get-tuple-element.43.above.below.grads, bf16[20,64,512]{2,1,0:T(8,128)(2,1)} %get-tuple-element.43.above.below.grads, bf16[20,2,512]{2,1,0:T(2,128)(2,1)} %copy-done.5, bf16[20,2,512]{2,1,0:T(2,128)(2,1)} %copy-done.6), custom_call_target="tpu_custom_call" | custom-call | tf_op jit(solution)/shard_map/ends/pallas_call | solution.py:605
  97.8 2.0 %collective-permute-start.6 = (bf16[2,64,512]{2,1,0:T(8,128)(2,1)}, bf16[2,64,512]{2,1,0:T(8,128)(2,1)S(1)}, u32[]{:S(2)}, u32[]{:S(2)}) collective-permute-start(bf16[2,64,512]{2,1,0:T(8,128)(2,1)} %get-tuple-element.46), channel_id=1, source_target_pairs={{0,4},{4,8},{8,12},{12,16},{16,20},{20,24},{24,28},{1,5},{5,9},{9,... | collective-permute-start | bytes 393224 | tf_op jit(solution)/shard_map/ppermute | solution.py:20
  99.8 4.2 %collective-permute-start.7 = (bf16[2,64,512]{2,1,0:T(8,128)(2,1)}, bf16[2,64,512]{2,1,0:T(8,128)(2,1)S(1)}, u32[]{:S(2)}, u32[]{:S(2)}) collective-permute-start(bf16[2,64,512]{2,1,0:T(8,128)(2,1)} %get-tuple-element.47), channel_id=1, source_target_pairs={{4,0},{8,4},{12,8},{16,12},{20,16},{24,20},{28,24},{5,1},{9,5},{13... | collective-permute-start | bytes 393224 | tf_op jit(solution)/shard_map/ppermute | solution.py:20
  104.0 0.7 collective-permute-done.6.from_above
  104.7 2.9 %collective-permute-done.7.from_below = bf16[2,64,512]{2,1,0:T(8,128)(2,1)S(1)} collective-permute-done((bf16[2,64,512]{2,1,0:T(8,128)(2,1)}, bf16[2,64,512]{2,1,0:T(8,128)(2,1)S(1)}, u32[]{:S(2)}, u32[]{:S(2)}) %collective-permute-start.7) | collective-permute-done | bytes 131104 | tf_op jit(solution)/shard_map/ppermute | solution.py:20
  107.6 0.7 copy-done.8
  108.3 3.5 %join.1 = bf16[16,64,512]{2,1,0:T(8,128)(2,1)} custom-call(bf16[20,64,512]{2,1,0:T(8,128)(2,1)} %get-tuple-element.43.above.below.grads, bf16[16,64,640]{2,1,0:T(8,128)(2,1)} %get-tuple-element.31.packed.codes, bf16[20,2,512]{2,1,0:T(2,128)(2,1)} %copy-done.5, bf16[20,2,512]{2,1,0:T(2,128)(2,1)} %copy-done.6, bf16[2,64,512]{2,1,0:T(8,128)(2,1)} %copy-done.7, ...), custom_call_target="tpu_custom_call" | custom-call | tf_op jit(solution)/shard_map/join/pallas_call | solution.py:652
  111.7 0.7 copy-done.3
  112.4 2.6 %sums.1 = (f32[27,64,64]{2,1,0:T(8,128)}, f32[27,64,64]{2,1,0:T(8,128)}) custom-call(s32[1]{0:T(128)} %bitcast.core, bf16[14,64,128]{2,1,0:T(8,128)(2,1)} %bitcast.10, bf16[14,64,128]{2,1,0:T(8,128)(2,1)} %copy-done.3), custom_call_target="tpu_custom_call" | custom-call | tf_op jit(solution)/shard_map/sums/pallas_call | solution.py:707
  (30 shorter events, 1.4 us)
Async XLA Ops:
  3.9 8.1 %collective-permute-start = (bf16[2,64,640]{2,1,0:T(8,128)(2,1)}, bf16[2,64,640]{2,1,0:T(8,128)(2,1)S(1)}, u32[]{:S(2)}, u32[]{:S(2)}) collective-permute-start(bf16[2,64,640]{2,1,0:T(8,128)(2,1)} %get-tuple-element.32), channel_id=1, source_target_pairs={{0,4},{4,8},{8,12},{12,16},{16,20},{20,24},{24,28},{1,5},{5,9},{9,... | collective-permute-start | bytes 491528 | tf_op jit(solution)/shard_map/ppermute | solution.py:20
  7.0 9.5 %collective-permute-start.1 = (bf16[2,64,640]{2,1,0:T(8,128)(2,1)}, bf16[2,64,640]{2,1,0:T(8,128)(2,1)S(1)}, u32[]{:S(2)}, u32[]{:S(2)}) collective-permute-start(bf16[2,64,640]{2,1,0:T(8,128)(2,1)} %get-tuple-element.33), channel_id=1, source_target_pairs={{4,0},{8,4},{12,8},{16,12},{20,16},{24,20},{28,24},{5,1},{9,5},{13... | collective-permute-start | bytes 491528 | tf_op jit(solution)/shard_map/ppermute | solution.py:20
  12.0 4.5 %copy-start = (bf16[2,64,640]{2,1,0:T(8,128)(2,1)}, bf16[2,64,640]{2,1,0:T(8,128)(2,1)S(1)}, u32[]{:S(2)}) copy-start(bf16[2,64,640]{2,1,0:T(8,128)(2,1)S(1)} %collective-permute-done.above) | copy-start | bytes 491524
  16.5 0.7 copy-start.1
  18.8 8.8 %collective-permute-start.2 = (bf16[20,2,640]{2,1,0:T(2,128)(2,1)}, bf16[20,2,640]{2,1,0:T(2,128)(2,1)S(1)}, u32[]{:S(2)}, u32[]{:S(2)}) collective-permute-start(bf16[20,2,640]{2,1,0:T(2,128)(2,1)} %get-tuple-element.36), channel_id=1, source_target_pairs={{0,1},{1,2},{2,3},{4,5},{5,6},{6,7},{8,9},{9,10},{10,11},{12,13},{... | collective-permute-start | bytes 153608 | tf_op jit(solution)/shard_map/ppermute | solution.py:20
  22.4 5.6 %collective-permute-start.3 = (bf16[20,2,640]{2,1,0:T(2,128)(2,1)}, bf16[20,2,640]{2,1,0:T(2,128)(2,1)S(1)}, u32[]{:S(2)}, u32[]{:S(2)}) collective-permute-start(bf16[20,2,640]{2,1,0:T(2,128)(2,1)} %get-tuple-element.37), channel_id=1, source_target_pairs={{1,0},{2,1},{3,2},{5,4},{6,5},{7,6},{9,8},{10,9},{11,10},{13,12},{... | collective-permute-start | bytes 153608 | tf_op jit(solution)/shard_map/ppermute | solution.py:20
  27.7 0.6 copy-start.12
  28.0 0.6 copy-start.13
  48.9 1.7 %collective-permute-start.8 = (bf16[14,64,128]{2,1,0:T(8,128)(2,1)}, bf16[14,64,128]{2,1,0:T(8,128)(2,1)S(1)}, u32[]{:S(2)}, u32[]{:S(2)}) collective-permute-start(bf16[14,64,128]{2,1,0:T(8,128)(2,1)} %get-tuple-element.49), channel_id=1, source_target_pairs={{0,1},{1,0},{2,3},{3,2},{4,5},{5,4},{6,7},{7,6},{8,9},{9,8},{10,11... | collective-permute-start | bytes 688136 | tf_op jit(solution)/shard_map/ppermute | solution.py:31
  50.6 0.7 copy-start.2
  53.1 3.5 %collective-permute-start.9 = (bf16[224,128]{1,0:T(8,128)(2,1)}, bf16[224,128]{1,0:T(8,128)(2,1)S(1)}, u32[]{:S(2)}, u32[]{:S(2)}) collective-permute-start(bf16[224,128]{1,0:T(8,128)(2,1)} %get-tuple-element.51), channel_id=1, source_target_pairs={{0,4},{1,5},{2,6},{3,7},{4,0},{5,1},{6,2},{7,3},{8,12},{9,13},{10,... | collective-permute-start | bytes 172040 | tf_op jit(solution)/shard_map/ppermute | solution.py:31
  54.0 3.3 %collective-permute-start.10 = (bf16[224,128]{1,0:T(8,128)(2,1)}, bf16[224,128]{1,0:T(8,128)(2,1)S(1)}, u32[]{:S(2)}, u32[]{:S(2)}) collective-permute-start(bf16[224,128]{1,0:T(8,128)(2,1)} %get-tuple-element.52), channel_id=1, source_target_pairs={{0,2},{1,3},{2,0},{3,1},{4,6},{5,7},{6,4},{7,5},{8,10},{9,11},{10,... | collective-permute-start | bytes 172040 | tf_op jit(solution)/shard_map/ppermute | solution.py:31
  55.1 4.1 %collective-permute-start.11 = (bf16[224,128]{1,0:T(8,128)(2,1)}, bf16[224,128]{1,0:T(8,128)(2,1)S(1)}, u32[]{:S(2)}, u32[]{:S(2)}) collective-permute-start(bf16[224,128]{1,0:T(8,128)(2,1)} %get-tuple-element.53), channel_id=1, source_target_pairs={{0,6},{1,7},{2,4},{3,5},{4,2},{5,3},{6,0},{7,1},{8,14},{9,15},{10,... | collective-permute-start | bytes 172040 | tf_op jit(solution)/shard_map/ppermute | solution.py:31
  60.1 3.1 %collective-permute-start.14 = (bf16[224,128]{1,0:T(8,128)(2,1)S(1)}, bf16[224,128]{1,0:T(8,128)(2,1)S(1)}, u32[]{:S(2)}, u32[]{:S(2)}) collective-permute-start(bf16[224,128]{1,0:T(8,128)(2,1)S(1)} %add_convert_fusion.1), channel_id=1, source_target_pairs={{0,24},{1,25},{2,26},{3,27},{4,28},{5,29},{6,30},{7,31},{8,16},{9,... | collective-permute-start | bytes 172040 | tf_op jit(solution)/shard_map/ppermute | solution.py:31
  60.3 5.2 %collective-permute-start.13 = (bf16[224,128]{1,0:T(8,128)(2,1)S(1)}, bf16[224,128]{1,0:T(8,128)(2,1)S(1)}, u32[]{:S(2)}, u32[]{:S(2)}) collective-permute-start(bf16[224,128]{1,0:T(8,128)(2,1)S(1)} %add_convert_fusion.1), channel_id=1, source_target_pairs={{0,16},{1,17},{2,18},{3,19},{4,20},{5,21},{6,22},{7,23},{8,24},{9,... | collective-permute-start | bytes 172040 | tf_op jit(solution)/shard_map/ppermute | solution.py:31
  62.9 3.5 %collective-permute-start.12 = (bf16[224,128]{1,0:T(8,128)(2,1)S(1)}, bf16[224,128]{1,0:T(8,128)(2,1)S(1)}, u32[]{:S(2)}, u32[]{:S(2)}) collective-permute-start(bf16[224,128]{1,0:T(8,128)(2,1)S(1)} %add_convert_fusion.1), channel_id=1, source_target_pairs={{0,8},{1,9},{2,10},{3,11},{4,12},{5,13},{6,14},{7,15},{8,0},{9,1},... | collective-permute-start | bytes 172040 | tf_op jit(solution)/shard_map/ppermute | solution.py:31
  66.5 5.1 %copy-start.4 = (bf16[224,128]{1,0:T(8,128)(2,1)}, bf16[224,128]{1,0:T(8,128)(2,1)S(1)}, u32[]{:S(2)}) copy-start(bf16[224,128]{1,0:T(8,128)(2,1)S(1)} %add_convert_fusion.refs_0_) | copy-start | bytes 172036
  66.5 4.0 %collective-permute-start.17 = (bf16[224,128]{1,0:T(8,128)(2,1)S(1)}, bf16[224,128]{1,0:T(8,128)(2,1)S(1)}, u32[]{:S(2)}, u32[]{:S(2)}) collective-permute-start(bf16[224,128]{1,0:T(8,128)(2,1)S(1)} %add_convert_fusion.refs_0_), channel_id=1, source_target_pairs={{0,6},{1,7},{2,4},{3,5},{4,2},{5,3},{6,0},{7,1},{8,14},{9,15},{10,... | collective-permute-start | bytes 172040 | tf_op jit(solution)/shard_map/ppermute | solution.py:31
  67.7 3.3 %collective-permute-start.16 = (bf16[224,128]{1,0:T(8,128)(2,1)S(1)}, bf16[224,128]{1,0:T(8,128)(2,1)S(1)}, u32[]{:S(2)}, u32[]{:S(2)}) collective-permute-start(bf16[224,128]{1,0:T(8,128)(2,1)S(1)} %add_convert_fusion.refs_0_), channel_id=1, source_target_pairs={{0,2},{1,3},{2,0},{3,1},{4,6},{5,7},{6,4},{7,5},{8,10},{9,11},{10,... | collective-permute-start | bytes 172040 | tf_op jit(solution)/shard_map/ppermute | solution.py:31
  68.5 3.0 %collective-permute-start.15 = (bf16[224,128]{1,0:T(8,128)(2,1)S(1)}, bf16[224,128]{1,0:T(8,128)(2,1)S(1)}, u32[]{:S(2)}, u32[]{:S(2)}) collective-permute-start(bf16[224,128]{1,0:T(8,128)(2,1)S(1)} %add_convert_fusion.refs_0_), channel_id=1, source_target_pairs={{0,4},{1,5},{2,6},{3,7},{4,0},{5,1},{6,2},{7,3},{8,12},{9,13},{10,... | collective-permute-start | bytes 172040 | tf_op jit(solution)/shard_map/ppermute | solution.py:31
  70.5 1.0 copy-start.9
  71.1 0.6 copy-start.10
  71.7 0.6 copy-start.11
  74.0 37.8 %collective-permute-start.18 = (bf16[14,64,128]{2,1,0:T(8,128)(2,1)}, bf16[14,64,128]{2,1,0:T(8,128)(2,1)S(1)}, u32[]{:S(2)}, u32[]{:S(2)}) collective-permute-start(bf16[14,64,128]{2,1,0:T(8,128)(2,1)} %bitcast.9), channel_id=1, source_target_pairs={{0,1},{1,0},{2,3},{3,2},{4,5},{5,4},{6,7},{7,6},{8,9},{9,8},{10,11... | collective-permute-start | bytes 688136 | tf_op jit(solution)/shard_map/ppermute | solution.py:31
  87.9 4.3 %collective-permute-start.4 = (bf16[20,2,512]{2,1,0:T(2,128)(2,1)}, bf16[20,2,512]{2,1,0:T(2,128)(2,1)S(1)}, u32[]{:S(2)}, u32[]{:S(2)}) collective-permute-start(bf16[20,2,512]{2,1,0:T(2,128)(2,1)} %get-tuple-element.44), channel_id=1, source_target_pairs={{0,1},{1,2},{2,3},{4,5},{5,6},{6,7},{8,9},{9,10},{10,11},{12,13},{... | collective-permute-start | bytes 122888 | tf_op jit(solution)/shard_map/ppermute | solution.py:20
  89.9 5.5 %collective-permute-start.5 = (bf16[20,2,512]{2,1,0:T(2,128)(2,1)}, bf16[20,2,512]{2,1,0:T(2,128)(2,1)S(1)}, u32[]{:S(2)}, u32[]{:S(2)}) collective-permute-start(bf16[20,2,512]{2,1,0:T(2,128)(2,1)} %get-tuple-element.45), channel_id=1, source_target_pairs={{1,0},{2,1},{3,2},{5,4},{6,5},{7,6},{9,8},{10,9},{11,10},{13,12},{... | collective-permute-start | bytes 122888 | tf_op jit(solution)/shard_map/ppermute | solution.py:20
  92.2 3.3 %copy-start.5 = (bf16[20,2,512]{2,1,0:T(2,128)(2,1)}, bf16[20,2,512]{2,1,0:T(2,128)(2,1)S(1)}, u32[]{:S(2)}) copy-start(bf16[20,2,512]{2,1,0:T(2,128)(2,1)S(1)} %collective-permute-done.4.from_left) | copy-start | bytes 122884
  95.5 0.6 copy-start.6
  97.8 6.9 %collective-permute-start.6 = (bf16[2,64,512]{2,1,0:T(8,128)(2,1)}, bf16[2,64,512]{2,1,0:T(8,128)(2,1)S(1)}, u32[]{:S(2)}, u32[]{:S(2)}) collective-permute-start(bf16[2,64,512]{2,1,0:T(8,128)(2,1)} %get-tuple-element.46), channel_id=1, source_target_pairs={{0,4},{4,8},{8,12},{12,16},{16,20},{20,24},{24,28},{1,5},{5,9},{9,... | collective-permute-start | bytes 393224 | tf_op jit(solution)/shard_map/ppermute | solution.py:20
  99.8 7.8 %collective-permute-start.7 = (bf16[2,64,512]{2,1,0:T(8,128)(2,1)}, bf16[2,64,512]{2,1,0:T(8,128)(2,1)S(1)}, u32[]{:S(2)}, u32[]{:S(2)}) collective-permute-start(bf16[2,64,512]{2,1,0:T(8,128)(2,1)} %get-tuple-element.47), channel_id=1, source_target_pairs={{4,0},{8,4},{12,8},{16,12},{20,16},{24,20},{28,24},{5,1},{9,5},{13... | collective-permute-start | bytes 393224 | tf_op jit(solution)/shard_map/ppermute | solution.py:20
  104.7 2.9 %copy-start.7 = (bf16[2,64,512]{2,1,0:T(8,128)(2,1)}, bf16[2,64,512]{2,1,0:T(8,128)(2,1)S(1)}, u32[]{:S(2)}) copy-start(bf16[2,64,512]{2,1,0:T(8,128)(2,1)S(1)} %collective-permute-done.6.from_above) | copy-start | bytes 393220
  107.6 0.7 copy-start.8
  111.7 0.7 copy-start.3
where the time goes:
time: 116 us; the launch traced here: 115 us
  Pallas kernels  48.3 us (42%)
  starting transfers between devices  35.6 us (31%)
  waiting for transfers between devices  24.7 us (21%)
  local copies, waits for them, and re-layouts  4.74 us (4%)
    ppermute x8, starting transfers between devices, shifted_in(): return lax.ppermute(array, axis, pairs)  22.1 us
    pallas_call x1, Pallas kernels, brick_call(): pl.pallas_call(brick_kernel, out_shape=(shape((lx, ly, width), BF16), sha...  20.3 us
    ppermute x8, waiting for transfers between devices, shifted_in(): return lax.ppermute(array, axis, pairs)  13.6 us
    ppermute x11, starting transfers between devices, flat_permute(): return lax.ppermute(array, ('gx', 'gy'), pairs)  13.5 us
    ppermute x11, waiting for transfers between devices, flat_permute(): return lax.ppermute(array, ('gx', 'gy'), pairs)  11.1 us
    pallas_call x1, Pallas kernels, input_call(): pl.pallas_call(input_kernel, out_shape=(shape((lx + 4, ly, width), BF16),...  8.65 us
    unnamed x28, local copies, waits for them, and re-layouts  4.74 us
    pallas_call x1, Pallas kernels, join_call(): pl.pallas_call(join_kernel, out_shape=shape((lx, ly, width), BF16), grid=...  3.47 us
  transfers between devices with their start and end apart: 19, of which 16 were waited for; matrix products, arithmetic and copies ran while one was open for 0% of the time, Pallas kernels for 15%

commit v1 on v0

--- a/solution.py
+++ b/solution.py
@@ -7,6 +7,7 @@
 from jax.experimental.pallas import tpu as pltpu
 from jax.sharding import PartitionSpec as P
 
+
 BRICK = 8
 ACT_MAX = 4
 SHARE = 2
@@ -18,17 +19,6 @@
     devices = lax.axis_size(axis)
     pairs = [(i, i + by) for i in range(devices) if 0 <= i + by < devices]
     return lax.ppermute(array, axis, pairs)
-
-
-def flat_permute(array, move):
-    nx, ny = lax.axis_size("gx"), lax.axis_size("gy")
-    pairs = []
-    for x in range(nx):
-        for y in range(ny):
-            to = move(x, y)
-            if to is not None:
-                pairs.append((x * ny + y, to[0] * ny + to[1]))
-    return lax.ppermute(array, ("gx", "gy"), pairs)
 
 
 def low_lanes(shape):
@@ -59,62 +49,54 @@
 shape = jax.ShapeDtypeStruct
 
 
-def decoded(code):
-    floor = jnp.floor(code * (1.0 / 16.0))
-    return floor, code - 16.0 * floor
-
-
-def mask_of(bounds, z_low):
+EMPTY_FEATURE = 256.0
+
+
+def encode(feature, low, high, z_low):
     z = jnp.where(low_lanes((1, 128)), 1.0 * z_low, z_low + 1.0)
-    return (z >= bounds[0]) & (z < bounds[1])
-
-
-def edge_kernel(features, low, high, packed, top, bottom, first, last):
-    lx, ly = low.shape
-    code = (low[...] * 16 + high[...]).astype(F32)
+    feature = jnp.where(feature == 0.0, EMPTY_FEATURE, feature)
+    return jnp.where((z >= low) & (z < high), feature, 0.0)
+
+
+def column_bounds(low, high, x):
+    ly = low.shape[1]
+    code = (low[x : x + 1, :] * 16 + high[x : x + 1, :]).astype(F32)
     same = lax.broadcasted_iota(jnp.int32, (ly, ly), 0) == lax.broadcasted_iota(
         jnp.int32, (ly, ly), 1
     )
-    ones = jnp.ones((ly, 128), BF16)
-    low_row = low_lanes((1, 128))
-    for x in range(lx):
-        spread = jnp.where(same, code[x : x + 1, :], 0.0).astype(BF16)
-        column = jnp.dot(spread, ones, preferred_element_type=F32)
-        bounds = decoded(column)
-        pieces = []
-        for m in range(4):
-            v = features[x, :, 128 * m : 128 * m + 128].astype(F32)
-            pieces.append(jnp.where(mask_of(bounds, 2 * m), v, 0.0))
-        for p, v in enumerate(to_shifted(pieces)):
-            if p == 0:
-                v = jnp.where(low_row, column, v)
-            lanes = slice(128 * p, 128 * p + 128)
-            v16 = v.astype(BF16)
-            packed[x, :, lanes] = v16
-            if x < 2:
-                top[x, :, lanes] = v16
-            if x >= lx - 2:
-                bottom[x - (lx - 2), :, lanes] = v16
-            first[x, :, lanes] = v[0:2].astype(BF16)
-            last[x, :, lanes] = v[ly - 2 : ly].astype(BF16)
-
-
-def edge_call(features, low, high):
+    spread = jnp.where(same, code, 0.0).astype(BF16)
+    column = jnp.dot(spread, jnp.ones((ly, 128), BF16), preferred_element_type=F32)
+    floor = jnp.floor(column * (1.0 / 16.0))
+    return floor, column - 16.0 * floor
+
+
+def strip_kernel(top_in, bottom_in, low, high, top, bottom):
+    lx = low.shape[0]
+    for source, target, base in ((top_in, top, 0), (bottom_in, bottom, lx - 2)):
+        for x in range(2):
+            floor, high_of = column_bounds(low, high, base + x)
+            for m in range(4):
+                lanes = slice(128 * m, 128 * m + 128)
+                v = encode(source[x, :, lanes].astype(F32), floor, high_of, 2 * m)
+                target[x, :, lanes] = v.astype(BF16)
+
+
+def strip_call(features, low, high):
     lx, ly, width = features.shape
-    wide = width + 128
+    end = lx // 2 - 1
     return pl.pallas_call(
-        edge_kernel,
-        out_shape=(
-            shape((lx, ly, wide), BF16),
-            shape((2, ly, wide), BF16),
-            shape((2, ly, wide), BF16),
-            shape((lx, 2, wide), BF16),
-            shape((lx, 2, wide), BF16),
-        ),
-        in_specs=[VMEM] * 3,
-        out_specs=(VMEM,) * 5,
-        name="edges",
-    )(features, low, high)
+        strip_kernel,
+        out_shape=(shape((2, ly, width), BF16), shape((2, ly, width), BF16)),
+        grid=(1,),
+        in_specs=[
+            pl.BlockSpec((2, ly, width), lambda i: (0, 0, 0)),
+            pl.BlockSpec((2, ly, width), lambda i: (end, 0, 0)),
+            VMEM,
+            VMEM,
+        ],
+        out_specs=(VMEM, VMEM),
+        name="strips",
+    )(features, features, low, high)
 
 
 def side_kernel(above, below, first, last, to_left, to_right):
@@ -140,7 +122,9 @@
     )(above, below, first, last)
 
 
-def tile_kernel(low, high, weight_one, weight_two, slots, tiles, tiles_last):
+def tile_kernel(
+    features, low, high, weight_one, weight_two, slots, tiles, tiles_last, packed, first, last
+):
     lx, ly = low.shape
     filled = jnp.where(high[...] > low[...], 1.0, 0.0)
     rows = [
@@ -173,6 +157,15 @@
             slots[2 * ACT_MAX + seat] = 1
 
         seat = seat + has.astype(jnp.int32)
+
+    for x in range(lx):
+        floor, high_of = column_bounds(low, high, x)
+        for m in range(4):
+            lanes = slice(128 * m, 128 * m + 128)
+            v = encode(features[x, :, lanes].astype(F32), floor, high_of, 2 * m)
+            packed[x, :, lanes] = v.astype(BF16)
+            first[x, :, lanes] = v[0:2].astype(BF16)
+            last[x, :, lanes] = v[ly - 2 : ly].astype(BF16)
 
     zero = jnp.zeros((64, 64), BF16)
     for conv, weight in enumerate((weight_one, weight_two, weight_two, weight_one)):
@@ -192,18 +185,22 @@
                     tiles_last[tap, d] = tile
 
 
-def tile_call(low, high, weight_one, weight_two):
+def tile_call(features, low, high, weight_one, weight_two):
+    lx, _, width = features.shape
     return pl.pallas_call(
         tile_kernel,
         out_shape=(
             shape((3 * ACT_MAX,), jnp.int32),
             shape((3, 9, 4, 64, 128), BF16),
             shape((9, 4, 64, 128), BF16),
+            shape(features.shape, BF16),
+            shape((lx, 2, width), BF16),
+            shape((lx, 2, width), BF16),
         ),
-        in_specs=[VMEM] * 4,
-        out_specs=(SMEM, VMEM, VMEM),
+        in_specs=[VMEM] * 5,
+        out_specs=(SMEM,) + (VMEM,) * 5,
         name="tiles",
-    )(low, high, weight_one, weight_two)
+    )(features, low, high, weight_one, weight_two)
 
 
 def build_bands(bands, tile_at):
@@ -242,9 +239,9 @@
 
 
 def brick_kernel(
-    slots, core, packed, above, below, left, right, cotangent, tiles, s_one, t_one, s_two, t_two,
-    out, errors_out, grads_out, keep, send,
-    fx, ms, bands_a, bands_b, bands_c, c1, c2, c3, acc, slope, h, e2, er2, ets, et1, folded, total,
+    slots, packed, above, below, left, right, cotangent, tiles, s_one, t_one, s_two, t_two,
+    out, errors_out, grads_out, total,
+    fx, ms, bands_a, bands_b, bands_c, c1, c2, c3, acc, slope, h, e2, er2, ets, et1, folded,
 ):
     lx, ly = out.shape[0], out.shape[1]
     low_row = low_lanes((1, 128))
@@ -254,26 +251,25 @@
     build_bands(bands_a, lambda t, d: tiles[0, t, d])
 
     def put(x, strip, start, stop):
-        for p in range(5):
-            v = strip(p).astype(F32)
-            if p == 0:
-                bounds = decoded(jnp.where(low_row, v, turn(v)))
-                v = jnp.where(low_row, 0.0, v)
-                for m in range(4):
-                    ms[m, x, start:stop, :] = jnp.where(mask_of(bounds, 2 * m), 1.0, 0.0)
+        pieces = []
+        for m in range(4):
+            v = strip(m).astype(F32)
+            ms[m, x, start:stop, :] = jnp.where(v == 0.0, 0.0, 1.0)
+            pieces.append(jnp.where(v == EMPTY_FEATURE, 0.0, v))
+        for p, v in enumerate(to_shifted(pieces)):
             fx[p, x, start:stop, :] = v
 
     def own_row(i, _):
         for k in range(2):
             x = 2 * i + k
-            put(x + 2, lambda p: packed[x, :, 128 * p : 128 * p + 128], 8, 8 + ly)
+            put(x + 2, lambda m: packed[x, :, 128 * m : 128 * m + 128], 8, 8 + ly)
             out[x] = jnp.zeros(out.shape[1:], BF16)
         return 0
 
     lax.fori_loop(0, lx // 2, own_row, 0)
     for x in range(2):
-        put(x, lambda p: above[x, :, 128 * p : 128 * p + 128], 8, 8 + ly)
-        put(lx + 2 + x, lambda p: below[x, :, 128 * p : 128 * p + 128], 8, 8 + ly)
+        put(x, lambda m: above[x, :, 128 * m : 128 * m + 128], 8, 8 + ly)
+        put(lx + 2 + x, lambda m: below[x, :, 128 * m : 128 * m + 128], 8, 8 + ly)
 
     def side_row(i, _):
         for k in range(4):
@@ -283,14 +279,14 @@
                     ms[m, x, base : base + 8, :] = jnp.zeros((8, 128), F32)
                 for p in range(5):
                     fx[p, x, base : base + 8, :] = jnp.zeros((8, 128), F32)
-            put(x, lambda p: left[x, :, 128 * p : 128 * p + 128], 6, 8)
-            put(x, lambda p: right[x, :, 128 * p : 128 * p + 128], 8 + ly, 10 + ly)
+            put(x, lambda m: left[x, :, 128 * m : 128 * m + 128], 6, 8)
+            put(x, lambda m: right[x, :, 128 * m : 128 * m + 128], 8 + ly, 10 + ly)
         return 0
 
     lax.fori_loop(0, (lx + 4) // 4, side_row, 0)
 
     def gather_one(s, _):
-        x0, y0, live = place(slots, s)
+        x0, y0, _ = place(slots, s)
         for p in range(5):
             view = fx.at[p, pl.ds(x0, 12), pl.ds(y0, 24), :]
             for oy in range(3):
@@ -432,12 +428,9 @@
     weight_sums(c1, et1, 10, 0)
     weight_sums(c2, ets, 8, 1)
     total[27] = jnp.zeros((64, 128), BF16)
-    mine = core[0] * 14
-    keep[...] = total[pl.ds(mine, 14)]
-    send[...] = total[pl.ds(14 - mine, 14)]
-
-
-def brick_call(slots, core, packed, above, below, left, right, cotangent, tiles, *vectors):
+
+
+def brick_call(slots, packed, above, below, left, right, cotangent, tiles, *vectors):
     lx, ly, width = cotangent.shape
     n = ACT_MAX
     wide = ly + 16
@@ -447,11 +440,10 @@
             shape((lx, ly, width), BF16),
             shape((n * 160, width), BF16),
             shape((n, 8, 8, width), F32),
-            shape((14, 64, 128), BF16),
-            shape((14, 64, 128), BF16),
+            shape((28, 64, 128), BF16),
         ),
-        in_specs=[SMEM, SMEM] + [VMEM] * 11,
-        out_specs=(VMEM,) * 5,
+        in_specs=[SMEM] + [VMEM] * 11,
+        out_specs=(VMEM,) * 4,
         scratch_shapes=[
             pltpu.VMEM((5, lx + 4, wide, 128), F32),
             pltpu.VMEM((4, lx + 4, wide, 128), F32),
@@ -469,16 +461,16 @@
             pltpu.VMEM((768, n * 64), BF16),
             pltpu.VMEM((768, n * 160), BF16),
             pltpu.VMEM((27, 64, 128), F32),
-            pltpu.VMEM((28, 64, 128), BF16),
         ],
         name="bricks",
-    )(slots, core, packed, above, below, left, right, cotangent, tiles, *vectors)
+    )(slots, packed, above, below, left, right, cotangent, tiles, *vectors)
 
 
 def input_kernel(
-    slots, errors, grads, codes, tiles, grad_own, grad_left, grad_right, e1, c4, bands, acc, grid
+    slots, errors, grads, packed, tiles, grad_own, grad_above, grad_below, grad_left, grad_right,
+    e1, c4, bands, acc, grid,
 ):
-    lx, ly = grad_own.shape[0] - 4, grad_own.shape[1]
+    lx, ly = grad_own.shape[0], grad_own.shape[1]
     wide = grid.shape[2]
     build_bands(bands, lambda t, d: tiles[t, d])
 
@@ -512,7 +504,7 @@
     convolve(c4, bands, acc, 12)
 
     def finish(s, _):
-        x0, y0, live = place(slots, s)
+        x0, y0, _ = place(slots, s)
         for x in range(12):
             at = pl.multiple_of((s * 12 + x) * 16, 16)
             for m in range(4):
@@ -528,50 +520,46 @@
 
     lax.fori_loop(0, ACT_MAX, finish, 0)
 
-    def write_row(x, inside):
-        low_row = low_lanes((1, 128))
-        if inside:
-            v = codes[x - 2].astype(F32)
-            bounds = decoded(jnp.where(low_row, v, turn(v)))
-        for m in range(4):
-            lanes = slice(128 * m, 128 * m + 128)
-            v = grid[m, x, 8 : 8 + ly, :]
-            if inside:
-                v = jnp.where(mask_of(bounds, 2 * m), v, 0.0)
-            grad_own[x, :, lanes] = v.astype(BF16)
-            grad_left[x, :, lanes] = grid[m, x, 6:8, :].astype(BF16)
-            grad_right[x, :, lanes] = grid[m, x, 8 + ly : 10 + ly, :].astype(BF16)
-
     def own_rows(i, _):
         for k in range(2):
-            write_row(2 + 2 * i + k, True)
+            x = 2 * i + k
+            for m in range(4):
+                lanes = slice(128 * m, 128 * m + 128)
+                v = grid[m, x + 2, 8 : 8 + ly, :]
+                v = jnp.where(packed[x, :, lanes].astype(F32) == 0.0, 0.0, v)
+                grad_own[x, :, lanes] = v.astype(BF16)
+                grad_left[x, :, lanes] = grid[m, x + 2, 6:8, :].astype(BF16)
+                grad_right[x, :, lanes] = grid[m, x + 2, 8 + ly : 10 + ly, :].astype(BF16)
         return 0
 
     lax.fori_loop(0, lx // 2, own_rows, 0)
-    for x in (0, 1, lx + 2, lx + 3):
-        write_row(x, False)
+    for target, base in ((grad_above, 0), (grad_below, lx + 2)):
+        for x in range(2):
+            for m in range(4):
+                lanes = slice(128 * m, 128 * m + 128)
+                target[x, 0:ly, lanes] = grid[m, base + x, 8 : 8 + ly, :].astype(BF16)
+                corners = [
+                    grid[m, base + x, 6:8, :],
+                    grid[m, base + x, 8 + ly : 10 + ly, :],
+                    jnp.zeros((4, 128), F32),
+                ]
+                target[x, ly : ly + 8, lanes] = jnp.concatenate(corners, axis=0).astype(BF16)
 
 
 def input_call(slots, errors, grads, packed, tiles):
-    lx, ly, wide = packed.shape
-    width = wide - 128
+    lx, ly, width = packed.shape
     n = ACT_MAX
     return pl.pallas_call(
         input_kernel,
         out_shape=(
-            shape((lx + 4, ly, width), BF16),
-            shape((lx + 4, 2, width), BF16),
-            shape((lx + 4, 2, width), BF16),
+            shape((lx, ly, width), BF16),
+            shape((2, ly + 8, width), BF16),
+            shape((2, ly + 8, width), BF16),
+            shape((lx, 2, width), BF16),
+            shape((lx, 2, width), BF16),
         ),
-        grid=(1,),
-        in_specs=[
-            SMEM,
-            VMEM,
-            VMEM,
-            pl.BlockSpec((lx, ly, 128), lambda i: (0, 0, 0)),
-            VMEM,
-        ],
-        out_specs=(VMEM,) * 3,
+        in_specs=[SMEM] + [VMEM] * 4,
+        out_specs=(VMEM,) * 5,
         scratch_shapes=[
             pltpu.VMEM((5, 14, 24, 128), F32),
             pltpu.VMEM((n, 14, 16, 1920), BF16),
@@ -583,206 +571,167 @@
     )(slots, errors, grads, packed, tiles)
 
 
-def ends_kernel(above, below, from_left, from_right, top, bottom):
-    ly = above.shape[1]
-    lx = from_left.shape[0] - 4
-    for source, base, target in ((above, 0, top), (below, lx + 2, bottom)):
+def ends_kernel(left, right, from_above, from_below, to_left, to_right):
+    lx = left.shape[0]
+    to_left[...] = left[...]
+    to_right[...] = right[...]
+    for source, base in ((from_above, 0), (from_below, lx - 2)):
         for x in range(2):
             v = source[x].astype(F32)
-            one = jnp.concatenate(
-                [from_left[base + x].astype(F32), jnp.zeros((6, v.shape[1]), F32)], axis=0
-            )
-            two = jnp.concatenate(
-                [jnp.zeros((6, v.shape[1]), F32), from_right[base + x].astype(F32)], axis=0
-            )
-            v = jnp.concatenate([v[0:8] + one, v[8 : ly - 8], v[ly - 8 : ly] + two], axis=0)
-            target[x] = v.astype(BF16)
-
-
-def ends_call(grads, from_left, from_right):
-    lx4, ly, width = grads.shape
-    half = lx4 // 2 - 1
+            for strip, target, at in ((left, to_left, 0), (right, to_right, 2)):
+                target[base + x] = (strip[base + x].astype(F32) + v[at : at + 2]).astype(BF16)
+
+
+def ends_call(left, right, from_above, from_below):
+    ly, width = from_above.shape[1] - 8, from_above.shape[2]
+    corners = pl.BlockSpec((2, 8, width), lambda i: (0, ly // 8, 0))
     return pl.pallas_call(
         ends_kernel,
-        out_shape=(shape((2, ly, width), BF16), shape((2, ly, width), BF16)),
+        out_shape=(shape(left.shape, BF16), shape(left.shape, BF16)),
         grid=(1,),
-        in_specs=[
-            pl.BlockSpec((2, ly, width), lambda i: (0, 0, 0)),
-            pl.BlockSpec((2, ly, width), lambda i: (half, 0, 0)),
-            VMEM,
-            VMEM,
-        ],
+        in_specs=[VMEM, VMEM, corners, corners],
         out_specs=(VMEM, VMEM),
         name="ends",
-    )(grads, grads, from_left, from_right)
-
-
-def join_kernel(grads, codes, from_left, from_right, from_above, from_below, grad_features):
-    lx, ly = grad_features.shape[0], grad_features.shape[1]
-    low_row = low_lanes((1, 128))
-
-    def row(x, extra):
-        code = codes[x].astype(F32)
-        bounds = decoded(jnp.where(low_row, code, turn(code)))
-        for m in range(4):
-            lanes = slice(128 * m, 128 * m + 128)
-            v = grads[x + 2, :, lanes].astype(F32)
-            zero = jnp.zeros((6, 128), F32)
-            one = jnp.concatenate([from_left[x + 2, :, lanes].astype(F32), zero], axis=0)
-            two = jnp.concatenate([zero, from_right[x + 2, :, lanes].astype(F32)], axis=0)
-            v = jnp.concatenate([v[0:8] + one, v[8 : ly - 8], v[ly - 8 : ly] + two], axis=0)
-            if extra is not None:
-                v = v + extra[0][extra[1], :, lanes].astype(F32)
-            grad_features[x, :, lanes] = jnp.where(mask_of(bounds, 2 * m), v, 0.0).astype(BF16)
-
-    def inner(i, _):
-        for k in range(2):
-            row(2 + 2 * i + k, None)
-        return 0
-
-    lax.fori_loop(0, (lx - 4) // 2, inner, 0)
-    for x in range(2):
-        row(x, (from_above, x))
-        row(lx - 2 + x, (from_below, x))
-
-
-def join_call(grads, packed, from_left, from_right, from_above, from_below):
-    lx4, ly, width = grads.shape
-    lx = lx4 - 4
+    )(left, right, from_above, from_below)
+
+
+def join_kernel(
+    grads, top, bottom, first, last, from_left, from_right, from_above, from_below, joined,
+    rows_a, rows_b, cols_a, cols_b, sems,
+):
+    lx, ly, _ = joined.shape
+    places = (
+        (rows_a, lambda ref: ref.at[0:2]),
+        (rows_b, lambda ref: ref.at[lx - 2 : lx]),
+        (cols_a, lambda ref: ref.at[2 : lx - 2, 0:16, :]),
+        (cols_b, lambda ref: ref.at[2 : lx - 2, ly - 16 : ly, :]),
+    )
+    copies = [
+        pltpu.make_async_copy(at(grads), held, sems.at[n]) for n, (held, at) in enumerate(places)
+    ]
+    for copy in copies:
+        copy.start()
+    for copy in copies:
+        copy.wait()
+    width = rows_a.shape[2]
+
+    def first_add(strip, rows):
+        return jnp.concatenate([strip.astype(F32), jnp.zeros((rows - 2, width), F32)], axis=0)
+
+    def last_add(strip, rows):
+        return jnp.concatenate([jnp.zeros((rows - 2, width), F32), strip.astype(F32)], axis=0)
+
+    for held, code, extra, base in (
+        (rows_a, top, from_above, 0),
+        (rows_b, bottom, from_below, lx - 2),
+    ):
+        for x in range(2):
+            v = held[x].astype(F32) + extra[x, 0:ly].astype(F32)
+            one = v[0:8] + first_add(from_left[base + x], 8)
+            two = v[ly - 8 : ly] + last_add(from_right[base + x], 8)
+            v = jnp.concatenate([one, v[8 : ly - 8], two], axis=0)
+            held[x] = jnp.where(code[x].astype(F32) == 0.0, 0.0, v).astype(BF16)
+    for x in range(2, lx - 2):
+        kept = jnp.where(first[x].astype(F32) == 0.0, 0.0, from_left[x].astype(F32))
+        kept = first_add(kept, 16)
+        cols_a[x - 2] = (cols_a[x - 2].astype(F32) + kept).astype(BF16)
+        kept = jnp.where(last[x].astype(F32) == 0.0, 0.0, from_right[x].astype(F32))
+        kept = last_add(kept, 16)
+        cols_b[x - 2] = (cols_b[x - 2].astype(F32) + kept).astype(BF16)
+    copies = [
+        pltpu.make_async_copy(held, at(joined), sems.at[n]) for n, (held, at) in enumerate(places)
+    ]
+    for copy in copies:
+        copy.start()
+    for copy in copies:
+        copy.wait()
+
+
+def join_call(grads, *strips):
+    lx, ly, width = grads.shape
+    anywhere = pl.BlockSpec(memory_space=pl.ANY)
     return pl.pallas_call(
         join_kernel,
-        out_shape=shape((lx, ly, width), BF16),
-        grid=(1,),
-        in_specs=[VMEM, pl.BlockSpec((lx, ly, 128), lambda i: (0, 0, 0))] + [VMEM] * 4,
-        out_specs=VMEM,
+        out_shape=shape(grads.shape, BF16),
+        in_specs=[anywhere] + [VMEM] * 8,
+        out_specs=anywhere,
+        scratch_shapes=[
+            pltpu.VMEM((2, ly, width), BF16),
+            pltpu.VMEM((2, ly, width), BF16),
+            pltpu.VMEM((lx - 4, 16, width), BF16),
+            pltpu.VMEM((lx - 4, 16, width), BF16),
+            pltpu.SemaphoreType.DMA((4,)),
+        ],
+        input_output_aliases={0: 0},
         name="join",
-    )(grads, packed, from_left, from_right, from_above, from_below)
-
-
-def pair_kernel(member, keep, got, *parts):
-    for o, part in enumerate(parts):
-        at = member[0] ^ o
-        part[...] = (keep[at].astype(F32) + got[at].astype(F32)).astype(BF16)
-
-
-def pair_call(member, keep, got, count):
-    rows = keep.shape[0] * keep.shape[1] // count
-    keep, got = keep.reshape(count, rows, 128), got.reshape(count, rows, 128)
-    return pl.pallas_call(
-        pair_kernel,
-        out_shape=tuple(shape((rows, 128), BF16) for _ in range(count)),
-        in_specs=[SMEM, VMEM, VMEM],
-        out_specs=(VMEM,) * count,
-        name="pair",
-    )(member, keep, got)
-
-
-def seat_kernel(member, *refs):
-    parts, whole = refs[:-1], refs[-1]
-    for o, part in enumerate(parts):
-        whole[member[0] ^ o] = part[...]
-
-
-def seat_call(member, parts):
-    rows = parts[0].shape[0]
-    return pl.pallas_call(
-        seat_kernel,
-        out_shape=shape((len(parts), rows, 128), BF16),
-        in_specs=[SMEM] + [VMEM] * len(parts),
-        out_specs=VMEM,
-        name="seat",
-    )(member, *parts)
-
-
-def sums_kernel(core, mine, other, grad_one, grad_two, both, *, scale):
-    both[core[0]] = mine[...]
-    both[1 - core[0]] = other[...]
+    )(grads, *strips)
+
+
+def sums_kernel(sums, grad_one, grad_two, *, scale):
     for n in range(27):
-        v = both[n // 14, n % 14].astype(F32).T * scale
+        v = sums[64 * n : 64 * n + 64].astype(F32).T * scale
         grad_one[n] = v[0:64]
         grad_two[n] = v[64:128]
 
 
-def sums_call(core, mine, other, scale):
+def sums_call(sums, scale):
     return pl.pallas_call(
         functools.partial(sums_kernel, scale=scale),
         out_shape=(shape((27, 64, 64), F32), shape((27, 64, 64), F32)),
-        in_specs=[SMEM, VMEM, VMEM],
+        in_specs=[VMEM],
         out_specs=(VMEM, VMEM),
-        scratch_shapes=[pltpu.VMEM((2, 14, 64, 128), BF16)],
         name="sums",
-    )(core, mine, other)
-
-
-def reduce_sums(keep, send):
-    nx, ny = lax.axis_size("gx"), lax.axis_size("gy")
-    gx, gy = lax.axis_index("gx"), lax.axis_index("gy")
-    core = (gy % 2).reshape(1)
-    lines = ny // 2
-    near = max(nx // 4, 1)
-    far = nx // near
-
-    got = flat_permute(send, lambda x, y: (x, y ^ 1))
-    count = lines * near
-    member = ((gy // 2) * near + gx % near).reshape(1)
-
-    def in_plane(o):
-        def move(x, y):
-            to = ((y // 2) * near + x % near) ^ o
-            return (x // near * near + to % near, to // near * 2 + y % 2)
-
-        return move
-
-    def along(o):
-        return lambda x, y: (((x // near) ^ o) * near + x % near, y)
-
-    parts = pair_call(member, keep, got, count)
-    own = parts[0].astype(F32)
-    for o in range(1, count):
-        own = own + flat_permute(parts[o], in_plane(o)).astype(F32)
-    own = own.astype(BF16)
-    values = [own.astype(F32)] + [flat_permute(own, along(o)).astype(F32) for o in range(1, far)]
-    while len(values) > 1:
-        values = [values[i] + values[i + 1] for i in range(0, len(values), 2)]
-    own = values[0].astype(BF16)
-    others = [flat_permute(own, in_plane(o)) for o in range(1, count)]
-    half = seat_call(member, [own] + others).reshape(keep.shape)
-    other = flat_permute(half, lambda x, y: (x, y ^ 1))
-    return core, half, other
+    )(sums)
 
 
 def shards(
     features, cotangent, low, high, weight_one, weight_two, scale_one, shift_one, scale_two,
     shift_two,
 ):
-    packed, top, bottom, first, last = edge_call(features, low, high)
+    nx, ny = lax.axis_size("gx"), lax.axis_size("gy")
+    top, bottom = strip_call(features, low, high)
     above = shifted_in(bottom, "gx", 1)
     below = shifted_in(top, "gx", -1)
-    slots, tiles, tiles_last = tile_call(low, high, weight_one, weight_two)
+    slots, tiles, tiles_last, packed, first, last = tile_call(
+        features, low, high, weight_one, weight_two
+    )
     to_left, to_right = side_call(above, below, first, last)
     left = shifted_in(to_right, "gy", 1)
     right = shifted_in(to_left, "gy", -1)
-    core = (lax.axis_index("gy") % 2).reshape(1)
     vectors = [v.reshape(1, -1) for v in (scale_one, shift_one, scale_two, shift_two)]
-    out, errors, grads, keep, send = brick_call(
-        slots, core, packed, above, below, left, right, cotangent, tiles, *vectors
-    )
-    core, half, other = reduce_sums(keep, send)
-    grads, grad_left, grad_right = input_call(slots, errors, grads, packed, tiles_last)
-    from_right = shifted_in(grad_left, "gy", -1)
-    from_left = shifted_in(grad_right, "gy", 1)
-    top, bottom = ends_call(grads, from_left, from_right)
-    from_below = shifted_in(top, "gx", -1)
-    from_above = shifted_in(bottom, "gx", 1)
-    grad_features = join_call(grads, packed, from_left, from_right, from_above, from_below)
-    capacity = lax.axis_size("gx") * lax.axis_size("gy") * SHARE
-    grad_one, grad_two = sums_call(core, half, other, 1.0 / capacity)
+    out, errors, grads, sums = brick_call(
+        slots, packed, above, below, left, right, cotangent, tiles, *vectors
+    )
+
+    devices = nx * ny
+    parts = sums.reshape(devices, -1, 128)
+    slots, errors, parts = lax.optimization_barrier((slots, errors, parts))
+    got = lax.all_to_all(parts, ("gx", "gy"), 0, 0, tiled=True)
+    own, grad_above, grad_below, grad_left, grad_right = input_call(
+        slots, errors, grads, packed, tiles_last
+    )
+    from_below = shifted_in(grad_above, "gx", -1)
+    from_above = shifted_in(grad_below, "gx", 1)
+    got, own = lax.optimization_barrier((got, own))
+    mine = jnp.sum(got.astype(F32), axis=0, keepdims=True).astype(BF16)
+    back = lax.all_to_all(
+        jnp.broadcast_to(mine, parts.shape), ("gx", "gy"), 0, 0, tiled=True
+    )
+    to_left, to_right = ends_call(grad_left, grad_right, from_above, from_below)
+    from_right = shifted_in(to_left, "gy", -1)
+    from_left = shifted_in(to_right, "gy", 1)
+    grad_features = join_call(
+        own, top, bottom, first, last, from_left, from_right, from_above, from_below
+    )
+    back, grad_features = lax.optimization_barrier((back, grad_features))
+    grad_one, grad_two = sums_call(back.reshape(-1, 128), 1.0 / (devices * SHARE))
     return (out, grad_features, grad_one, grad_two)
 
 
 def solution(mesh):
     whole = P("gx", "gy", None)
     columns = P("gx", "gy")
+
     return jax.shard_map(
         shards,
         mesh=mesh,

time: 116 us -> 102 us (0.88)
  Pallas kernels: 48.3 us -> 42.6 us
  waiting for transfers between devices: 24.7 us -> 21.1 us
  starting transfers between devices: 35.6 us -> 32.6 us
    ppermute x11 -> x0, starting transfers between devices: 13.5 us -> none  [flat_permute(): return lax.ppermute(array, ('gx', 'gy'), pairs)]
    ppermute x11 -> x0, waiting for transfers between devices: 11.1 us -> none  [flat_permute(): return lax.ppermute(array, ('gx', 'gy'), pairs)]
    all_to_all x0 -> x2, starting transfers between devices: none -> 8.47 us  [the longest x1 4.39 us: shards(): lax.all_to_all(jnp.broadcast_to(mine, parts.shape), ('gx', 'gy'), 0, 0, t...]
    pallas_call x6 -> x4, Pallas kernels: 20.5 us -> 14.7 us  [the longest x1 8.07 us: input_call(): pl.pallas_call(input_kernel, out_shape=(shape((lx, ly, width), BF16), sha...]
    all_to_all x0 -> x2, waiting for transfers between devices: none -> 4.71 us  [the longest x1 4.71 us: shards(): got = lax.all_to_all(parts, ('gx', 'gy'), 0, 0, tiled=True)]
    ppermute x8, waiting for transfers between devices: 13.6 us -> 16.4 us  [shifted_in(): return lax.ppermute(array, axis, pairs)]
    ppermute x8, starting transfers between devices: 22.1 us -> 24.1 us  [shifted_in(): return lax.ppermute(array, axis, pairs)]
    unnamed x28 -> x22, local copies, waits for them, and re-layouts: 4.74 us -> 3.37 us
  transfers between devices with their start and end apart: 19 -> 10, of which waited for: 16 -> 5; matrix products, arithmetic and copies ran while one was open for 0% -> 0% of each run, Pallas kernels for 15% -> 17%
where the time goes in v1:
time: 102 us; the launch traced here: 101 us
  Pallas kernels  42.6 us (42%)
  starting transfers between devices  32.6 us (32%)
  waiting for transfers between devices  21.1 us (21%)
  local copies, waits for them, and re-layouts  4.2 us (4%)
    ppermute x8, starting transfers between devices, shifted_in(): return lax.ppermute(array, axis, pairs)  24.1 us
    pallas_call x1, Pallas kernels, brick_call(): pl.pallas_call(brick_kernel, out_shape=(shape((lx, ly, width), BF16), sha...  19.7 us
    ppermute x8, waiting for transfers between devices, shifted_in(): return lax.ppermute(array, axis, pairs)  16.4 us
    pallas_call x1, Pallas kernels, input_call(): pl.pallas_call(input_kernel, out_shape=(shape((lx, ly, width), BF16), sha...  8.07 us
    all_to_all x1, waiting for transfers between devices, shards(): got = lax.all_to_all(parts, ('gx', 'gy'), 0, 0, tiled=True)  4.71 us
    all_to_all x1, starting transfers between devices, shards(): lax.all_to_all(jnp.broadcast_to(mine, parts.shape), ('gx', 'gy'), 0, 0, t...  4.39 us
    all_to_all x1, starting transfers between devices, shards(): got = lax.all_to_all(parts, ('gx', 'gy'), 0, 0, tiled=True)  4.08 us
    pallas_call x1, Pallas kernels, tile_call(): pl.pallas_call(tile_kernel, out_shape=(shape((3 * ACT_MAX,), jnp.int32),...  4.08 us
  transfers between devices with their start and end apart: 10, of which 5 were waited for; matrix products, arithmetic and copies ran while one was open for 0% of the time, Pallas kernels for 17%

profile of v1, /device:TPU:17, one launch (start us, length us, event | category | flops | bytes accessed | tf_op | source)
XLA Modules:
  0.0 101.4 jit_solution(8442759803951054698)
XLA Ops:
  0.6 1.9 %strips.1 = (bf16[2,64,512]{2,1,0:T(8,128)(2,1)}, bf16[2,64,512]{2,1,0:T(8,128)(2,1)}) custom-call(bf16[16,64,512]{2,1,0:T(8,128)(2,1)} %bottom_in.1, bf16[16,64,512]{2,1,0:T(8,128)(2,1)} %bottom_in.1, s32[16,64]{1,0:T(8,128)} %low.3, s32[16,64]{1,0:T(8,128)} %high.3), custom_call_target="tpu_custom_call" | custom-call | tf_op jit(solution)/shard_map/strips/pallas_call | solution.py:87
  2.5 3.1 %collective-permute-start = (bf16[2,64,512]{2,1,0:T(8,128)(2,1)}, bf16[2,64,512]{2,1,0:T(8,128)(2,1)S(1)}, u32[]{:S(2)}, u32[]{:S(2)}) collective-permute-start(bf16[2,64,512]{2,1,0:T(8,128)(2,1)} %get-tuple-element.36.bottom), channel_id=1, source_target_pairs={{0,4},{4,8},{8,12},{12,16},{16,20},{20,24},{24,28},{1,5},{5,9},{9,... | collective-permute-start | bytes 393224 | tf_op jit(solution)/shard_map/ppermute | solution.py:21
  5.6 3.1 %collective-permute-start.1 = (bf16[2,64,512]{2,1,0:T(8,128)(2,1)}, bf16[2,64,512]{2,1,0:T(8,128)(2,1)S(1)}, u32[]{:S(2)}, u32[]{:S(2)}) collective-permute-start(bf16[2,64,512]{2,1,0:T(8,128)(2,1)} %get-tuple-element.37.top), channel_id=1, source_target_pairs={{4,0},{8,4},{12,8},{16,12},{20,16},{24,20},{28,24},{5,1},{9,5},{13... | collective-permute-start | bytes 393224 | tf_op jit(solution)/shard_map/ppermute | solution.py:21
  8.7 4.1 %tiles.1 = (s32[12]{0:T(128)}, bf16[3,9,4,64,128]{4,3,2,1,0:T(8,128)(2,1)}, bf16[9,4,64,128]{3,2,1,0:T(8,128)(2,1)}, bf16[16,64,512]{2,1,0:T(8,128)(2,1)}, bf16[...) custom-call(bf16[16,64,512]{2,1,0:T(8,128)(2,1)} %bottom_in.1, s32[16,64]{1,0:T(8,128)} %low.3, s32[16,64]{1,0:T(8,128)} %high.3, ...), custom_call_target="tpu_custom_call" | custom-call | tf_op jit(solution)/shard_map/tiles/pallas_call | solution.py:190
  12.8 0.0 collective-permute-done.above
  12.8 0.0 copy-start.3
  12.8 0.2 collective-permute-done.1.below
  13.0 0.0 copy-start.4
  13.0 0.5 copy-done.3
  13.5 0.2 copy-done.4
  13.7 1.6 %sides.1 = (bf16[20,2,512]{2,1,0:T(2,128)(2,1)}, bf16[20,2,512]{2,1,0:T(2,128)(2,1)}) custom-call(bf16[2,64,512]{2,1,0:T(8,128)(2,1)} %copy-done.3, bf16[2,64,512]{2,1,0:T(8,128)(2,1)} %copy-done.4, bf16[16,2,512]{2,1,0:T(2,128)(2,1)} %get-tuple-element.38.first, bf16[16,2,512]{2,1,0:T(2,128)(2,1)} %get-tuple-element.39.last), custom_call_target="tpu_custom_call" | custom-call | tf_op jit(solution)/shard_map/sides/pallas_call | solution.py:116
  15.3 4.2 %collective-permute-start.2 = (bf16[20,2,512]{2,1,0:T(2,128)(2,1)}, bf16[20,2,512]{2,1,0:T(2,128)(2,1)S(1)}, u32[]{:S(2)}, u32[]{:S(2)}) collective-permute-start(bf16[20,2,512]{2,1,0:T(2,128)(2,1)} %get-tuple-element.40), channel_id=1, source_target_pairs={{0,1},{1,2},{2,3},{4,5},{5,6},{6,7},{8,9},{9,10},{10,11},{12,13},{... | collective-permute-start | bytes 122888 | tf_op jit(solution)/shard_map/ppermute | solution.py:21
  19.5 1.9 %collective-permute-start.3 = (bf16[20,2,512]{2,1,0:T(2,128)(2,1)}, bf16[20,2,512]{2,1,0:T(2,128)(2,1)S(1)}, u32[]{:S(2)}, u32[]{:S(2)}) collective-permute-start(bf16[20,2,512]{2,1,0:T(2,128)(2,1)} %get-tuple-element.41), channel_id=1, source_target_pairs={{1,0},{2,1},{3,2},{5,4},{6,5},{7,6},{9,8},{10,9},{11,10},{13,12},{... | collective-permute-start | bytes 122888 | tf_op jit(solution)/shard_map/ppermute | solution.py:21
  21.5 0.0 collective-permute-done.2.left
  21.5 0.0 copy-start.5
  21.5 3.6 %collective-permute-done.3.right = bf16[20,2,512]{2,1,0:T(2,128)(2,1)S(1)} collective-permute-done((bf16[20,2,512]{2,1,0:T(2,128)(2,1)}, bf16[20,2,512]{2,1,0:T(2,128)(2,1)S(1)}, u32[]{:S(2)}, u32[]{:S(2)}) %collective-permute-start.3) | collective-permute-done | bytes 40992 | tf_op jit(solution)/shard_map/ppermute | solution.py:21
  25.1 0.0 copy-start.6
  25.1 0.0 copy-done.5
  25.1 0.6 copy-done.6
  25.7 19.7 %bricks.1 = (bf16[16,64,512]{2,1,0:T(8,128)(2,1)}, bf16[640,512]{1,0:T(8,128)(2,1)}, f32[4,8,8,512]{3,2,1,0:T(8,128)}, bf16[28,64,128]{2,1,0:T(8,128)(2,1)}) custom-call(s32[12]{0:T(128)} %get-tuple-element.47.slots, bf16[16,64,512]{2,1,0:T(8,128)(2,1)} %get-tuple-element.35.packed, bf16[2,64,512]{2,1,0:T(8,128)(2,1)} %copy-done.3, ...), custom_call_target="tpu_custom_call" | custom-call | tf_op jit(solution)/shard_map/bricks/pallas_call | solution.py:437
  45.4 4.1 %all-to-all-start = ((bf16[32,56,128]{2,1,0:T(8,128)(2,1)}), bf16[32,56,128]{2,1,0:T(8,128)(2,1)S(1)}, u32[]{:S(2)}, u32[]{:S(2)}) async-start(bf16[32,56,128]{2,1,0:T(8,128)(2,1)} %bitcast.7), calls=%async_computation | async-start | bytes 917504 | tf_op jit(solution)/shard_map/all_to_all | solution.py:709
  49.5 8.1 %inputs.1 = (bf16[16,64,512]{2,1,0:T(8,128)(2,1)}, bf16[2,72,512]{2,1,0:T(8,128)(2,1)}, bf16[2,72,512]{2,1,0:T(8,128)(2,1)}, bf16[16,2,512]{2,1,0:T(2,128)(2,1)}, bf16[16,2,512]{2,1,0:T(2,128)(2,1)}) custom-call(s32[12]{0:T(128)} %get-tuple-element.47.slots, bf16[640,512]{1,0:T(8,128)(2,1)} %get-tuple-element.48.errors, ...), custom_call_target="tpu_custom_call" | custom-call | tf_op jit(solution)/shard_map/inputs/pallas_call | solution.py:552
  57.6 0.0 copy-start.10
  57.6 4.7 %all-to-all-done = bf16[32,56,128]{2,1,0:T(8,128)(2,1)S(1)} async-done(((bf16[32,56,128]{2,1,0:T(8,128)(2,1)}), bf16[32,56,128]{2,1,0:T(8,128)(2,1)S(1)}, u32[]{:S(2)}, u32[]{:S(2)}) %all-to-all-start) | async-done | bytes 458784 | tf_op jit(solution)/shard_map/all_to_all | solution.py:709
  62.3 0.1 reduce_sum.12
  62.4 0.8 broadcast_in_dim.2
  63.2 4.4 %all-to-all-start.1 = ((bf16[32,56,128]{2,1,0:T(8,128)(2,1)}), bf16[32,56,128]{2,1,0:T(8,128)(2,1)S(1)}, u32[]{:S(2)}, u32[]{:S(2)}) async-start(bf16[32,56,128]{2,1,0:T(8,128)(2,1)} %broadcast_in_dim.2), calls=%async_computation.1 | async-start | bytes 917504 | tf_op jit(solution)/shard_map/all_to_all | solution.py:717
  67.6 0.0 copy-done.10
  67.6 3.1 %collective-permute-start.4 = (bf16[2,72,512]{2,1,0:T(8,128)(2,1)S(1)}, bf16[2,72,512]{2,1,0:T(8,128)(2,1)S(1)}, u32[]{:S(2)}, u32[]{:S(2)}) collective-permute-start(bf16[2,72,512]{2,1,0:T(8,128)(2,1)S(1)} %copy-done.10), channel_id=1, source_target_pairs={{0,4},{4,8},{8,12},{12,16},{16,20},{20,24},{24,28},{1,5},{5,9},{9,... | collective-permute-start | bytes 442376 | tf_op jit(solution)/shard_map/ppermute | solution.py:21
  70.7 0.0 copy-done.9
  70.7 3.1 %collective-permute-start.5 = (bf16[2,72,512]{2,1,0:T(8,128)(2,1)S(1)}, bf16[2,72,512]{2,1,0:T(8,128)(2,1)S(1)}, u32[]{:S(2)}, u32[]{:S(2)}) collective-permute-start(bf16[2,72,512]{2,1,0:T(8,128)(2,1)S(1)} %copy-done.9), channel_id=1, source_target_pairs={{4,0},{8,4},{12,8},{16,12},{20,16},{24,20},{28,24},{5,1},{9,5},{13... | collective-permute-start | bytes 442376 | tf_op jit(solution)/shard_map/ppermute | solution.py:21
  73.8 9.1 %collective-permute-done.4.from_above = bf16[2,72,512]{2,1,0:T(8,128)(2,1)S(1)} collective-permute-done((bf16[2,72,512]{2,1,0:T(8,128)(2,1)S(1)}, bf16[2,72,512]{2,1,0:T(8,128)(2,1)S(1)}, u32[]{:S(2)}, u32[]{:S(2)}) %collective-permute-start.4) | collective-permute-done | bytes 147488 | tf_op jit(solution)/shard_map/ppermute | solution.py:21
  82.9 0.0 collective-permute-done.5.from_below
  82.9 0.7 copy-done.1
  83.6 0.1 copy-done.2
  83.6 1.4 %ends.1 = (bf16[16,2,512]{2,1,0:T(2,128)(2,1)}, bf16[16,2,512]{2,1,0:T(2,128)(2,1)}) custom-call(bf16[16,2,512]{2,1,0:T(2,128)(2,1)} %get-tuple-element.54.left, bf16[16,2,512]{2,1,0:T(2,128)(2,1)} %get-tuple-element.55.right, bf16[2,72,512]{2,1,0:T(8,128)(2,1)} %copy-done.1, bf16[2,72,512]{2,1,0:T(8,128)(2,1)} %copy-done.2), custom_call_target="tpu_custom_call" | custom-call | tf_op jit(solution)/shard_map/ends/pallas_call | solution.py:588
  85.1 3.7 %collective-permute-start.6 = (bf16[16,2,512]{2,1,0:T(2,128)(2,1)}, bf16[16,2,512]{2,1,0:T(2,128)(2,1)S(1)}, u32[]{:S(2)}, u32[]{:S(2)}) collective-permute-start(bf16[16,2,512]{2,1,0:T(2,128)(2,1)} %get-tuple-element.58), channel_id=1, source_target_pairs={{0,1},{1,2},{2,3},{4,5},{5,6},{6,7},{8,9},{9,10},{10,11},{12,13},{... | collective-permute-start | bytes 98312 | tf_op jit(solution)/shard_map/ppermute | solution.py:21
  88.8 1.9 %collective-permute-start.7 = (bf16[16,2,512]{2,1,0:T(2,128)(2,1)}, bf16[16,2,512]{2,1,0:T(2,128)(2,1)S(1)}, u32[]{:S(2)}, u32[]{:S(2)}) collective-permute-start(bf16[16,2,512]{2,1,0:T(2,128)(2,1)} %get-tuple-element.59), channel_id=1, source_target_pairs={{1,0},{2,1},{3,2},{5,4},{6,5},{7,6},{9,8},{10,9},{11,10},{13,12},{... | collective-permute-start | bytes 98312 | tf_op jit(solution)/shard_map/ppermute | solution.py:21
  90.7 0.0 collective-permute-done.6.from_left
  90.7 0.0 copy-start.7
  90.7 3.5 %collective-permute-done.7.from_right = bf16[16,2,512]{2,1,0:T(2,128)(2,1)S(1)} collective-permute-done((bf16[16,2,512]{2,1,0:T(2,128)(2,1)}, bf16[16,2,512]{2,1,0:T(2,128)(2,1)S(1)}, u32[]{:S(2)}, u32[]{:S(2)}) %collective-permute-start.7) | collective-permute-done | bytes 32800 | tf_op jit(solution)/shard_map/ppermute | solution.py:21
  94.2 0.0 copy-done.7
  94.2 0.6 copy-done.8
  94.8 3.3 %join.1 = bf16[16,64,512]{2,1,0:T(8,128)(2,1)} custom-call(bf16[16,64,512]{2,1,0:T(8,128)(2,1)} %get-tuple-element.53.grads, bf16[2,64,512]{2,1,0:T(8,128)(2,1)} %get-tuple-element.37.top, bf16[2,64,512]{2,1,0:T(8,128)(2,1)} %get-tuple-element.36.bottom, bf16[16,2,512]{2,1,0:T(2,128)(2,1)} %get-tuple-element.38.first, ...), custom_call_target="tpu_custom_call", output_to_operand_aliasing={{}: (0, {})} | custom-call | tf_op jit(solution)/shard_map/join/pallas_call | solution.py:653
  98.1 0.0 all-to-all-done.1
  98.1 0.0 copy-start
  98.1 0.8 copy-done
  98.9 2.5 %sums.1 = (f32[27,64,64]{2,1,0:T(8,128)}, f32[27,64,64]{2,1,0:T(8,128)}) custom-call(bf16[1792,128]{1,0:T(8,128)(2,1)} %bitcast.6), custom_call_target="tpu_custom_call" | custom-call | tf_op jit(solution)/shard_map/sums/pallas_call | solution.py:678
  (4 shorter events, 0.0 us)
Async XLA Ops:
  2.5 10.3 %collective-permute-start = (bf16[2,64,512]{2,1,0:T(8,128)(2,1)}, bf16[2,64,512]{2,1,0:T(8,128)(2,1)S(1)}, u32[]{:S(2)}, u32[]{:S(2)}) collective-permute-start(bf16[2,64,512]{2,1,0:T(8,128)(2,1)} %get-tuple-element.36.bottom), channel_id=1, source_target_pairs={{0,4},{4,8},{8,12},{12,16},{16,20},{20,24},{24,28},{1,5},{5,9},{9,... | collective-permute-start | bytes 393224 | tf_op jit(solution)/shard_map/ppermute | solution.py:21
  5.6 7.4 %collective-permute-start.1 = (bf16[2,64,512]{2,1,0:T(8,128)(2,1)}, bf16[2,64,512]{2,1,0:T(8,128)(2,1)S(1)}, u32[]{:S(2)}, u32[]{:S(2)}) collective-permute-start(bf16[2,64,512]{2,1,0:T(8,128)(2,1)} %get-tuple-element.37.top), channel_id=1, source_target_pairs={{4,0},{8,4},{12,8},{16,12},{20,16},{24,20},{28,24},{5,1},{9,5},{13... | collective-permute-start | bytes 393224 | tf_op jit(solution)/shard_map/ppermute | solution.py:21
  12.8 0.7 copy-start.3
  13.0 0.7 copy-start.4
  15.3 6.2 %collective-permute-start.2 = (bf16[20,2,512]{2,1,0:T(2,128)(2,1)}, bf16[20,2,512]{2,1,0:T(2,128)(2,1)S(1)}, u32[]{:S(2)}, u32[]{:S(2)}) collective-permute-start(bf16[20,2,512]{2,1,0:T(2,128)(2,1)} %get-tuple-element.40), channel_id=1, source_target_pairs={{0,1},{1,2},{2,3},{4,5},{5,6},{6,7},{8,9},{9,10},{10,11},{12,13},{... | collective-permute-start | bytes 122888 | tf_op jit(solution)/shard_map/ppermute | solution.py:21
  19.5 5.5 %collective-permute-start.3 = (bf16[20,2,512]{2,1,0:T(2,128)(2,1)}, bf16[20,2,512]{2,1,0:T(2,128)(2,1)S(1)}, u32[]{:S(2)}, u32[]{:S(2)}) collective-permute-start(bf16[20,2,512]{2,1,0:T(2,128)(2,1)} %get-tuple-element.41), channel_id=1, source_target_pairs={{1,0},{2,1},{3,2},{5,4},{6,5},{7,6},{9,8},{10,9},{11,10},{13,12},{... | collective-permute-start | bytes 122888 | tf_op jit(solution)/shard_map/ppermute | solution.py:21
  21.5 3.6 %copy-start.5 = (bf16[20,2,512]{2,1,0:T(2,128)(2,1)}, bf16[20,2,512]{2,1,0:T(2,128)(2,1)S(1)}, u32[]{:S(2)}) copy-start(bf16[20,2,512]{2,1,0:T(2,128)(2,1)S(1)} %collective-permute-done.2.left) | copy-start | bytes 122884
  25.1 0.6 copy-start.6
  45.4 16.9 %all-to-all-start = ((bf16[32,56,128]{2,1,0:T(8,128)(2,1)}), bf16[32,56,128]{2,1,0:T(8,128)(2,1)S(1)}, u32[]{:S(2)}, u32[]{:S(2)}) async-start(bf16[32,56,128]{2,1,0:T(8,128)(2,1)} %bitcast.7), calls=%async_computation | async-start | bytes 917504 | tf_op jit(solution)/shard_map/all_to_all | solution.py:709
  57.6 10.0 %copy-start.10 = (bf16[2,72,512]{2,1,0:T(8,128)(2,1)S(1)}, bf16[2,72,512]{2,1,0:T(8,128)(2,1)}, u32[]{:S(2)}) copy-start(bf16[2,72,512]{2,1,0:T(8,128)(2,1)} %get-tuple-element.56) | copy-start | bytes 442372
  57.6 13.1 %copy-start.9 = (bf16[2,72,512]{2,1,0:T(8,128)(2,1)S(1)}, bf16[2,72,512]{2,1,0:T(8,128)(2,1)}, u32[]{:S(2)}) copy-start(bf16[2,72,512]{2,1,0:T(8,128)(2,1)} %get-tuple-element.57) | copy-start | bytes 442372
  63.2 34.9 %all-to-all-start.1 = ((bf16[32,56,128]{2,1,0:T(8,128)(2,1)}), bf16[32,56,128]{2,1,0:T(8,128)(2,1)S(1)}, u32[]{:S(2)}, u32[]{:S(2)}) async-start(bf16[32,56,128]{2,1,0:T(8,128)(2,1)} %broadcast_in_dim.2), calls=%async_computation.1 | async-start | bytes 917504 | tf_op jit(solution)/shard_map/all_to_all | solution.py:717
  67.6 15.3 %collective-permute-start.4 = (bf16[2,72,512]{2,1,0:T(8,128)(2,1)S(1)}, bf16[2,72,512]{2,1,0:T(8,128)(2,1)S(1)}, u32[]{:S(2)}, u32[]{:S(2)}) collective-permute-start(bf16[2,72,512]{2,1,0:T(8,128)(2,1)S(1)} %copy-done.10), channel_id=1, source_target_pairs={{0,4},{4,8},{8,12},{12,16},{16,20},{20,24},{24,28},{1,5},{5,9},{9,... | collective-permute-start | bytes 442376 | tf_op jit(solution)/shard_map/ppermute | solution.py:21
  70.7 12.2 %collective-permute-start.5 = (bf16[2,72,512]{2,1,0:T(8,128)(2,1)S(1)}, bf16[2,72,512]{2,1,0:T(8,128)(2,1)S(1)}, u32[]{:S(2)}, u32[]{:S(2)}) collective-permute-start(bf16[2,72,512]{2,1,0:T(8,128)(2,1)S(1)} %copy-done.9), channel_id=1, source_target_pairs={{4,0},{8,4},{12,8},{16,12},{20,16},{24,20},{28,24},{5,1},{9,5},{13... | collective-permute-start | bytes 442376 | tf_op jit(solution)/shard_map/ppermute | solution.py:21
  82.9 0.7 copy-start.1
  82.9 0.7 copy-start.2
  85.1 5.6 %collective-permute-start.6 = (bf16[16,2,512]{2,1,0:T(2,128)(2,1)}, bf16[16,2,512]{2,1,0:T(2,128)(2,1)S(1)}, u32[]{:S(2)}, u32[]{:S(2)}) collective-permute-start(bf16[16,2,512]{2,1,0:T(2,128)(2,1)} %get-tuple-element.58), channel_id=1, source_target_pairs={{0,1},{1,2},{2,3},{4,5},{5,6},{6,7},{8,9},{9,10},{10,11},{12,13},{... | collective-permute-start | bytes 98312 | tf_op jit(solution)/shard_map/ppermute | solution.py:21
  88.8 5.4 %collective-permute-start.7 = (bf16[16,2,512]{2,1,0:T(2,128)(2,1)}, bf16[16,2,512]{2,1,0:T(2,128)(2,1)S(1)}, u32[]{:S(2)}, u32[]{:S(2)}) collective-permute-start(bf16[16,2,512]{2,1,0:T(2,128)(2,1)} %get-tuple-element.59), channel_id=1, source_target_pairs={{1,0},{2,1},{3,2},{5,4},{6,5},{7,6},{9,8},{10,9},{11,10},{13,12},{... | collective-permute-start | bytes 98312 | tf_op jit(solution)/shard_map/ppermute | solution.py:21
  90.7 3.5 %copy-start.7 = (bf16[16,2,512]{2,1,0:T(2,128)(2,1)}, bf16[16,2,512]{2,1,0:T(2,128)(2,1)S(1)}, u32[]{:S(2)}) copy-start(bf16[16,2,512]{2,1,0:T(2,128)(2,1)S(1)} %collective-permute-done.6.from_left) | copy-start | bytes 98308
  94.2 0.6 copy-start.8
  98.1 0.8 copy-start

commit v2 on v1

--- a/solution.py
+++ b/solution.py
@@ -47,6 +47,11 @@
 VMEM = pl.BlockSpec(memory_space=pltpu.VMEM)
 SMEM = pl.BlockSpec(memory_space=pltpu.SMEM)
 shape = jax.ShapeDtypeStruct
+held = pltpu.VMEM
+
+
+def near(*arrays):
+    return [pltpu.with_memory_space_constraint(a, pltpu.VMEM) for a in arrays]
 
 
 EMPTY_FEATURE = 256.0
@@ -86,7 +91,7 @@
     end = lx // 2 - 1
     return pl.pallas_call(
         strip_kernel,
-        out_shape=(shape((2, ly, width), BF16), shape((2, ly, width), BF16)),
+        out_shape=(held((2, ly, width), BF16), held((2, ly, width), BF16)),
         grid=(1,),
         in_specs=[
             pl.BlockSpec((2, ly, width), lambda i: (0, 0, 0)),
@@ -95,6 +100,7 @@
             VMEM,
         ],
         out_specs=(VMEM, VMEM),
+        compiler_params=pltpu.CompilerParams(vmem_limit_bytes=12 << 20),
         name="strips",
     )(features, features, low, high)
 
@@ -115,11 +121,12 @@
     tall = (first.shape[0] + 4,) + first.shape[1:]
     return pl.pallas_call(
         side_kernel,
-        out_shape=(shape(tall, BF16), shape(tall, BF16)),
+        out_shape=(held(tall, BF16), held(tall, BF16)),
         in_specs=[VMEM] * 4,
         out_specs=(VMEM, VMEM),
+        compiler_params=pltpu.CompilerParams(vmem_limit_bytes=12 << 20),
         name="sides",
-    )(above, below, first, last)
+    )(*near(above, below, first, last))
 
 
 def tile_kernel(
@@ -191,14 +198,15 @@
         tile_kernel,
         out_shape=(
             shape((3 * ACT_MAX,), jnp.int32),
-            shape((3, 9, 4, 64, 128), BF16),
-            shape((9, 4, 64, 128), BF16),
-            shape(features.shape, BF16),
-            shape((lx, 2, width), BF16),
-            shape((lx, 2, width), BF16),
+            held((3, 9, 4, 64, 128), BF16),
+            held((9, 4, 64, 128), BF16),
+            held(features.shape, BF16),
+            held((lx, 2, width), BF16),
+            held((lx, 2, width), BF16),
         ),
         in_specs=[VMEM] * 5,
         out_specs=(SMEM,) + (VMEM,) * 5,
+        compiler_params=pltpu.CompilerParams(vmem_limit_bytes=16 << 20),
         name="tiles",
     )(features, low, high, weight_one, weight_two)
 
@@ -211,8 +219,8 @@
                 for q in range(2):
                     d = r - 2 * q
                     if 0 <= d < 4:
-                        row = ((r // 2) * 3 + oy) * 128 + (r % 2) * 64
-                        bands[ox, row : row + 64, 128 * q : 128 * q + 128] = tile_at(
+                        row = 1152 * ox + ((r // 2) * 3 + oy) * 128 + (r % 2) * 64
+                        bands[row : row + 64, 128 * q : 128 * q + 128] = tile_at(
                             ox * 3 + oy, d
                         )
 
@@ -220,12 +228,13 @@
 def convolve(source, bands, acc, xs):
     rows = source.shape[0] * xs * 16
     for half in range(2):
-        total = None
-        for ox in range(3):
-            part = source[:, ox : ox + xs, :, 768 * half : 768 * half + 1152]
-            part = jnp.dot(part.reshape(rows, 1152), bands[ox], preferred_element_type=F32)
-            total = part if total is None else total + part
-        acc[0:rows, 256 * half : 256 * half + 256] = total
+        parts = [
+            source[:, ox : ox + xs, :, 768 * half : 768 * half + 1152].reshape(rows, 1152)
+            for ox in range(3)
+        ]
+        acc[0:rows, 256 * half : 256 * half + 256] = jnp.dot(
+            jnp.concatenate(parts, axis=1), bands[...], preferred_element_type=F32
+        )
 
 
 def place(slots, s):
@@ -402,25 +411,29 @@
 
     def weight_sums(source, errors_t, xs, which):
         rows = source.shape[0] * xs * 16
-        for ox in range(3):
-            sums = None
-            for p in range(5):
-                part = source[:, ox : ox + xs, :, 384 * p : 384 * p + 384].reshape(rows, 384)
-                part = jnp.dot(
-                    errors_t[128 * p : 128 * p + 256, :], part, preferred_element_type=F32
-                )
-                sums = part if sums is None else sums + part
-            for oy in range(3):
-                block = sums[:, 128 * oy : 128 * oy + 128]
-                turned = turn(block)
-                for oz in range(3):
-                    one, two = 64 * (2 - oz), 64 * (3 - oz)
-                    n = ox * 9 + oy * 3 + oz
-                    if which == 0:
-                        folded[n] = block[one : one + 64] + turned[two : two + 64]
-                    else:
-                        v = turned[one : one + 64] + block[two : two + 64]
-                        total[n] = jnp.where(low_row, folded[n], v).astype(BF16)
+        sums = None
+        for p in range(5):
+            parts = [
+                source[:, ox : ox + xs, :, 384 * p : 384 * p + 384].reshape(rows, 384)
+                for ox in range(3)
+            ]
+            part = jnp.dot(
+                errors_t[128 * p : 128 * p + 256, :],
+                jnp.concatenate(parts, axis=1),
+                preferred_element_type=F32,
+            )
+            sums = part if sums is None else sums + part
+        for tap in range(9):
+            block = sums[:, 128 * tap : 128 * tap + 128]
+            turned = turn(block)
+            for oz in range(3):
+                one, two = 64 * (2 - oz), 64 * (3 - oz)
+                n = tap * 3 + oz
+                if which == 0:
+                    folded[n] = block[one : one + 64] + turned[two : two + 64]
+                else:
+                    v = turned[one : one + 64] + block[two : two + 64]
+                    total[n] = jnp.where(low_row, folded[n], v).astype(BF16)
 
     et1[0:128] = jnp.zeros((128, et1.shape[1]), BF16)
     et1[640:768] = jnp.zeros((128, et1.shape[1]), BF16)
@@ -438,18 +451,18 @@
         brick_kernel,
         out_shape=(
             shape((lx, ly, width), BF16),
-            shape((n * 160, width), BF16),
-            shape((n, 8, 8, width), F32),
-            shape((28, 64, 128), BF16),
+            held((n * 160, width), BF16),
+            held((n, 8, 8, width), F32),
+            held((28, 64, 128), BF16),
         ),
         in_specs=[SMEM] + [VMEM] * 11,
         out_specs=(VMEM,) * 4,
         scratch_shapes=[
             pltpu.VMEM((5, lx + 4, wide, 128), F32),
             pltpu.VMEM((4, lx + 4, wide, 128), F32),
-            pltpu.VMEM((3, 1152, 256), BF16),
-            pltpu.VMEM((3, 1152, 256), BF16),
-            pltpu.VMEM((3, 1152, 256), BF16),
+            pltpu.VMEM((3456, 256), BF16),
+            pltpu.VMEM((3456, 256), BF16),
+            pltpu.VMEM((3456, 256), BF16),
             pltpu.VMEM((n, 12, 16, 1920), BF16),
             pltpu.VMEM((n // 2, 10, 16, 1920), BF16),
             pltpu.VMEM((n, 12, 16, 1920), BF16),
@@ -462,8 +475,15 @@
             pltpu.VMEM((768, n * 160), BF16),
             pltpu.VMEM((27, 64, 128), F32),
         ],
+        compiler_params=pltpu.CompilerParams(vmem_limit_bytes=40 << 20),
         name="bricks",
-    )(slots, packed, above, below, left, right, cotangent, tiles, *vectors)
+    )(
+        slots,
+        *near(packed, above, below, left, right),
+        cotangent,
+        *near(tiles),
+        *vectors,
+    )
 
 
 def input_kernel(
@@ -553,46 +573,46 @@
         input_kernel,
         out_shape=(
             shape((lx, ly, width), BF16),
-            shape((2, ly + 8, width), BF16),
-            shape((2, ly + 8, width), BF16),
-            shape((lx, 2, width), BF16),
-            shape((lx, 2, width), BF16),
+            held((2, ly + 8, width), BF16),
+            held((2, ly + 8, width), BF16),
+            held((lx, 2, width), BF16),
+            held((lx, 2, width), BF16),
         ),
         in_specs=[SMEM] + [VMEM] * 4,
         out_specs=(VMEM,) * 5,
         scratch_shapes=[
             pltpu.VMEM((5, 14, 24, 128), F32),
             pltpu.VMEM((n, 14, 16, 1920), BF16),
-            pltpu.VMEM((3, 1152, 256), BF16),
+            pltpu.VMEM((3456, 256), BF16),
             pltpu.VMEM((n * 192, width), F32),
             pltpu.VMEM((4, lx + 4, ly + 16, 128), F32),
         ],
+        compiler_params=pltpu.CompilerParams(vmem_limit_bytes=24 << 20),
         name="inputs",
-    )(slots, errors, grads, packed, tiles)
+    )(slots, *near(errors, grads, packed, tiles))
 
 
 def ends_kernel(left, right, from_above, from_below, to_left, to_right):
     lx = left.shape[0]
+    ly = from_above.shape[1] - 8
     to_left[...] = left[...]
     to_right[...] = right[...]
     for source, base in ((from_above, 0), (from_below, lx - 2)):
         for x in range(2):
-            v = source[x].astype(F32)
+            v = source[x, ly : ly + 8].astype(F32)
             for strip, target, at in ((left, to_left, 0), (right, to_right, 2)):
                 target[base + x] = (strip[base + x].astype(F32) + v[at : at + 2]).astype(BF16)
 
 
 def ends_call(left, right, from_above, from_below):
-    ly, width = from_above.shape[1] - 8, from_above.shape[2]
-    corners = pl.BlockSpec((2, 8, width), lambda i: (0, ly // 8, 0))
     return pl.pallas_call(
         ends_kernel,
-        out_shape=(shape(left.shape, BF16), shape(left.shape, BF16)),
-        grid=(1,),
-        in_specs=[VMEM, VMEM, corners, corners],
+        out_shape=(held(left.shape, BF16), held(left.shape, BF16)),
+        in_specs=[VMEM] * 4,
         out_specs=(VMEM, VMEM),
+        compiler_params=pltpu.CompilerParams(vmem_limit_bytes=12 << 20),
         name="ends",
-    )(left, right, from_above, from_below)
+    )(*near(left, right, from_above, from_below))
 
 
 def join_kernel(
@@ -663,25 +683,31 @@
             pltpu.SemaphoreType.DMA((4,)),
         ],
         input_output_aliases={0: 0},
+        compiler_params=pltpu.CompilerParams(vmem_limit_bytes=16 << 20),
         name="join",
-    )(grads, *strips)
+    )(grads, *near(*strips))
 
 
 def sums_kernel(sums, grad_one, grad_two, *, scale):
-    for n in range(27):
-        v = sums[64 * n : 64 * n + 64].astype(F32).T * scale
+    base = pl.program_id(0) * 9
+    for n in range(9):
+        at = pl.multiple_of(64 * (base + n), 64)
+        v = sums[pl.ds(at, 64)].astype(F32).T * scale
         grad_one[n] = v[0:64]
         grad_two[n] = v[64:128]
 
 
 def sums_call(sums, scale):
+    taps = pl.BlockSpec((9, 64, 64), lambda i: (i, 0, 0))
     return pl.pallas_call(
         functools.partial(sums_kernel, scale=scale),
         out_shape=(shape((27, 64, 64), F32), shape((27, 64, 64), F32)),
+        grid=(3,),
         in_specs=[VMEM],
-        out_specs=(VMEM, VMEM),
+        out_specs=(taps, taps),
+        compiler_params=pltpu.CompilerParams(vmem_limit_bytes=16 << 20),
         name="sums",
-    )(sums)
+    )(*near(sums))
 
 
 def shards(

time: 102 us -> 93.3 us (0.915)
  Pallas kernels: 42.6 us -> 29.4 us
  waiting for transfers between devices: 21.1 us -> 22.7 us
  local copies, waits for them, and re-layouts: 4.2 us -> 5.49 us
  other arithmetic: 0.08 us -> 1.1 us
    pallas_call x5, Pallas kernels: 32.7 us -> 23.9 us  [the longest x1 17 us: brick_call(): pl.pallas_call(brick_kernel, out_shape=(shape((lx, ly, width), BF16), hel...]
    pallas_call x1, Pallas kernels: 4.08 us -> 1.4 us  [tile_call(): pl.pallas_call(tile_kernel, out_shape=(shape((3 * ACT_MAX,), jnp.int32),...]
    all_to_all x1, waiting for transfers between devices: 4.71 us -> 6.26 us  [shards(): got = lax.all_to_all(parts, ('gx', 'gy'), 0, 0, tiled=True)]
    unnamed x22 -> x26, local copies, waits for them, and re-layouts: 3.37 us -> 4.66 us
    pallas_call x1, Pallas kernels: 3.28 us -> 2.09 us  [join_call(): pl.pallas_call(join_kernel, out_shape=shape(grads.shape, BF16), in_specs=...]
    reduce_sum x1, other arithmetic: 0.08 us -> 1.1 us  [shards(): mine = jnp.sum(got.astype(F32), axis=0, keepdims=True).astype(BF16)]
  transfers between devices with their start and end apart: 10 -> 10, of which waited for: 5 -> 5; matrix products, arithmetic and copies ran while one was open for 0% -> 0% of each run, Pallas kernels for 17% -> 11%
where the time goes in v2:
time: 93.3 us; the launch traced here: 92.4 us
  starting transfers between devices  32.9 us (35%)
  Pallas kernels  29.4 us (32%)
  waiting for transfers between devices  22.7 us (24%)
  local copies, waits for them, and re-layouts  5.49 us (6%)
  other arithmetic  1.1 us (1%)
    ppermute x8, starting transfers between devices, shifted_in(): return lax.ppermute(array, axis, pairs)  24.4 us
    pallas_call x1, Pallas kernels, brick_call(): pl.pallas_call(brick_kernel, out_shape=(shape((lx, ly, width), BF16), hel...  17 us
    ppermute x8, waiting for transfers between devices, shifted_in(): return lax.ppermute(array, axis, pairs)  16.4 us
    pallas_call x1, Pallas kernels, input_call(): pl.pallas_call(input_kernel, out_shape=(shape((lx, ly, width), BF16), hel...  6.59 us
    all_to_all x1, waiting for transfers between devices, shards(): got = lax.all_to_all(parts, ('gx', 'gy'), 0, 0, tiled=True)  6.26 us
    unnamed x26, local copies, waits for them, and re-layouts  4.66 us
    all_to_all x1, starting transfers between devices, shards(): lax.all_to_all(jnp.broadcast_to(mine, parts.shape), ('gx', 'gy'), 0, 0, t...  4.39 us
    all_to_all x1, starting transfers between devices, shards(): got = lax.all_to_all(parts, ('gx', 'gy'), 0, 0, tiled=True)  4.11 us
  transfers between devices with their start and end apart: 10, of which 5 were waited for; matrix products, arithmetic and copies ran while one was open for 0% of the time, Pallas kernels for 11%

profile of v2, /device:TPU:17, one launch (start us, length us, event | category | flops | bytes accessed | tf_op | source)
XLA Modules:
  0.0 92.4 jit_solution(3844658436723871008)
XLA Ops:
  0.6 0.0 copy-start
  0.6 1.2 %copy-done = bf16[16,64,512]{2,1,0:T(8,128)(2,1)S(1)} copy-done((bf16[16,64,512]{2,1,0:T(8,128)(2,1)S(1)}, bf16[16,64,512]{2,1,0:T(8,128)(2,1)}, u32[]{:S(2)}) %copy-start) | copy-done | bytes 1048600
  1.9 0.0 copy-start.5
  1.9 0.7 copy-done.5
  2.6 0.7 copy-done.7
  3.3 0.0 copy-start.9
  3.3 0.0 copy-start.10
  3.3 0.0 copy-start.11
  3.3 0.0 copy-start.12
  3.3 0.3 strips.1
  3.6 3.3 %collective-permute-start = (bf16[2,64,512]{2,1,0:T(8,128)(2,1)S(1)}, bf16[2,64,512]{2,1,0:T(8,128)(2,1)S(1)}, u32[]{:S(2)}, u32[]{:S(2)}) collective-permute-start(bf16[2,64,512]{2,1,0:T(8,128)(2,1)S(1)} %get-tuple-element.36.bottom), channel_id=1, source_target_pairs={{0,4},{4,8},{8,12},{12,16},{16,20},{20,24},{24,28},{1,5},{5,9},{9,... | collective-permute-start | bytes 393224 | tf_op jit(solution)/shard_map/ppermute | solution.py:21
  6.8 3.1 %collective-permute-start.1 = (bf16[2,64,512]{2,1,0:T(8,128)(2,1)S(1)}, bf16[2,64,512]{2,1,0:T(8,128)(2,1)S(1)}, u32[]{:S(2)}, u32[]{:S(2)}) collective-permute-start(bf16[2,64,512]{2,1,0:T(8,128)(2,1)S(1)} %get-tuple-element.37.top), channel_id=1, source_target_pairs={{4,0},{8,4},{12,8},{16,12},{20,16},{24,20},{28,24},{5,1},{9,5},{13... | collective-permute-start | bytes 393224 | tf_op jit(solution)/shard_map/ppermute | solution.py:21
  9.9 0.0 copy-done.1
  9.9 0.0 copy-done.6
  9.9 0.0 copy-done.8
  9.9 0.0 copy-start.3
  9.9 1.0 %copy-done.3 = bf16[27,64,64]{2,1,0:T(8,128)(2,1)S(1)} copy-done((bf16[27,64,64]{2,1,0:T(8,128)(2,1)S(1)}, bf16[27,64,64]{2,1,0:T(8,128)(2,1)}, u32[]{:S(2)}) %copy-start.3) | copy-done | bytes 221208
  10.9 1.0 %copy-done.4 = bf16[27,64,64]{2,1,0:T(8,128)(2,1)S(1)} copy-done((bf16[27,64,64]{2,1,0:T(8,128)(2,1)S(1)}, bf16[27,64,64]{2,1,0:T(8,128)(2,1)}, u32[]{:S(2)}) %copy-start.4) | copy-done | bytes 221208
  12.0 1.4 %tiles.1 = (s32[12]{0:T(128)S(1)}, bf16[3,9,4,64,128]{4,3,2,1,0:T(8,128)(2,1)S(1)}, bf16[9,4,64,128]{3,2,1,0:T(8,128)(2,1)S(1)}, bf16[16,64,512]{2,1,0:T(8,128)(...) custom-call(bf16[16,64,512]{2,1,0:T(8,128)(2,1)S(1)} %copy-done.1, s32[16,64]{1,0:T(8,128)S(1)} %copy-done.6, ...), custom_call_target="tpu_custom_call" | custom-call | tf_op jit(solution)/shard_map/tiles/pallas_call | solution.py:197
  13.4 0.0 collective-permute-done.above
  13.4 0.6 collective-permute-done.1.below
  14.0 4.3 %collective-permute-start.2 = (bf16[20,2,512]{2,1,0:T(2,128)(2,1)S(1)}, bf16[20,2,512]{2,1,0:T(2,128)(2,1)S(1)}, u32[]{:S(2)}, u32[]{:S(2)}) collective-permute-start(bf16[20,2,512]{2,1,0:T(2,128)(2,1)S(1)} %get-tuple-element.40), channel_id=1, source_target_pairs={{0,1},{1,2},{2,3},{4,5},{5,6},{6,7},{8,9},{9,10},{10,11},{12,13},{... | collective-permute-start | bytes 122888 | tf_op jit(solution)/shard_map/ppermute | solution.py:21
  18.3 1.9 %collective-permute-start.3 = (bf16[20,2,512]{2,1,0:T(2,128)(2,1)S(1)}, bf16[20,2,512]{2,1,0:T(2,128)(2,1)S(1)}, u32[]{:S(2)}, u32[]{:S(2)}) collective-permute-start(bf16[20,2,512]{2,1,0:T(2,128)(2,1)S(1)} %get-tuple-element.41), channel_id=1, source_target_pairs={{1,0},{2,1},{3,2},{5,4},{6,5},{7,6},{9,8},{10,9},{11,10},{13,12},{... | collective-permute-start | bytes 122888 | tf_op jit(solution)/shard_map/ppermute | solution.py:21
  20.2 0.0 collective-permute-done.2.left
  20.2 3.4 %collective-permute-done.3.right = bf16[20,2,512]{2,1,0:T(2,128)(2,1)S(1)} collective-permute-done((bf16[20,2,512]{2,1,0:T(2,128)(2,1)S(1)}, bf16[20,2,512]{2,1,0:T(2,128)(2,1)S(1)}, u32[]{:S(2)}, u32[]{:S(2)}) %collective-permute-start.3) | collective-permute-done | bytes 40992 | tf_op jit(solution)/shard_map/ppermute | solution.py:21
  23.6 0.0 copy-done.2
  23.6 0.0 copy-done.9
  23.6 0.0 copy-done.10
  23.6 0.0 copy-done.11
  23.6 0.0 copy-done.12
  23.6 17.0 %bricks.1 = (bf16[16,64,512]{2,1,0:T(8,128)(2,1)}, bf16[640,512]{1,0:T(8,128)(2,1)S(1)}, f32[4,8,8,512]{3,2,1,0:T(8,128)S(1)}, bf16[28,64,128]{2,1,0:T(8,128)(2,1)}) custom-call(s32[12]{0:T(128)S(1)} %get-tuple-element.47.slots, bf16[16,64,512]{2,1,0:T(8,128)(2,1)S(1)} %get-tuple-element.35.packed, bf16[2,64,512]{2,1,0:T(8,128)(2,1)S(1)} %collective-permute-done.above, ...), custom_call_target="tpu_custom_call" | custom-call | tf_op jit(solution)/shard_map/bricks/pallas_call | solution.py:450
  40.7 4.1 %all-to-all-start = ((bf16[32,56,128]{2,1,0:T(8,128)(2,1)}), bf16[32,56,128]{2,1,0:T(8,128)(2,1)}, u32[]{:S(2)}, u32[]{:S(2)}) async-start(bf16[32,56,128]{2,1,0:T(8,128)(2,1)} %bitcast.4), calls=%async_computation | async-start | bytes 917504 | tf_op jit(solution)/shard_map/all_to_all | solution.py:735
  44.8 6.6 %inputs.1 = (bf16[16,64,512]{2,1,0:T(8,128)(2,1)}, bf16[2,72,512]{2,1,0:T(8,128)(2,1)S(1)}, bf16[2,72,512]{2,1,0:T(8,128)(2,1)S(1)}, bf16[16,2,512]{2,1,0:T(2,128)(2,1)S(1)}, bf16[16,2,512]{2,1,0:T(2,128)(2,1)S(1)}) custom-call(s32[12]{0:T(128)S(1)} %get-tuple-element.47.slots, bf16[640,512]{1,0:T(8,128)(2,1)S(1)} %get-tuple-element.48.errors, ...), custom_call_target="tpu_custom_call" | custom-call | tf_op jit(solution)/shard_map/inputs/pallas_call | solution.py:572
  51.4 6.3 %all-to-all-done = bf16[32,56,128]{2,1,0:T(8,128)(2,1)} async-done(((bf16[32,56,128]{2,1,0:T(8,128)(2,1)}), bf16[32,56,128]{2,1,0:T(8,128)(2,1)}, u32[]{:S(2)}, u32[]{:S(2)}) %all-to-all-start) | async-done | bytes 458784 | tf_op jit(solution)/shard_map/all_to_all | solution.py:735
  57.6 1.1 %reduce_sum.12 = bf16[56,128]{1,0:T(8,128)(2,1)S(1)} reduce(bf16[32,56,128]{2,1,0:T(8,128)(2,1)} %all-to-all-done, bf16[]{:T(256)} %constant.2.clone.1), dimensions={0}, to_apply=%region_0.0 | reduce | flops 222208 | bytes 473090 | tf_op jit(solution)/shard_map/reduce_sum | solution.py:742
  58.7 0.8 broadcast_in_dim.2
  59.6 4.4 %all-to-all-start.1 = ((bf16[32,56,128]{2,1,0:T(8,128)(2,1)}), bf16[32,56,128]{2,1,0:T(8,128)(2,1)S(1)}, u32[]{:S(2)}, u32[]{:S(2)}) async-start(bf16[32,56,128]{2,1,0:T(8,128)(2,1)} %broadcast_in_dim.2), calls=%async_computation.1 | async-start | bytes 917504 | tf_op jit(solution)/shard_map/all_to_all | solution.py:743
  64.0 3.1 %collective-permute-start.4 = (bf16[2,72,512]{2,1,0:T(8,128)(2,1)S(1)}, bf16[2,72,512]{2,1,0:T(8,128)(2,1)S(1)}, u32[]{:S(2)}, u32[]{:S(2)}) collective-permute-start(bf16[2,72,512]{2,1,0:T(8,128)(2,1)S(1)} %get-tuple-element.56), channel_id=1, source_target_pairs={{0,4},{4,8},{8,12},{12,16},{16,20},{20,24},{24,28},{1,5},{5,9},{9,... | collective-permute-start | bytes 442376 | tf_op jit(solution)/shard_map/ppermute | solution.py:21
  67.1 3.1 %collective-permute-start.5 = (bf16[2,72,512]{2,1,0:T(8,128)(2,1)S(1)}, bf16[2,72,512]{2,1,0:T(8,128)(2,1)S(1)}, u32[]{:S(2)}, u32[]{:S(2)}) collective-permute-start(bf16[2,72,512]{2,1,0:T(8,128)(2,1)S(1)} %get-tuple-element.57), channel_id=1, source_target_pairs={{4,0},{8,4},{12,8},{16,12},{20,16},{24,20},{28,24},{5,1},{9,5},{13... | collective-permute-start | bytes 442376 | tf_op jit(solution)/shard_map/ppermute | solution.py:21
  70.2 9.1 %collective-permute-done.4.from_above = bf16[2,72,512]{2,1,0:T(8,128)(2,1)S(1)} collective-permute-done((bf16[2,72,512]{2,1,0:T(8,128)(2,1)S(1)}, bf16[2,72,512]{2,1,0:T(8,128)(2,1)S(1)}, u32[]{:S(2)}, u32[]{:S(2)}) %collective-permute-start.4) | collective-permute-done | bytes 147488 | tf_op jit(solution)/shard_map/ppermute | solution.py:21
  79.3 0.0 collective-permute-done.5.from_below
  79.3 3.7 %collective-permute-start.6 = (bf16[16,2,512]{2,1,0:T(2,128)(2,1)S(1)}, bf16[16,2,512]{2,1,0:T(2,128)(2,1)S(1)}, u32[]{:S(2)}, u32[]{:S(2)}) collective-permute-start(bf16[16,2,512]{2,1,0:T(2,128)(2,1)S(1)} %get-tuple-element.58), channel_id=1, source_target_pairs={{0,1},{1,2},{2,3},{4,5},{5,6},{6,7},{8,9},{9,10},{10,11},{12,13},{... | collective-permute-start | bytes 98312 | tf_op jit(solution)/shard_map/ppermute | solution.py:21
  83.1 1.9 %collective-permute-start.7 = (bf16[16,2,512]{2,1,0:T(2,128)(2,1)S(1)}, bf16[16,2,512]{2,1,0:T(2,128)(2,1)S(1)}, u32[]{:S(2)}, u32[]{:S(2)}) collective-permute-start(bf16[16,2,512]{2,1,0:T(2,128)(2,1)S(1)} %get-tuple-element.59), channel_id=1, source_target_pairs={{1,0},{2,1},{3,2},{5,4},{6,5},{7,6},{9,8},{10,9},{11,10},{13,12},{... | collective-permute-start | bytes 98312 | tf_op jit(solution)/shard_map/ppermute | solution.py:21
  85.0 0.0 collective-permute-done.6.from_left
  85.0 3.3 %collective-permute-done.7.from_right = bf16[16,2,512]{2,1,0:T(2,128)(2,1)S(1)} collective-permute-done((bf16[16,2,512]{2,1,0:T(2,128)(2,1)S(1)}, bf16[16,2,512]{2,1,0:T(2,128)(2,1)S(1)}, u32[]{:S(2)}, u32[]{:S(2)}) %collective-permute-start.7) | collective-permute-done | bytes 32800 | tf_op jit(solution)/shard_map/ppermute | solution.py:21
  88.3 2.1 %join.1 = bf16[16,64,512]{2,1,0:T(8,128)(2,1)} custom-call(bf16[16,64,512]{2,1,0:T(8,128)(2,1)} %get-tuple-element.53.grads, bf16[2,64,512]{2,1,0:T(8,128)(2,1)S(1)} %get-tuple-element.37.top, bf16[2,64,512]{2,1,0:T(8,128)(2,1)S(1)} %get-tuple-element.36.bottom, bf16[16,2,512]{2,1,0:T(2,128)(2,1)S(1)} %get-tuple-element.38.first, ...), custom_call_target="tpu_custom_call", output_to_operand_aliasing={{}: (0, {})} | custom-call | tf_op jit(solution)/shard_map/join/pallas_call | solution.py:673
  90.4 0.0 all-to-all-done.1
  90.4 2.0 %sums.1 = (f32[27,64,64]{2,1,0:T(8,128)}, f32[27,64,64]{2,1,0:T(8,128)}) custom-call(bf16[1792,128]{1,0:T(8,128)(2,1)S(1)} %bitcast.6), custom_call_target="tpu_custom_call" | custom-call | tf_op jit(solution)/shard_map/sums/pallas_call | solution.py:702
  (8 shorter events, 0.1 us)
Async XLA Ops:
  0.6 1.2 %copy-start = (bf16[16,64,512]{2,1,0:T(8,128)(2,1)S(1)}, bf16[16,64,512]{2,1,0:T(8,128)(2,1)}, u32[]{:S(2)}) copy-start(bf16[16,64,512]{2,1,0:T(8,128)(2,1)} %bottom_in.1) | copy-start | bytes 3145732
  1.9 0.7 copy-start.5
  2.6 0.7 copy-start.7
  3.3 6.6 %copy-start.1 = (bf16[16,64,512]{2,1,0:T(8,128)(2,1)S(1)}, bf16[16,64,512]{2,1,0:T(8,128)(2,1)}, u32[]{:S(2)}) copy-start(bf16[16,64,512]{2,1,0:T(8,128)(2,1)} %bottom_in.1) | copy-start | bytes 3145732
  3.3 6.7 %copy-start.6 = (s32[16,64]{1,0:T(8,128)S(1)}, s32[16,64]{1,0:T(8,128)}, u32[]{:S(2)}) copy-start(s32[16,64]{1,0:T(8,128)} %low.3) | copy-start | bytes 12292
  3.3 6.7 %copy-start.8 = (s32[16,64]{1,0:T(8,128)S(1)}, s32[16,64]{1,0:T(8,128)}, u32[]{:S(2)}) copy-start(s32[16,64]{1,0:T(8,128)} %high.3) | copy-start | bytes 12292
  3.3 20.3 %copy-start.2 = (bf16[16,64,512]{2,1,0:T(8,128)(2,1)S(1)}, bf16[16,64,512]{2,1,0:T(8,128)(2,1)}, u32[]{:S(2)}) copy-start(bf16[16,64,512]{2,1,0:T(8,128)(2,1)} %cotangent.1) | copy-start | bytes 3145732
  3.3 20.3 %copy-start.9 = (f32[64]{0:T(128)S(1)}, f32[64]{0:T(128)}, u32[]{:S(2)}) copy-start(f32[64]{0:T(128)} %param.16) | copy-start | bytes 772
  3.3 20.3 %copy-start.10 = (f32[64]{0:T(128)S(1)}, f32[64]{0:T(128)}, u32[]{:S(2)}) copy-start(f32[64]{0:T(128)} %param.17) | copy-start | bytes 772
  3.3 20.3 %copy-start.11 = (f32[64]{0:T(128)S(1)}, f32[64]{0:T(128)}, u32[]{:S(2)}) copy-start(f32[64]{0:T(128)} %param.18) | copy-start | bytes 772
  3.3 20.3 %copy-start.12 = (f32[64]{0:T(128)S(1)}, f32[64]{0:T(128)}, u32[]{:S(2)}) copy-start(f32[64]{0:T(128)} %param.19) | copy-start | bytes 772
  3.6 9.8 %collective-permute-start = (bf16[2,64,512]{2,1,0:T(8,128)(2,1)S(1)}, bf16[2,64,512]{2,1,0:T(8,128)(2,1)S(1)}, u32[]{:S(2)}, u32[]{:S(2)}) collective-permute-start(bf16[2,64,512]{2,1,0:T(8,128)(2,1)S(1)} %get-tuple-element.36.bottom), channel_id=1, source_target_pairs={{0,4},{4,8},{8,12},{12,16},{16,20},{20,24},{24,28},{1,5},{5,9},{9,... | collective-permute-start | bytes 393224 | tf_op jit(solution)/shard_map/ppermute | solution.py:21
  6.8 7.2 %collective-permute-start.1 = (bf16[2,64,512]{2,1,0:T(8,128)(2,1)S(1)}, bf16[2,64,512]{2,1,0:T(8,128)(2,1)S(1)}, u32[]{:S(2)}, u32[]{:S(2)}) collective-permute-start(bf16[2,64,512]{2,1,0:T(8,128)(2,1)S(1)} %get-tuple-element.37.top), channel_id=1, source_target_pairs={{4,0},{8,4},{12,8},{16,12},{20,16},{24,20},{28,24},{5,1},{9,5},{13... | collective-permute-start | bytes 393224 | tf_op jit(solution)/shard_map/ppermute | solution.py:21
  9.9 1.0 %copy-start.3 = (bf16[27,64,64]{2,1,0:T(8,128)(2,1)S(1)}, bf16[27,64,64]{2,1,0:T(8,128)(2,1)}, u32[]{:S(2)}) copy-start(bf16[27,64,64]{2,1,0:T(8,128)(2,1)} %weight_one.1) | copy-start | bytes 663556
  10.9 1.0 %copy-start.4 = (bf16[27,64,64]{2,1,0:T(8,128)(2,1)S(1)}, bf16[27,64,64]{2,1,0:T(8,128)(2,1)}, u32[]{:S(2)}) copy-start(bf16[27,64,64]{2,1,0:T(8,128)(2,1)} %weight_two.1) | copy-start | bytes 663556
  14.0 6.2 %collective-permute-start.2 = (bf16[20,2,512]{2,1,0:T(2,128)(2,1)S(1)}, bf16[20,2,512]{2,1,0:T(2,128)(2,1)S(1)}, u32[]{:S(2)}, u32[]{:S(2)}) collective-permute-start(bf16[20,2,512]{2,1,0:T(2,128)(2,1)S(1)} %get-tuple-element.40), channel_id=1, source_target_pairs={{0,1},{1,2},{2,3},{4,5},{5,6},{6,7},{8,9},{9,10},{10,11},{12,13},{... | collective-permute-start | bytes 122888 | tf_op jit(solution)/shard_map/ppermute | solution.py:21
  18.3 5.3 %collective-permute-start.3 = (bf16[20,2,512]{2,1,0:T(2,128)(2,1)S(1)}, bf16[20,2,512]{2,1,0:T(2,128)(2,1)S(1)}, u32[]{:S(2)}, u32[]{:S(2)}) collective-permute-start(bf16[20,2,512]{2,1,0:T(2,128)(2,1)S(1)} %get-tuple-element.41), channel_id=1, source_target_pairs={{1,0},{2,1},{3,2},{5,4},{6,5},{7,6},{9,8},{10,9},{11,10},{13,12},{... | collective-permute-start | bytes 122888 | tf_op jit(solution)/shard_map/ppermute | solution.py:21
  40.7 17.0 %all-to-all-start = ((bf16[32,56,128]{2,1,0:T(8,128)(2,1)}), bf16[32,56,128]{2,1,0:T(8,128)(2,1)}, u32[]{:S(2)}, u32[]{:S(2)}) async-start(bf16[32,56,128]{2,1,0:T(8,128)(2,1)} %bitcast.4), calls=%async_computation | async-start | bytes 917504 | tf_op jit(solution)/shard_map/all_to_all | solution.py:735
  59.6 30.9 %all-to-all-start.1 = ((bf16[32,56,128]{2,1,0:T(8,128)(2,1)}), bf16[32,56,128]{2,1,0:T(8,128)(2,1)S(1)}, u32[]{:S(2)}, u32[]{:S(2)}) async-start(bf16[32,56,128]{2,1,0:T(8,128)(2,1)} %broadcast_in_dim.2), calls=%async_computation.1 | async-start | bytes 917504 | tf_op jit(solution)/shard_map/all_to_all | solution.py:743
  64.0 15.3 %collective-permute-start.4 = (bf16[2,72,512]{2,1,0:T(8,128)(2,1)S(1)}, bf16[2,72,512]{2,1,0:T(8,128)(2,1)S(1)}, u32[]{:S(2)}, u32[]{:S(2)}) collective-permute-start(bf16[2,72,512]{2,1,0:T(8,128)(2,1)S(1)} %get-tuple-element.56), channel_id=1, source_target_pairs={{0,4},{4,8},{8,12},{12,16},{16,20},{20,24},{24,28},{1,5},{5,9},{9,... | collective-permute-start | bytes 442376 | tf_op jit(solution)/shard_map/ppermute | solution.py:21
  67.1 12.2 %collective-permute-start.5 = (bf16[2,72,512]{2,1,0:T(8,128)(2,1)S(1)}, bf16[2,72,512]{2,1,0:T(8,128)(2,1)S(1)}, u32[]{:S(2)}, u32[]{:S(2)}) collective-permute-start(bf16[2,72,512]{2,1,0:T(8,128)(2,1)S(1)} %get-tuple-element.57), channel_id=1, source_target_pairs={{4,0},{8,4},{12,8},{16,12},{20,16},{24,20},{28,24},{5,1},{9,5},{13... | collective-permute-start | bytes 442376 | tf_op jit(solution)/shard_map/ppermute | solution.py:21
  79.3 5.7 %collective-permute-start.6 = (bf16[16,2,512]{2,1,0:T(2,128)(2,1)S(1)}, bf16[16,2,512]{2,1,0:T(2,128)(2,1)S(1)}, u32[]{:S(2)}, u32[]{:S(2)}) collective-permute-start(bf16[16,2,512]{2,1,0:T(2,128)(2,1)S(1)} %get-tuple-element.58), channel_id=1, source_target_pairs={{0,1},{1,2},{2,3},{4,5},{5,6},{6,7},{8,9},{9,10},{10,11},{12,13},{... | collective-permute-start | bytes 98312 | tf_op jit(solution)/shard_map/ppermute | solution.py:21
  83.1 5.2 %collective-permute-start.7 = (bf16[16,2,512]{2,1,0:T(2,128)(2,1)S(1)}, bf16[16,2,512]{2,1,0:T(2,128)(2,1)S(1)}, u32[]{:S(2)}, u32[]{:S(2)}) collective-permute-start(bf16[16,2,512]{2,1,0:T(2,128)(2,1)S(1)} %get-tuple-element.59), channel_id=1, source_target_pairs={{1,0},{2,1},{3,2},{5,4},{6,5},{7,6},{9,8},{10,9},{11,10},{13,12},{... | collective-permute-start | bytes 98312 | tf_op jit(solution)/shard_map/ppermute | solution.py:21

commit v3 on v2

--- a/solution.py
+++ b/solution.py
@@ -52,6 +52,10 @@
 
 def near(*arrays):
     return [pltpu.with_memory_space_constraint(a, pltpu.VMEM) for a in arrays]
+
+
+def far(*arrays):
+    return [pltpu.with_memory_space_constraint(a, pltpu.HBM) for a in arrays]
 
 
 EMPTY_FEATURE = 256.0
@@ -100,9 +104,9 @@
             VMEM,
         ],
         out_specs=(VMEM, VMEM),
-        compiler_params=pltpu.CompilerParams(vmem_limit_bytes=12 << 20),
+        compiler_params=pltpu.CompilerParams(vmem_limit_bytes=4 << 20),
         name="strips",
-    )(features, features, low, high)
+    )(*far(features, features, low, high))
 
 
 def side_kernel(above, below, first, last, to_left, to_right):
@@ -124,7 +128,7 @@
         out_shape=(held(tall, BF16), held(tall, BF16)),
         in_specs=[VMEM] * 4,
         out_specs=(VMEM, VMEM),
-        compiler_params=pltpu.CompilerParams(vmem_limit_bytes=12 << 20),
+        compiler_params=pltpu.CompilerParams(vmem_limit_bytes=4 << 20),
         name="sides",
     )(*near(above, below, first, last))
 
@@ -206,7 +210,7 @@
         ),
         in_specs=[VMEM] * 5,
         out_specs=(SMEM,) + (VMEM,) * 5,
-        compiler_params=pltpu.CompilerParams(vmem_limit_bytes=16 << 20),
+        compiler_params=pltpu.CompilerParams(vmem_limit_bytes=8 << 20),
         name="tiles",
     )(features, low, high, weight_one, weight_two)
 
@@ -411,18 +415,22 @@
 
     def weight_sums(source, errors_t, xs, which):
         rows = source.shape[0] * xs * 16
-        sums = None
-        for p in range(5):
-            parts = [
-                source[:, ox : ox + xs, :, 384 * p : 384 * p + 384].reshape(rows, 384)
-                for ox in range(3)
-            ]
-            part = jnp.dot(
-                errors_t[128 * p : 128 * p + 256, :],
-                jnp.concatenate(parts, axis=1),
-                preferred_element_type=F32,
+        left_side = jnp.concatenate(
+            [errors_t[128 * p : 128 * p + 256, :] for p in range(5)], axis=1
+        )
+        right_side = [
+            jnp.concatenate(
+                [
+                    source[:, ox : ox + xs, :, 384 * p : 384 * p + 384].reshape(rows, 384)
+                    for ox in range(3)
+                ],
+                axis=1,
             )
-            sums = part if sums is None else sums + part
+            for p in range(5)
+        ]
+        sums = jnp.dot(
+            left_side, jnp.concatenate(right_side, axis=0), preferred_element_type=F32
+        )
         for tap in range(9):
             block = sums[:, 128 * tap : 128 * tap + 128]
             turned = turn(block)
@@ -453,7 +461,7 @@
             shape((lx, ly, width), BF16),
             held((n * 160, width), BF16),
             held((n, 8, 8, width), F32),
-            held((28, 64, 128), BF16),
+            pltpu.HBM((28, 64, 128), BF16),
         ),
         in_specs=[SMEM] + [VMEM] * 11,
         out_specs=(VMEM,) * 4,
@@ -475,13 +483,11 @@
             pltpu.VMEM((768, n * 160), BF16),
             pltpu.VMEM((27, 64, 128), F32),
         ],
-        compiler_params=pltpu.CompilerParams(vmem_limit_bytes=40 << 20),
+        compiler_params=pltpu.CompilerParams(vmem_limit_bytes=33 << 20),
         name="bricks",
     )(
         slots,
-        *near(packed, above, below, left, right),
-        cotangent,
-        *near(tiles),
+        *near(packed, above, below, left, right, cotangent, tiles),
         *vectors,
     )
 
@@ -587,7 +593,7 @@
             pltpu.VMEM((n * 192, width), F32),
             pltpu.VMEM((4, lx + 4, ly + 16, 128), F32),
         ],
-        compiler_params=pltpu.CompilerParams(vmem_limit_bytes=24 << 20),
+        compiler_params=pltpu.CompilerParams(vmem_limit_bytes=15 << 20),
         name="inputs",
     )(slots, *near(errors, grads, packed, tiles))
 
@@ -610,7 +616,7 @@
         out_shape=(held(left.shape, BF16), held(left.shape, BF16)),
         in_specs=[VMEM] * 4,
         out_specs=(VMEM, VMEM),
-        compiler_params=pltpu.CompilerParams(vmem_limit_bytes=12 << 20),
+        compiler_params=pltpu.CompilerParams(vmem_limit_bytes=4 << 20),
         name="ends",
     )(*near(left, right, from_above, from_below))
 
@@ -683,9 +689,26 @@
             pltpu.SemaphoreType.DMA((4,)),
         ],
         input_output_aliases={0: 0},
-        compiler_params=pltpu.CompilerParams(vmem_limit_bytes=16 << 20),
+        compiler_params=pltpu.CompilerParams(vmem_limit_bytes=8 << 20),
         name="join",
     )(grads, *near(*strips))
+
+
+def part_kernel(got, whole):
+    mine = jnp.sum(got[...].astype(F32), axis=0).astype(BF16)
+    for n in range(whole.shape[0]):
+        whole[n] = mine
+
+
+def part_call(got):
+    return pl.pallas_call(
+        part_kernel,
+        out_shape=held(got.shape, BF16),
+        in_specs=[VMEM],
+        out_specs=VMEM,
+        compiler_params=pltpu.CompilerParams(vmem_limit_bytes=4 << 20),
+        name="part",
+    )(*near(got))
 
 
 def sums_kernel(sums, grad_one, grad_two, *, scale):
@@ -705,7 +728,7 @@
         grid=(3,),
         in_specs=[VMEM],
         out_specs=(taps, taps),
-        compiler_params=pltpu.CompilerParams(vmem_limit_bytes=16 << 20),
+        compiler_params=pltpu.CompilerParams(vmem_limit_bytes=8 << 20),
         name="sums",
     )(*near(sums))
 
@@ -739,10 +762,8 @@
     from_below = shifted_in(grad_above, "gx", -1)
     from_above = shifted_in(grad_below, "gx", 1)
     got, own = lax.optimization_barrier((got, own))
-    mine = jnp.sum(got.astype(F32), axis=0, keepdims=True).astype(BF16)
-    back = lax.all_to_all(
-        jnp.broadcast_to(mine, parts.shape), ("gx", "gy"), 0, 0, tiled=True
-    )
+    mine = part_call(got)
+    back = lax.all_to_all(mine, ("gx", "gy"), 0, 0, tiled=True)
     to_left, to_right = ends_call(grad_left, grad_right, from_above, from_below)
     from_right = shifted_in(to_left, "gy", -1)
     from_left = shifted_in(to_right, "gy", 1)

time: 93.3 us -> 90 us (0.965)
  local copies, waits for them, and re-layouts: 5.49 us -> 1.37 us
  Pallas kernels: 29.4 us -> 31 us
  other arithmetic: 1.1 us -> 0 us
    unnamed x26 -> x32, local copies, waits for them, and re-layouts: 4.66 us -> 1.37 us
    ppermute x8, waiting for transfers between devices: 16.4 us -> 18.4 us  [shifted_in(): return lax.ppermute(array, axis, pairs)]
    all_to_all x1, waiting for transfers between devices: 6.26 us -> 4.88 us  [shards(): got = lax.all_to_all(parts, ('gx', 'gy'), 0, 0, tiled=True)]
    pallas_call x1, Pallas kernels: 0.25 us -> 1.38 us  [strip_call(): pl.pallas_call(strip_kernel, out_shape=(held((2, ly, width), BF16), held(...]
    reduce_sum x1 -> x0, other arithmetic: 1.1 us -> none  [shards(): mine = jnp.sum(got.astype(F32), axis=0, keepdims=True).astype(BF16)]
where the time goes in v3:
time: 90 us; the launch traced here: 89.3 us
  starting transfers between devices  32.7 us (36%)
  Pallas kernels  31 us (34%)
  waiting for transfers between devices  23.3 us (26%)
  local copies, waits for them, and re-layouts  1.37 us (2%)
  between operations  0.96 us (1%)
    ppermute x8, starting transfers between devices, shifted_in(): return lax.ppermute(array, axis, pairs)  24.2 us
    ppermute x8, waiting for transfers between devices, shifted_in(): return lax.ppermute(array, axis, pairs)  18.4 us
    pallas_call x1, Pallas kernels, brick_call(): pl.pallas_call(brick_kernel, out_shape=(shape((lx, ly, width), BF16), hel...  16.7 us
    pallas_call x1, Pallas kernels, input_call(): pl.pallas_call(input_kernel, out_shape=(shape((lx, ly, width), BF16), hel...  6.59 us
    all_to_all x1, waiting for transfers between devices, shards(): got = lax.all_to_all(parts, ('gx', 'gy'), 0, 0, tiled=True)  4.88 us
    all_to_all x1, starting transfers between devices, shards(): back = lax.all_to_all(mine, ('gx', 'gy'), 0, 0, tiled=True)  4.39 us
    all_to_all x1, starting transfers between devices, shards(): got = lax.all_to_all(parts, ('gx', 'gy'), 0, 0, tiled=True)  4.07 us
    pallas_call x1, Pallas kernels, join_call(): pl.pallas_call(join_kernel, out_shape=shape(grads.shape, BF16), in_specs=...  2.09 us
  transfers between devices with their start and end apart: 10, of which 5 were waited for; matrix products, arithmetic and copies ran while one was open for 0% of the time, Pallas kernels for 11%

profile of v3, /device:TPU:17, one launch (start us, length us, event | category | flops | bytes accessed | tf_op | source)
XLA Modules:
  0.0 89.3 jit_solution(10806566675961079287)
XLA Ops:
  0.6 0.0 copy-start.7
  0.6 0.0 copy-start.6
  0.7 0.0 copy-start
  0.7 0.0 copy-start.3
  0.7 0.0 copy-start.2
  0.7 0.0 copy-start.11
  0.7 0.0 copy-start.10
  0.7 0.0 copy-start.9
  0.7 0.0 copy-start.8
  0.7 0.0 copy-start.1
  0.7 1.4 %strips.1 = (bf16[2,64,512]{2,1,0:T(8,128)(2,1)S(1)}, bf16[2,64,512]{2,1,0:T(8,128)(2,1)S(1)}) custom-call(bf16[16,64,512]{2,1,0:T(8,128)(2,1)} %bottom_in.1, bf16[16,64,512]{2,1,0:T(8,128)(2,1)} %bottom_in.1, s32[16,64]{1,0:T(8,128)} %low.3, s32[16,64]{1,0:T(8,128)} %high.3), custom_call_target="tpu_custom_call" | custom-call | tf_op jit(solution)/shard_map/strips/pallas_call | solution.py:96
  2.1 0.0 copy-start.4
  2.1 3.1 %collective-permute-start = (bf16[2,64,512]{2,1,0:T(8,128)(2,1)S(1)}, bf16[2,64,512]{2,1,0:T(8,128)(2,1)S(1)}, u32[]{:S(2)}, u32[]{:S(2)}) collective-permute-start(bf16[2,64,512]{2,1,0:T(8,128)(2,1)S(1)} %get-tuple-element.36.bottom), channel_id=1, source_target_pairs={{0,4},{4,8},{8,12},{12,16},{16,20},{20,24},{24,28},{1,5},{5,9},{9,... | collective-permute-start | bytes 393224 | tf_op jit(solution)/shard_map/ppermute | solution.py:21
  5.3 3.1 %collective-permute-start.1 = (bf16[2,64,512]{2,1,0:T(8,128)(2,1)S(1)}, bf16[2,64,512]{2,1,0:T(8,128)(2,1)S(1)}, u32[]{:S(2)}, u32[]{:S(2)}) collective-permute-start(bf16[2,64,512]{2,1,0:T(8,128)(2,1)S(1)} %get-tuple-element.37.top), channel_id=1, source_target_pairs={{4,0},{8,4},{12,8},{16,12},{20,16},{24,20},{28,24},{5,1},{9,5},{13... | collective-permute-start | bytes 393224 | tf_op jit(solution)/shard_map/ppermute | solution.py:21
  8.3 0.0 copy-done.7
  8.3 0.0 copy-done.6
  8.3 0.0 copy-done
  8.4 0.0 copy-done.3
  8.4 0.0 copy-done.2
  8.4 1.4 %tiles.1 = (s32[12]{0:T(128)S(1)}, bf16[3,9,4,64,128]{4,3,2,1,0:T(8,128)(2,1)S(1)}, bf16[9,4,64,128]{3,2,1,0:T(8,128)(2,1)S(1)}, bf16[16,64,512]{2,1,0:T(8,128)(...) custom-call(bf16[16,64,512]{2,1,0:T(8,128)(2,1)S(1)} %copy-done, s32[16,64]{1,0:T(8,128)S(1)} %copy-done.6, ...), custom_call_target="tpu_custom_call" | custom-call | tf_op jit(solution)/shard_map/tiles/pallas_call | solution.py:201
  9.8 0.0 collective-permute-done.above
  9.8 2.6 %collective-permute-done.1.below = bf16[2,64,512]{2,1,0:T(8,128)(2,1)S(1)} collective-permute-done((bf16[2,64,512]{2,1,0:T(8,128)(2,1)S(1)}, bf16[2,64,512]{2,1,0:T(8,128)(2,1)S(1)}, u32[]{:S(2)}, u32[]{:S(2)}) %collective-permute-start.1) | collective-permute-done | bytes 131104 | tf_op jit(solution)/shard_map/ppermute | solution.py:21
  12.4 4.3 %collective-permute-start.2 = (bf16[20,2,512]{2,1,0:T(2,128)(2,1)S(1)}, bf16[20,2,512]{2,1,0:T(2,128)(2,1)S(1)}, u32[]{:S(2)}, u32[]{:S(2)}) collective-permute-start(bf16[20,2,512]{2,1,0:T(2,128)(2,1)S(1)} %get-tuple-element.40), channel_id=1, source_target_pairs={{0,1},{1,2},{2,3},{4,5},{5,6},{6,7},{8,9},{9,10},{10,11},{12,13},{... | collective-permute-start | bytes 122888 | tf_op jit(solution)/shard_map/ppermute | solution.py:21
  16.7 1.9 %collective-permute-start.3 = (bf16[20,2,512]{2,1,0:T(2,128)(2,1)S(1)}, bf16[20,2,512]{2,1,0:T(2,128)(2,1)S(1)}, u32[]{:S(2)}, u32[]{:S(2)}) collective-permute-start(bf16[20,2,512]{2,1,0:T(2,128)(2,1)S(1)} %get-tuple-element.41), channel_id=1, source_target_pairs={{1,0},{2,1},{3,2},{5,4},{6,5},{7,6},{9,8},{10,9},{11,10},{13,12},{... | collective-permute-start | bytes 122888 | tf_op jit(solution)/shard_map/ppermute | solution.py:21
  18.6 0.0 collective-permute-done.2.left
  18.6 3.4 %collective-permute-done.3.right = bf16[20,2,512]{2,1,0:T(2,128)(2,1)S(1)} collective-permute-done((bf16[20,2,512]{2,1,0:T(2,128)(2,1)S(1)}, bf16[20,2,512]{2,1,0:T(2,128)(2,1)S(1)}, u32[]{:S(2)}, u32[]{:S(2)}) %collective-permute-start.3) | collective-permute-done | bytes 40992 | tf_op jit(solution)/shard_map/ppermute | solution.py:21
  22.0 0.0 copy-done.4
  22.0 0.0 copy-done.11
  22.0 0.0 copy-done.10
  22.1 16.7 %bricks.1 = (bf16[16,64,512]{2,1,0:T(8,128)(2,1)}, bf16[640,512]{1,0:T(8,128)(2,1)S(1)}, f32[4,8,8,512]{3,2,1,0:T(8,128)S(1)}, bf16[28,64,128]{2,1,0:T(8,128)(2,1)}) custom-call(s32[12]{0:T(128)S(1)} %get-tuple-element.47.slots, bf16[16,64,512]{2,1,0:T(8,128)(2,1)S(1)} %get-tuple-element.35.packed, bf16[2,64,512]{2,1,0:T(8,128)(2,1)S(1)} %collective-permute-done.above, ...), custom_call_target="tpu_custom_call" | custom-call | tf_op jit(solution)/shard_map/bricks/pallas_call | solution.py:458
  38.8 4.1 %all-to-all-start = ((bf16[32,56,128]{2,1,0:T(8,128)(2,1)}), bf16[32,56,128]{2,1,0:T(8,128)(2,1)S(1)}, u32[]{:S(2)}, u32[]{:S(2)}) async-start(bf16[32,56,128]{2,1,0:T(8,128)(2,1)} %bitcast.11), calls=%async_computation | async-start | bytes 917504 | tf_op jit(solution)/shard_map/all_to_all | solution.py:758
  42.8 6.6 %inputs.1 = (bf16[16,64,512]{2,1,0:T(8,128)(2,1)}, bf16[2,72,512]{2,1,0:T(8,128)(2,1)S(1)}, bf16[2,72,512]{2,1,0:T(8,128)(2,1)S(1)}, bf16[16,2,512]{2,1,0:T(2,128)(2,1)S(1)}, bf16[16,2,512]{2,1,0:T(2,128)(2,1)S(1)}) custom-call(s32[12]{0:T(128)S(1)} %get-tuple-element.47.slots, bf16[640,512]{1,0:T(8,128)(2,1)S(1)} %get-tuple-element.48.errors, ...), custom_call_target="tpu_custom_call" | custom-call | tf_op jit(solution)/shard_map/inputs/pallas_call | solution.py:578
  49.4 0.6 copy-done.12
  50.1 0.7 copy-done.14
  50.7 4.9 %all-to-all-done.got = bf16[32,56,128]{2,1,0:T(8,128)(2,1)S(1)} async-done(((bf16[32,56,128]{2,1,0:T(8,128)(2,1)}), bf16[32,56,128]{2,1,0:T(8,128)(2,1)S(1)}, u32[]{:S(2)}, u32[]{:S(2)}) %all-to-all-start) | async-done | bytes 458784 | tf_op jit(solution)/shard_map/all_to_all | solution.py:758
  55.6 0.9 part.1
  56.5 4.4 %all-to-all-start.1 = ((bf16[32,56,128]{2,1,0:T(8,128)(2,1)}), bf16[32,56,128]{2,1,0:T(8,128)(2,1)S(1)}, u32[]{:S(2)}, u32[]{:S(2)}) async-start(bf16[32,56,128]{2,1,0:T(8,128)(2,1)} %part.1), calls=%async_computation.1 | async-start | bytes 917504 | tf_op jit(solution)/shard_map/all_to_all | solution.py:766
  60.9 3.1 %collective-permute-start.4 = (bf16[2,72,512]{2,1,0:T(8,128)(2,1)S(1)}, bf16[2,72,512]{2,1,0:T(8,128)(2,1)S(1)}, u32[]{:S(2)}, u32[]{:S(2)}) collective-permute-start(bf16[2,72,512]{2,1,0:T(8,128)(2,1)S(1)} %copy-done.15), channel_id=1, source_target_pairs={{0,4},{4,8},{8,12},{12,16},{16,20},{20,24},{24,28},{1,5},{5,9},{9,... | collective-permute-start | bytes 442376 | tf_op jit(solution)/shard_map/ppermute | solution.py:21
  64.0 3.1 %collective-permute-start.5 = (bf16[2,72,512]{2,1,0:T(8,128)(2,1)S(1)}, bf16[2,72,512]{2,1,0:T(8,128)(2,1)S(1)}, u32[]{:S(2)}, u32[]{:S(2)}) collective-permute-start(bf16[2,72,512]{2,1,0:T(8,128)(2,1)S(1)} %copy-done.13), channel_id=1, source_target_pairs={{4,0},{8,4},{12,8},{16,12},{20,16},{24,20},{28,24},{5,1},{9,5},{13... | collective-permute-start | bytes 442376 | tf_op jit(solution)/shard_map/ppermute | solution.py:21
  67.1 9.1 %collective-permute-done.4.from_above = bf16[2,72,512]{2,1,0:T(8,128)(2,1)S(1)} collective-permute-done((bf16[2,72,512]{2,1,0:T(8,128)(2,1)S(1)}, bf16[2,72,512]{2,1,0:T(8,128)(2,1)S(1)}, u32[]{:S(2)}, u32[]{:S(2)}) %collective-permute-start.4) | collective-permute-done | bytes 147488 | tf_op jit(solution)/shard_map/ppermute | solution.py:21
  76.2 0.0 collective-permute-done.5.from_below
  76.3 3.8 %collective-permute-start.6 = (bf16[16,2,512]{2,1,0:T(2,128)(2,1)S(1)}, bf16[16,2,512]{2,1,0:T(2,128)(2,1)S(1)}, u32[]{:S(2)}, u32[]{:S(2)}) collective-permute-start(bf16[16,2,512]{2,1,0:T(2,128)(2,1)S(1)} %get-tuple-element.58), channel_id=1, source_target_pairs={{0,1},{1,2},{2,3},{4,5},{5,6},{6,7},{8,9},{9,10},{10,11},{12,13},{... | collective-permute-start | bytes 98312 | tf_op jit(solution)/shard_map/ppermute | solution.py:21
  80.0 1.9 %collective-permute-start.7 = (bf16[16,2,512]{2,1,0:T(2,128)(2,1)S(1)}, bf16[16,2,512]{2,1,0:T(2,128)(2,1)S(1)}, u32[]{:S(2)}, u32[]{:S(2)}) collective-permute-start(bf16[16,2,512]{2,1,0:T(2,128)(2,1)S(1)} %get-tuple-element.59), channel_id=1, source_target_pairs={{1,0},{2,1},{3,2},{5,4},{6,5},{7,6},{9,8},{10,9},{11,10},{13,12},{... | collective-permute-start | bytes 98312 | tf_op jit(solution)/shard_map/ppermute | solution.py:21
  82.0 0.0 collective-permute-done.6.from_left
  82.0 3.3 %collective-permute-done.7.from_right = bf16[16,2,512]{2,1,0:T(2,128)(2,1)S(1)} collective-permute-done((bf16[16,2,512]{2,1,0:T(2,128)(2,1)S(1)}, bf16[16,2,512]{2,1,0:T(2,128)(2,1)S(1)}, u32[]{:S(2)}, u32[]{:S(2)}) %collective-permute-start.7) | collective-permute-done | bytes 32800 | tf_op jit(solution)/shard_map/ppermute | solution.py:21
  85.3 2.1 %join.1 = bf16[16,64,512]{2,1,0:T(8,128)(2,1)} custom-call(bf16[16,64,512]{2,1,0:T(8,128)(2,1)} %get-tuple-element.53.grads, bf16[2,64,512]{2,1,0:T(8,128)(2,1)S(1)} %get-tuple-element.37.top, bf16[2,64,512]{2,1,0:T(8,128)(2,1)S(1)} %copy-done.5, bf16[16,2,512]{2,1,0:T(2,128)(2,1)S(1)} %get-tuple-element.38.first, ...), custom_call_target="tpu_custom_call", output_to_operand_aliasing={{}: (0, {})} | custom-call | tf_op jit(solution)/shard_map/join/pallas_call | solution.py:679
  87.4 0.0 all-to-all-done.1
  87.4 2.0 %sums.1 = (f32[27,64,64]{2,1,0:T(8,128)}, f32[27,64,64]{2,1,0:T(8,128)}) custom-call(bf16[1792,128]{1,0:T(8,128)(2,1)S(1)} %bitcast.6), custom_call_target="tpu_custom_call" | custom-call | tf_op jit(solution)/shard_map/sums/pallas_call | solution.py:725
  (13 shorter events, 0.1 us)
Async XLA Ops:
  0.6 7.7 %copy-start.7 = (s32[16,64]{1,0:T(8,128)S(1)}, s32[16,64]{1,0:T(8,128)}, u32[]{:S(2)}) copy-start(s32[16,64]{1,0:T(8,128)} %high.3) | copy-start | bytes 12292
  0.6 7.7 %copy-start.6 = (s32[16,64]{1,0:T(8,128)S(1)}, s32[16,64]{1,0:T(8,128)}, u32[]{:S(2)}) copy-start(s32[16,64]{1,0:T(8,128)} %low.3) | copy-start | bytes 12292
  0.7 7.7 %copy-start = (bf16[16,64,512]{2,1,0:T(8,128)(2,1)S(1)}, bf16[16,64,512]{2,1,0:T(8,128)(2,1)}, u32[]{:S(2)}) copy-start(bf16[16,64,512]{2,1,0:T(8,128)(2,1)} %bottom_in.1) | copy-start | bytes 3145732
  0.7 7.7 %copy-start.3 = (bf16[27,64,64]{2,1,0:T(8,128)(2,1)S(1)}, bf16[27,64,64]{2,1,0:T(8,128)(2,1)}, u32[]{:S(2)}) copy-start(bf16[27,64,64]{2,1,0:T(8,128)(2,1)} %weight_two.1) | copy-start | bytes 663556
  0.7 7.7 %copy-start.2 = (bf16[27,64,64]{2,1,0:T(8,128)(2,1)S(1)}, bf16[27,64,64]{2,1,0:T(8,128)(2,1)}, u32[]{:S(2)}) copy-start(bf16[27,64,64]{2,1,0:T(8,128)(2,1)} %weight_one.1) | copy-start | bytes 663556
  0.7 21.3 %copy-start.11 = (f32[64]{0:T(128)S(1)}, f32[64]{0:T(128)}, u32[]{:S(2)}) copy-start(f32[64]{0:T(128)} %param.19) | copy-start | bytes 772
  0.7 21.3 %copy-start.10 = (f32[64]{0:T(128)S(1)}, f32[64]{0:T(128)}, u32[]{:S(2)}) copy-start(f32[64]{0:T(128)} %param.18) | copy-start | bytes 772
  0.7 21.3 %copy-start.9 = (f32[64]{0:T(128)S(1)}, f32[64]{0:T(128)}, u32[]{:S(2)}) copy-start(f32[64]{0:T(128)} %param.17) | copy-start | bytes 772
  0.7 21.3 %copy-start.8 = (f32[64]{0:T(128)S(1)}, f32[64]{0:T(128)}, u32[]{:S(2)}) copy-start(f32[64]{0:T(128)} %param.16) | copy-start | bytes 772
  0.7 21.3 %copy-start.1 = (bf16[16,64,512]{2,1,0:T(8,128)(2,1)S(1)}, bf16[16,64,512]{2,1,0:T(8,128)(2,1)}, u32[]{:S(2)}) copy-start(bf16[16,64,512]{2,1,0:T(8,128)(2,1)} %cotangent.1) | copy-start | bytes 3145732
  2.1 19.9 %copy-start.4 = (bf16[2,64,512]{2,1,0:T(8,128)(2,1)}, bf16[2,64,512]{2,1,0:T(8,128)(2,1)S(1)}, u32[]{:S(2)}) copy-start(bf16[2,64,512]{2,1,0:T(8,128)(2,1)S(1)} %get-tuple-element.36.bottom) | copy-start | bytes 393220
  2.1 7.7 %collective-permute-start = (bf16[2,64,512]{2,1,0:T(8,128)(2,1)S(1)}, bf16[2,64,512]{2,1,0:T(8,128)(2,1)S(1)}, u32[]{:S(2)}, u32[]{:S(2)}) collective-permute-start(bf16[2,64,512]{2,1,0:T(8,128)(2,1)S(1)} %get-tuple-element.36.bottom), channel_id=1, source_target_pairs={{0,4},{4,8},{8,12},{12,16},{16,20},{20,24},{24,28},{1,5},{5,9},{9,... | collective-permute-start | bytes 393224 | tf_op jit(solution)/shard_map/ppermute | solution.py:21
  5.3 7.2 %collective-permute-start.1 = (bf16[2,64,512]{2,1,0:T(8,128)(2,1)S(1)}, bf16[2,64,512]{2,1,0:T(8,128)(2,1)S(1)}, u32[]{:S(2)}, u32[]{:S(2)}) collective-permute-start(bf16[2,64,512]{2,1,0:T(8,128)(2,1)S(1)} %get-tuple-element.37.top), channel_id=1, source_target_pairs={{4,0},{8,4},{12,8},{16,12},{20,16},{24,20},{28,24},{5,1},{9,5},{13... | collective-permute-start | bytes 393224 | tf_op jit(solution)/shard_map/ppermute | solution.py:21
  12.4 6.2 %collective-permute-start.2 = (bf16[20,2,512]{2,1,0:T(2,128)(2,1)S(1)}, bf16[20,2,512]{2,1,0:T(2,128)(2,1)S(1)}, u32[]{:S(2)}, u32[]{:S(2)}) collective-permute-start(bf16[20,2,512]{2,1,0:T(2,128)(2,1)S(1)} %get-tuple-element.40), channel_id=1, source_target_pairs={{0,1},{1,2},{2,3},{4,5},{5,6},{6,7},{8,9},{9,10},{10,11},{12,13},{... | collective-permute-start | bytes 122888 | tf_op jit(solution)/shard_map/ppermute | solution.py:21
  16.7 5.3 %collective-permute-start.3 = (bf16[20,2,512]{2,1,0:T(2,128)(2,1)S(1)}, bf16[20,2,512]{2,1,0:T(2,128)(2,1)S(1)}, u32[]{:S(2)}, u32[]{:S(2)}) collective-permute-start(bf16[20,2,512]{2,1,0:T(2,128)(2,1)S(1)} %get-tuple-element.41), channel_id=1, source_target_pairs={{1,0},{2,1},{3,2},{5,4},{6,5},{7,6},{9,8},{10,9},{11,10},{13,12},{... | collective-permute-start | bytes 122888 | tf_op jit(solution)/shard_map/ppermute | solution.py:21
  38.8 16.9 %all-to-all-start = ((bf16[32,56,128]{2,1,0:T(8,128)(2,1)}), bf16[32,56,128]{2,1,0:T(8,128)(2,1)S(1)}, u32[]{:S(2)}, u32[]{:S(2)}) async-start(bf16[32,56,128]{2,1,0:T(8,128)(2,1)} %bitcast.11), calls=%async_computation | async-start | bytes 917504 | tf_op jit(solution)/shard_map/all_to_all | solution.py:758
  49.4 0.7 copy-start.12
  50.1 0.7 copy-start.14
  50.7 34.5 %copy-start.5 = (bf16[2,64,512]{2,1,0:T(8,128)(2,1)S(1)}, bf16[2,64,512]{2,1,0:T(8,128)(2,1)}, u32[]{:S(2)}) copy-start(bf16[2,64,512]{2,1,0:T(8,128)(2,1)} %copy-done.4) | copy-start | bytes 393220
  55.6 5.3 %copy-start.15 = (bf16[2,72,512]{2,1,0:T(8,128)(2,1)S(1)}, bf16[2,72,512]{2,1,0:T(8,128)(2,1)}, u32[]{:S(2)}) copy-start(bf16[2,72,512]{2,1,0:T(8,128)(2,1)} %copy-done.14) | copy-start | bytes 442372
  55.6 8.4 %copy-start.13 = (bf16[2,72,512]{2,1,0:T(8,128)(2,1)S(1)}, bf16[2,72,512]{2,1,0:T(8,128)(2,1)}, u32[]{:S(2)}) copy-start(bf16[2,72,512]{2,1,0:T(8,128)(2,1)} %copy-done.12) | copy-start | bytes 442372
  56.5 30.9 %all-to-all-start.1 = ((bf16[32,56,128]{2,1,0:T(8,128)(2,1)}), bf16[32,56,128]{2,1,0:T(8,128)(2,1)S(1)}, u32[]{:S(2)}, u32[]{:S(2)}) async-start(bf16[32,56,128]{2,1,0:T(8,128)(2,1)} %part.1), calls=%async_computation.1 | async-start | bytes 917504 | tf_op jit(solution)/shard_map/all_to_all | solution.py:766
  60.9 15.3 %collective-permute-start.4 = (bf16[2,72,512]{2,1,0:T(8,128)(2,1)S(1)}, bf16[2,72,512]{2,1,0:T(8,128)(2,1)S(1)}, u32[]{:S(2)}, u32[]{:S(2)}) collective-permute-start(bf16[2,72,512]{2,1,0:T(8,128)(2,1)S(1)} %copy-done.15), channel_id=1, source_target_pairs={{0,4},{4,8},{8,12},{12,16},{16,20},{20,24},{24,28},{1,5},{5,9},{9,... | collective-permute-start | bytes 442376 | tf_op jit(solution)/shard_map/ppermute | solution.py:21
  64.0 12.2 %collective-permute-start.5 = (bf16[2,72,512]{2,1,0:T(8,128)(2,1)S(1)}, bf16[2,72,512]{2,1,0:T(8,128)(2,1)S(1)}, u32[]{:S(2)}, u32[]{:S(2)}) collective-permute-start(bf16[2,72,512]{2,1,0:T(8,128)(2,1)S(1)} %copy-done.13), channel_id=1, source_target_pairs={{4,0},{8,4},{12,8},{16,12},{20,16},{24,20},{28,24},{5,1},{9,5},{13... | collective-permute-start | bytes 442376 | tf_op jit(solution)/shard_map/ppermute | solution.py:21
  76.3 5.7 %collective-permute-start.6 = (bf16[16,2,512]{2,1,0:T(2,128)(2,1)S(1)}, bf16[16,2,512]{2,1,0:T(2,128)(2,1)S(1)}, u32[]{:S(2)}, u32[]{:S(2)}) collective-permute-start(bf16[16,2,512]{2,1,0:T(2,128)(2,1)S(1)} %get-tuple-element.58), channel_id=1, source_target_pairs={{0,1},{1,2},{2,3},{4,5},{5,6},{6,7},{8,9},{9,10},{10,11},{12,13},{... | collective-permute-start | bytes 98312 | tf_op jit(solution)/shard_map/ppermute | solution.py:21
  80.0 5.2 %collective-permute-start.7 = (bf16[16,2,512]{2,1,0:T(2,128)(2,1)S(1)}, bf16[16,2,512]{2,1,0:T(2,128)(2,1)S(1)}, u32[]{:S(2)}, u32[]{:S(2)}) collective-permute-start(bf16[16,2,512]{2,1,0:T(2,128)(2,1)S(1)} %get-tuple-element.59), channel_id=1, source_target_pairs={{1,0},{2,1},{3,2},{5,4},{6,5},{7,6},{9,8},{10,9},{11,10},{13,12},{... | collective-permute-start | bytes 98312 | tf_op jit(solution)/shard_map/ppermute | solution.py:21

commit v4 on v3

--- a/solution.py
+++ b/solution.py
@@ -46,6 +46,7 @@
 
 VMEM = pl.BlockSpec(memory_space=pltpu.VMEM)
 SMEM = pl.BlockSpec(memory_space=pltpu.SMEM)
+ANY = pl.BlockSpec(memory_space=pl.ANY)
 shape = jax.ShapeDtypeStruct
 held = pltpu.VMEM
 
@@ -133,8 +134,18 @@
     )(*near(above, below, first, last))
 
 
+def decode(fx, ms, x, pieces, start, stop):
+    kept = []
+    for m, v in enumerate(pieces):
+        ms[m, x, start:stop, :] = jnp.where(v == 0.0, 0.0, 1.0)
+        kept.append(jnp.where(v == EMPTY_FEATURE, 0.0, v))
+    for p, v in enumerate(to_shifted(kept)):
+        fx[p, x, start:stop, :] = v
+
+
 def tile_kernel(
-    features, low, high, weight_one, weight_two, slots, tiles, tiles_last, packed, first, last
+    features, low, high, weight_one, weight_two, slots, bands_a, bands_b, bands_c, bands_d,
+    packed, first, last, fx, ms,
 ):
     lx, ly = low.shape
     filled = jnp.where(high[...] > low[...], 1.0, 0.0)
@@ -171,15 +182,32 @@
 
     for x in range(lx):
         floor, high_of = column_bounds(low, high, x)
+        pieces = []
         for m in range(4):
             lanes = slice(128 * m, 128 * m + 128)
             v = encode(features[x, :, lanes].astype(F32), floor, high_of, 2 * m)
             packed[x, :, lanes] = v.astype(BF16)
             first[x, :, lanes] = v[0:2].astype(BF16)
             last[x, :, lanes] = v[ly - 2 : ly].astype(BF16)
+            pieces.append(v)
+        decode(fx, ms, x + 2, pieces, 8, 8 + ly)
+    for x in range(lx + 4):
+        for base in (0, 8 + ly):
+            for m in range(4):
+                ms[m, x, base : base + 8, :] = jnp.zeros((8, 128), F32)
+            for p in range(5):
+                fx[p, x, base : base + 8, :] = jnp.zeros((8, 128), F32)
 
     zero = jnp.zeros((64, 64), BF16)
-    for conv, weight in enumerate((weight_one, weight_two, weight_two, weight_one)):
+    for conv, (weight, bands) in enumerate(
+        (
+            (weight_one, bands_a),
+            (weight_two, bands_b),
+            (weight_two, bands_c),
+            (weight_one, bands_d),
+        )
+    ):
+        bands[...] = jnp.zeros(bands.shape, BF16)
         for tap in range(9):
             taps = []
             for oz in range(3):
@@ -190,43 +218,33 @@
             taps = [zero] + taps + [zero]
             for d in range(4):
                 tile = jnp.concatenate([taps[d + 1], taps[d]], axis=1)
-                if conv < 3:
-                    tiles[conv, tap, d] = tile
-                else:
-                    tiles_last[tap, d] = tile
+                for q in range(2):
+                    r = d + 2 * q
+                    row = 1152 * (tap // 3) + ((r // 2) * 3 + tap % 3) * 128 + (r % 2) * 64
+                    bands[row : row + 64, 128 * q : 128 * q + 128] = tile
 
 
 def tile_call(features, low, high, weight_one, weight_two):
-    lx, _, width = features.shape
+    lx, ly, width = features.shape
     return pl.pallas_call(
         tile_kernel,
         out_shape=(
             shape((3 * ACT_MAX,), jnp.int32),
-            held((3, 9, 4, 64, 128), BF16),
-            held((9, 4, 64, 128), BF16),
+            held((3456, 256), BF16),
+            held((3456, 256), BF16),
+            held((3456, 256), BF16),
+            held((3456, 256), BF16),
             held(features.shape, BF16),
             held((lx, 2, width), BF16),
             held((lx, 2, width), BF16),
+            held((5, lx + 4, ly + 16, 128), F32),
+            held((4, lx + 4, ly + 16, 128), F32),
         ),
         in_specs=[VMEM] * 5,
-        out_specs=(SMEM,) + (VMEM,) * 5,
+        out_specs=(SMEM,) + (VMEM,) * 9,
         compiler_params=pltpu.CompilerParams(vmem_limit_bytes=8 << 20),
         name="tiles",
-    )(features, low, high, weight_one, weight_two)
-
-
-def build_bands(bands, tile_at):
-    bands[...] = jnp.zeros(bands.shape, BF16)
-    for ox in range(3):
-        for oy in range(3):
-            for r in range(6):
-                for q in range(2):
-                    d = r - 2 * q
-                    if 0 <= d < 4:
-                        row = 1152 * ox + ((r // 2) * 3 + oy) * 128 + (r % 2) * 64
-                        bands[row : row + 64, 128 * q : 128 * q + 128] = tile_at(
-                            ox * 3 + oy, d
-                        )
+    )(*far(features, low, high, weight_one, weight_two))
 
 
 def convolve(source, bands, acc, xs):
@@ -252,48 +270,29 @@
 
 
 def brick_kernel(
-    slots, packed, above, below, left, right, cotangent, tiles, s_one, t_one, s_two, t_two,
-    out, errors_out, grads_out, total,
-    fx, ms, bands_a, bands_b, bands_c, c1, c2, c3, acc, slope, h, e2, er2, ets, et1, folded,
+    slots, bands_a, bands_b, bands_c, fx_in, ms_in, above, below, left, right, cotangent,
+    s_one, t_one, s_two, t_two,
+    results, errors_out, grads_out, total, fx, ms,
+    c1, c2, c3, acc, slope, h, e2, er2, ets, et1, folded,
 ):
-    lx, ly = out.shape[0], out.shape[1]
+    lx, ly = cotangent.shape[0], cotangent.shape[1]
     low_row = low_lanes((1, 128))
     scale_one, shift_one = twice(s_one[...]), twice(t_one[...])
     scale_two, shift_two = twice(s_two[...]), twice(t_two[...])
 
-    build_bands(bands_a, lambda t, d: tiles[0, t, d])
-
     def put(x, strip, start, stop):
-        pieces = []
-        for m in range(4):
-            v = strip(m).astype(F32)
-            ms[m, x, start:stop, :] = jnp.where(v == 0.0, 0.0, 1.0)
-            pieces.append(jnp.where(v == EMPTY_FEATURE, 0.0, v))
-        for p, v in enumerate(to_shifted(pieces)):
-            fx[p, x, start:stop, :] = v
-
-    def own_row(i, _):
-        for k in range(2):
-            x = 2 * i + k
-            put(x + 2, lambda m: packed[x, :, 128 * m : 128 * m + 128], 8, 8 + ly)
-            out[x] = jnp.zeros(out.shape[1:], BF16)
-        return 0
-
-    lax.fori_loop(0, lx // 2, own_row, 0)
+        lanes = [slice(128 * m, 128 * m + 128) for m in range(4)]
+        decode(fx, ms, x, [strip[:, at].astype(F32) for at in lanes], start, stop)
+
     for x in range(2):
-        put(x, lambda m: above[x, :, 128 * m : 128 * m + 128], 8, 8 + ly)
-        put(lx + 2 + x, lambda m: below[x, :, 128 * m : 128 * m + 128], 8, 8 + ly)
+        put(x, above.at[x], 8, 8 + ly)
+        put(lx + 2 + x, below.at[x], 8, 8 + ly)
 
     def side_row(i, _):
         for k in range(4):
             x = 4 * i + k
-            for base in (0, 8 + ly):
-                for m in range(4):
-                    ms[m, x, base : base + 8, :] = jnp.zeros((8, 128), F32)
-                for p in range(5):
-                    fx[p, x, base : base + 8, :] = jnp.zeros((8, 128), F32)
-            put(x, lambda m: left[x, :, 128 * m : 128 * m + 128], 6, 8)
-            put(x, lambda m: right[x, :, 128 * m : 128 * m + 128], 8 + ly, 10 + ly)
+            put(x, left.at[x], 6, 8)
+            put(x, right.at[x], 8 + ly, 10 + ly)
         return 0
 
     lax.fori_loop(0, (lx + 4) // 4, side_row, 0)
@@ -308,7 +307,6 @@
         return 0
 
     lax.fori_loop(0, ACT_MAX, gather_one, 0)
-    build_bands(bands_b, lambda t, d: tiles[1, t, d])
     convolve(c1, bands_a, acc, 10)
 
     def hidden_of(i, _):
@@ -345,7 +343,6 @@
         return 0
 
     lax.fori_loop(0, ACT_MAX // 2, gather_two, 0)
-    build_bands(bands_c, lambda t, d: tiles[2, t, d])
     convolve(c2, bands_b, acc, 8)
 
     def finish_two(s, _):
@@ -374,13 +371,7 @@
                 errors.append(error)
                 er2[pl.ds(at, 8), lanes] = error
                 grads_out[s, x, :, lanes] = grad
-                result = jnp.where(
-                    odd,
-                    jnp.concatenate([zero, result], axis=0),
-                    jnp.concatenate([result, zero], axis=0),
-                )
-                now = out[x0 + x, pl.ds(y16, 16), lanes].astype(F32)
-                out[x0 + x, pl.ds(y16, 16), lanes] = (now + result).astype(BF16)
+                results[s, x, :, lanes] = result.astype(BF16)
             for p, v in enumerate(to_shifted(errors)):
                 e2[s, p, x + 2, 0:8, :] = zero
                 e2[s, p, x + 2, 8:16, :] = v
@@ -451,26 +442,22 @@
     total[27] = jnp.zeros((64, 128), BF16)
 
 
-def brick_call(slots, packed, above, below, left, right, cotangent, tiles, *vectors):
-    lx, ly, width = cotangent.shape
+def brick_call(slots, bands, fx, ms, above, below, left, right, cotangent, *vectors):
+    _, _, width = cotangent.shape
     n = ACT_MAX
-    wide = ly + 16
     return pl.pallas_call(
         brick_kernel,
         out_shape=(
-            shape((lx, ly, width), BF16),
-            held((n * 160, width), BF16),
-            held((n, 8, 8, width), F32),
+            pltpu.HBM((n, 8, 8, width), BF16),
+            pltpu.HBM((n * 160, width), BF16),
+            pltpu.HBM((n, 8, 8, width), F32),
             pltpu.HBM((28, 64, 128), BF16),
+            held(fx.shape, F32),
+            held(ms.shape, F32),
         ),
-        in_specs=[SMEM] + [VMEM] * 11,
-        out_specs=(VMEM,) * 4,
+        in_specs=[SMEM] + [VMEM] * 14,
+        out_specs=(VMEM,) * 6,
         scratch_shapes=[
-            pltpu.VMEM((5, lx + 4, wide, 128), F32),
-            pltpu.VMEM((4, lx + 4, wide, 128), F32),
-            pltpu.VMEM((3456, 256), BF16),
-            pltpu.VMEM((3456, 256), BF16),
-            pltpu.VMEM((3456, 256), BF16),
             pltpu.VMEM((n, 12, 16, 1920), BF16),
             pltpu.VMEM((n // 2, 10, 16, 1920), BF16),
             pltpu.VMEM((n, 12, 16, 1920), BF16),
@@ -483,22 +470,18 @@
             pltpu.VMEM((768, n * 160), BF16),
             pltpu.VMEM((27, 64, 128), F32),
         ],
-        compiler_params=pltpu.CompilerParams(vmem_limit_bytes=33 << 20),
+        input_output_aliases={4: 4, 5: 5},
+        compiler_params=pltpu.CompilerParams(vmem_limit_bytes=24 << 20),
         name="bricks",
-    )(
-        slots,
-        *near(packed, above, below, left, right, cotangent, tiles),
-        *vectors,
-    )
+    )(slots, *near(*bands, fx, ms, above, below, left, right, cotangent), *vectors)
 
 
 def input_kernel(
-    slots, errors, grads, packed, tiles, grad_own, grad_above, grad_below, grad_left, grad_right,
-    e1, c4, bands, acc, grid,
+    slots, errors, grads, packed, bands, grad_own, grad_above, grad_below, grad_left, grad_right,
+    e1, c4, acc, grid,
 ):
     lx, ly = grad_own.shape[0], grad_own.shape[1]
     wide = grid.shape[2]
-    build_bands(bands, lambda t, d: tiles[t, d])
 
     def clear_row(i, _):
         for k in range(2):
@@ -572,7 +555,7 @@
                 target[x, ly : ly + 8, lanes] = jnp.concatenate(corners, axis=0).astype(BF16)
 
 
-def input_call(slots, errors, grads, packed, tiles):
+def input_call(slots, errors, grads, packed, bands):
     lx, ly, width = packed.shape
     n = ACT_MAX
     return pl.pallas_call(
@@ -589,13 +572,12 @@
         scratch_shapes=[
             pltpu.VMEM((5, 14, 24, 128), F32),
             pltpu.VMEM((n, 14, 16, 1920), BF16),
-            pltpu.VMEM((3456, 256), BF16),
             pltpu.VMEM((n * 192, width), F32),
             pltpu.VMEM((4, lx + 4, ly + 16, 128), F32),
         ],
         compiler_params=pltpu.CompilerParams(vmem_limit_bytes=15 << 20),
         name="inputs",
-    )(slots, *near(errors, grads, packed, tiles))
+    )(slots, *far(errors, grads), *near(packed, bands))
 
 
 def ends_kernel(left, right, from_above, from_below, to_left, to_right):
@@ -622,7 +604,8 @@
 
 
 def join_kernel(
-    grads, top, bottom, first, last, from_left, from_right, from_above, from_below, joined,
+    slots, grads, results, top, bottom, first, last, from_left, from_right, from_above,
+    from_below, joined, out,
     rows_a, rows_b, cols_a, cols_b, sems,
 ):
     lx, ly, _ = joined.shape
@@ -637,9 +620,31 @@
     ]
     for copy in copies:
         copy.start()
+    width = rows_a.shape[2]
+
+    def clear_row(x, _):
+        out[x] = jnp.zeros(out.shape[1:], BF16)
+        return 0
+
+    lax.fori_loop(0, lx, clear_row, 0)
+
+    def put_brick(s, _):
+        x0, _, _ = place(slots, s)
+        odd = lax.rem(slots[ACT_MAX + s], 2) == 1
+        y16 = pl.multiple_of(slots[ACT_MAX + s] // 2 * 16, 16)
+        for x in range(8):
+            v = results[s, x].astype(F32)
+            zero = jnp.zeros_like(v)
+            v = jnp.where(
+                odd, jnp.concatenate([zero, v], axis=0), jnp.concatenate([v, zero], axis=0)
+            )
+            now = out[x0 + x, pl.ds(y16, 16), :].astype(F32)
+            out[x0 + x, pl.ds(y16, 16), :] = (now + v).astype(BF16)
+        return 0
+
+    lax.fori_loop(0, ACT_MAX, put_brick, 0)
     for copy in copies:
         copy.wait()
-    width = rows_a.shape[2]
 
     def first_add(strip, rows):
         return jnp.concatenate([strip.astype(F32), jnp.zeros((rows - 2, width), F32)], axis=0)
@@ -673,14 +678,13 @@
         copy.wait()
 
 
-def join_call(grads, *strips):
+def join_call(slots, grads, results, *strips):
     lx, ly, width = grads.shape
-    anywhere = pl.BlockSpec(memory_space=pl.ANY)
     return pl.pallas_call(
         join_kernel,
-        out_shape=shape(grads.shape, BF16),
-        in_specs=[anywhere] + [VMEM] * 8,
-        out_specs=anywhere,
+        out_shape=(shape(grads.shape, BF16), shape(grads.shape, BF16)),
+        in_specs=[SMEM, ANY] + [VMEM] * 9,
+        out_specs=(ANY, VMEM),
         scratch_shapes=[
             pltpu.VMEM((2, ly, width), BF16),
             pltpu.VMEM((2, ly, width), BF16),
@@ -688,10 +692,10 @@
             pltpu.VMEM((lx - 4, 16, width), BF16),
             pltpu.SemaphoreType.DMA((4,)),
         ],
-        input_output_aliases={0: 0},
+        input_output_aliases={1: 0},
         compiler_params=pltpu.CompilerParams(vmem_limit_bytes=8 << 20),
         name="join",
-    )(grads, *near(*strips))
+    )(slots, grads, *far(results), *near(*strips))
 
 
 def part_kernel(got, whole):
@@ -741,15 +745,15 @@
     top, bottom = strip_call(features, low, high)
     above = shifted_in(bottom, "gx", 1)
     below = shifted_in(top, "gx", -1)
-    slots, tiles, tiles_last, packed, first, last = tile_call(
+    slots, *bands, bands_last, packed, first, last, fx, ms = tile_call(
         features, low, high, weight_one, weight_two
     )
     to_left, to_right = side_call(above, below, first, last)
     left = shifted_in(to_right, "gy", 1)
     right = shifted_in(to_left, "gy", -1)
     vectors = [v.reshape(1, -1) for v in (scale_one, shift_one, scale_two, shift_two)]
-    out, errors, grads, sums = brick_call(
-        slots, packed, above, below, left, right, cotangent, tiles, *vectors
+    results, errors, grads, sums, _, _ = brick_call(
+        slots, bands, fx, ms, above, below, left, right, cotangent, *vectors
     )
 
     devices = nx * ny
@@ -757,7 +761,7 @@
     slots, errors, parts = lax.optimization_barrier((slots, errors, parts))
     got = lax.all_to_all(parts, ("gx", "gy"), 0, 0, tiled=True)
     own, grad_above, grad_below, grad_left, grad_right = input_call(
-        slots, errors, grads, packed, tiles_last
+        slots, errors, grads, packed, bands_last
     )
     from_below = shifted_in(grad_above, "gx", -1)
     from_above = shifted_in(grad_below, "gx", 1)
@@ -767,10 +771,11 @@
     to_left, to_right = ends_call(grad_left, grad_right, from_above, from_below)
     from_right = shifted_in(to_left, "gy", -1)
     from_left = shifted_in(to_right, "gy", 1)
-    grad_features = join_call(
-        own, top, bottom, first, last, from_left, from_right, from_above, from_below
+    grad_features, out = join_call(
+        slots, own, results, top, bottom, first, last, from_left, from_right, from_above,
+        from_below,
     )
-    back, grad_features = lax.optimization_barrier((back, grad_features))
+    back, grad_features, out = lax.optimization_barrier((back, grad_features, out))
     grad_one, grad_two = sums_call(back.reshape(-1, 128), 1.0 / (devices * SHARE))
     return (out, grad_features, grad_one, grad_two)
 

time: 90 us -> 91 us (1.011)
  Pallas kernels: 31 us -> 34.3 us
  waiting for transfers between devices: 23.3 us -> 20.3 us
    pallas_call x1, Pallas kernels: 1.4 us -> 4.23 us  [tile_call(): pl.pallas_call(tile_kernel, out_shape=(shape((3 * ACT_MAX,), jnp.int32),...]
    ppermute x8, waiting for transfers between devices: 18.4 us -> 15.8 us  [shifted_in(): return lax.ppermute(array, axis, pairs)]
    unnamed x32 -> x18, local copies, waits for them, and re-layouts: 1.37 us -> 2.24 us
  transfers between devices with their start and end apart: 10 -> 10, of which waited for: 5 -> 4; matrix products, arithmetic and copies ran while one was open for 0% -> 0% of each run, Pallas kernels for 11% -> 17%
where the time goes in v4:
time: 91 us; the launch traced here: 90.2 us
  Pallas kernels  34.3 us (38%)
  starting transfers between devices  32.5 us (36%)
  waiting for transfers between devices  20.3 us (22%)
  local copies, waits for them, and re-layouts  2.24 us (2%)
    ppermute x8, starting transfers between devices, shifted_in(): return lax.ppermute(array, axis, pairs)  24.2 us
    ppermute x8, waiting for transfers between devices, shifted_in(): return lax.ppermute(array, axis, pairs)  15.8 us
    pallas_call x1, Pallas kernels, brick_call(): pl.pallas_call(brick_kernel, out_shape=(pltpu.HBM((n, 8, 8, width), BF16)...  14.8 us
    pallas_call x1, Pallas kernels, input_call(): pl.pallas_call(input_kernel, out_shape=(shape((lx, ly, width), BF16), hel...  7.02 us
    all_to_all x1, waiting for transfers between devices, shards(): got = lax.all_to_all(parts, ('gx', 'gy'), 0, 0, tiled=True)  4.45 us
    all_to_all x1, starting transfers between devices, shards(): back = lax.all_to_all(mine, ('gx', 'gy'), 0, 0, tiled=True)  4.39 us
    pallas_call x1, Pallas kernels, tile_call(): pl.pallas_call(tile_kernel, out_shape=(shape((3 * ACT_MAX,), jnp.int32),...  4.23 us
    pallas_call x1, Pallas kernels, join_call(): pl.pallas_call(join_kernel, out_shape=(shape(grads.shape, BF16), shape(gr...  4.03 us
  transfers between devices with their start and end apart: 10, of which 4 were waited for; matrix products, arithmetic and copies ran while one was open for 0% of the time, Pallas kernels for 17%

profile of v4, /device:TPU:17, one launch (start us, length us, event | category | flops | bytes accessed | tf_op | source)
XLA Modules:
  0.0 90.2 jit_solution(4422556627805940604)
XLA Ops:
  0.6 0.0 copy-start.6
  0.6 0.0 copy-start.5
  0.7 0.0 copy-start.4
  0.7 0.0 copy-start.3
  0.7 0.0 copy-start
  0.7 1.3 %strips.1 = (bf16[2,64,512]{2,1,0:T(8,128)(2,1)S(1)}, bf16[2,64,512]{2,1,0:T(8,128)(2,1)S(1)}) custom-call(bf16[16,64,512]{2,1,0:T(8,128)(2,1)} %bottom_in.1, bf16[16,64,512]{2,1,0:T(8,128)(2,1)} %bottom_in.1, s32[16,64]{1,0:T(8,128)} %low.3, s32[16,64]{1,0:T(8,128)} %high.3), custom_call_target="tpu_custom_call" | custom-call | tf_op jit(solution)/shard_map/strips/pallas_call | solution.py:97
  2.0 0.0 copy-start.1
  2.0 3.1 %collective-permute-start = (bf16[2,64,512]{2,1,0:T(8,128)(2,1)S(1)}, bf16[2,64,512]{2,1,0:T(8,128)(2,1)S(1)}, u32[]{:S(2)}, u32[]{:S(2)}) collective-permute-start(bf16[2,64,512]{2,1,0:T(8,128)(2,1)S(1)} %get-tuple-element.47.bottom), channel_id=1, source_target_pairs={{0,4},{4,8},{8,12},{12,16},{16,20},{20,24},{24,28},{1,5},{5,9},{9,... | collective-permute-start | bytes 393224 | tf_op jit(solution)/shard_map/ppermute | solution.py:21
  5.1 3.1 %collective-permute-start.1 = (bf16[2,64,512]{2,1,0:T(8,128)(2,1)S(1)}, bf16[2,64,512]{2,1,0:T(8,128)(2,1)S(1)}, u32[]{:S(2)}, u32[]{:S(2)}) collective-permute-start(bf16[2,64,512]{2,1,0:T(8,128)(2,1)S(1)} %get-tuple-element.48.top), channel_id=1, source_target_pairs={{4,0},{8,4},{12,8},{16,12},{20,16},{24,20},{28,24},{5,1},{9,5},{13... | collective-permute-start | bytes 393224 | tf_op jit(solution)/shard_map/ppermute | solution.py:21
  8.2 4.2 %tiles.1 = (s32[12]{0:T(128)S(1)}, bf16[3456,256]{1,0:T(8,128)(2,1)S(1)}, bf16[3456,256]{1,0:T(8,128)(2,1)S(1)}, bf16[3456,256]{1,0:T(8,128)(2,1)S(1)}, bf16[345...) custom-call(bf16[16,64,512]{2,1,0:T(8,128)(2,1)} %bottom_in.1, ...), custom_call_target="tpu_custom_call" | custom-call | tf_op jit(solution)/shard_map/tiles/pallas_call | solution.py:229
  12.5 0.0 collective-permute-done.above
  12.5 0.0 collective-permute-done.1.below
  12.5 4.3 %collective-permute-start.2 = (bf16[20,2,512]{2,1,0:T(2,128)(2,1)S(1)}, bf16[20,2,512]{2,1,0:T(2,128)(2,1)S(1)}, u32[]{:S(2)}, u32[]{:S(2)}) collective-permute-start(bf16[20,2,512]{2,1,0:T(2,128)(2,1)S(1)} %get-tuple-element.51), channel_id=1, source_target_pairs={{0,1},{1,2},{2,3},{4,5},{5,6},{6,7},{8,9},{9,10},{10,11},{12,13},{... | collective-permute-start | bytes 122888 | tf_op jit(solution)/shard_map/ppermute | solution.py:21
  16.8 1.9 %collective-permute-start.3 = (bf16[20,2,512]{2,1,0:T(2,128)(2,1)S(1)}, bf16[20,2,512]{2,1,0:T(2,128)(2,1)S(1)}, u32[]{:S(2)}, u32[]{:S(2)}) collective-permute-start(bf16[20,2,512]{2,1,0:T(2,128)(2,1)S(1)} %get-tuple-element.52), channel_id=1, source_target_pairs={{1,0},{2,1},{3,2},{5,4},{6,5},{7,6},{9,8},{10,9},{11,10},{13,12},{... | collective-permute-start | bytes 122888 | tf_op jit(solution)/shard_map/ppermute | solution.py:21
  18.7 0.0 collective-permute-done.2.left
  18.7 3.4 %collective-permute-done.3.right = bf16[20,2,512]{2,1,0:T(2,128)(2,1)S(1)} collective-permute-done((bf16[20,2,512]{2,1,0:T(2,128)(2,1)S(1)}, bf16[20,2,512]{2,1,0:T(2,128)(2,1)S(1)}, u32[]{:S(2)}, u32[]{:S(2)}) %collective-permute-start.3) | collective-permute-done | bytes 40992 | tf_op jit(solution)/shard_map/ppermute | solution.py:21
  22.1 0.0 copy-done.6
  22.1 0.0 copy-done.5
  22.1 0.0 copy-done.4
  22.1 0.0 copy-done.3
  22.1 0.0 copy-done
  22.1 14.8 %bricks.1 = (bf16[4,8,8,512]{3,2,1,0:T(8,128)(2,1)}, bf16[640,512]{1,0:T(8,128)(2,1)}, f32[4,8,8,512]{3,2,1,0:T(8,128)}, bf16[28,64,128]{2,1,0:T(8,128)(2,1)}, f...) custom-call(s32[12]{0:T(128)S(1)} %get-tuple-element.56.slots, ...), custom_call_target="tpu_custom_call", output_to_operand_aliasing={{4}: (4, {}), {5}: (5, {})} | custom-call | tf_op jit(solution)/shard_map/bricks/pallas_call | solution.py:448
  37.0 0.0 copy-done.1
  37.0 3.9 %all-to-all-start = ((bf16[32,56,128]{2,1,0:T(8,128)(2,1)}), bf16[32,56,128]{2,1,0:T(8,128)(2,1)S(1)}, u32[]{:S(2)}, u32[]{:S(2)}) async-start(bf16[32,56,128]{2,1,0:T(8,128)(2,1)} %bitcast.11), calls=%async_computation | async-start | bytes 917504 | tf_op jit(solution)/shard_map/all_to_all | solution.py:762
  40.9 7.0 %inputs.1 = (bf16[16,64,512]{2,1,0:T(8,128)(2,1)}, bf16[2,72,512]{2,1,0:T(8,128)(2,1)S(1)}, bf16[2,72,512]{2,1,0:T(8,128)(2,1)S(1)}, bf16[16,2,512]{2,1,0:T(2,128)(2,1)S(1)}, bf16[16,2,512]{2,1,0:T(2,128)(2,1)S(1)}) custom-call(s32[12]{0:T(128)S(1)} %get-tuple-element.56.slots, bf16[640,512]{1,0:T(8,128)(2,1)} %get-tuple-element.57.errors, ...), custom_call_target="tpu_custom_call" | custom-call | tf_op jit(solution)/shard_map/inputs/pallas_call | solution.py:561
  47.9 0.0 copy-start.7
  47.9 0.6 copy-done.7
  48.6 0.0 copy-start.8
  48.6 0.7 copy-done.8
  49.2 4.4 %all-to-all-done.got = bf16[32,56,128]{2,1,0:T(8,128)(2,1)S(1)} async-done(((bf16[32,56,128]{2,1,0:T(8,128)(2,1)}), bf16[32,56,128]{2,1,0:T(8,128)(2,1)S(1)}, u32[]{:S(2)}, u32[]{:S(2)}) %all-to-all-start) | async-done | bytes 458784 | tf_op jit(solution)/shard_map/all_to_all | solution.py:762
  53.7 0.9 part.1
  54.5 4.4 %all-to-all-start.1 = ((bf16[32,56,128]{2,1,0:T(8,128)(2,1)}), bf16[32,56,128]{2,1,0:T(8,128)(2,1)S(1)}, u32[]{:S(2)}, u32[]{:S(2)}) async-start(bf16[32,56,128]{2,1,0:T(8,128)(2,1)} %part.1), calls=%async_computation.1 | async-start | bytes 917504 | tf_op jit(solution)/shard_map/all_to_all | solution.py:770
  58.9 3.1 %collective-permute-start.4 = (bf16[2,72,512]{2,1,0:T(8,128)(2,1)}, bf16[2,72,512]{2,1,0:T(8,128)(2,1)S(1)}, u32[]{:S(2)}, u32[]{:S(2)}) collective-permute-start(bf16[2,72,512]{2,1,0:T(8,128)(2,1)} %copy-done.8), channel_id=1, source_target_pairs={{0,4},{4,8},{8,12},{12,16},{16,20},{20,24},{24,28},{1,5},{5,9},{9,... | collective-permute-start | bytes 442376 | tf_op jit(solution)/shard_map/ppermute | solution.py:21
  62.0 3.1 %collective-permute-start.5 = (bf16[2,72,512]{2,1,0:T(8,128)(2,1)}, bf16[2,72,512]{2,1,0:T(8,128)(2,1)S(1)}, u32[]{:S(2)}, u32[]{:S(2)}) collective-permute-start(bf16[2,72,512]{2,1,0:T(8,128)(2,1)} %copy-done.7), channel_id=1, source_target_pairs={{4,0},{8,4},{12,8},{16,12},{20,16},{24,20},{28,24},{5,1},{9,5},{13... | collective-permute-start | bytes 442376 | tf_op jit(solution)/shard_map/ppermute | solution.py:21
  65.1 9.1 %collective-permute-done.4.from_above = bf16[2,72,512]{2,1,0:T(8,128)(2,1)S(1)} collective-permute-done((bf16[2,72,512]{2,1,0:T(8,128)(2,1)}, bf16[2,72,512]{2,1,0:T(8,128)(2,1)S(1)}, u32[]{:S(2)}, u32[]{:S(2)}) %collective-permute-start.4) | collective-permute-done | bytes 147488 | tf_op jit(solution)/shard_map/ppermute | solution.py:21
  74.3 0.0 collective-permute-done.5.from_below
  74.3 3.8 %collective-permute-start.6 = (bf16[16,2,512]{2,1,0:T(2,128)(2,1)S(1)}, bf16[16,2,512]{2,1,0:T(2,128)(2,1)S(1)}, u32[]{:S(2)}, u32[]{:S(2)}) collective-permute-start(bf16[16,2,512]{2,1,0:T(2,128)(2,1)S(1)} %get-tuple-element.69), channel_id=1, source_target_pairs={{0,1},{1,2},{2,3},{4,5},{5,6},{6,7},{8,9},{9,10},{10,11},{12,13},{... | collective-permute-start | bytes 98312 | tf_op jit(solution)/shard_map/ppermute | solution.py:21
  78.1 1.9 %collective-permute-start.7 = (bf16[16,2,512]{2,1,0:T(2,128)(2,1)S(1)}, bf16[16,2,512]{2,1,0:T(2,128)(2,1)S(1)}, u32[]{:S(2)}, u32[]{:S(2)}) collective-permute-start(bf16[16,2,512]{2,1,0:T(2,128)(2,1)S(1)} %get-tuple-element.70), channel_id=1, source_target_pairs={{1,0},{2,1},{3,2},{5,4},{6,5},{7,6},{9,8},{10,9},{11,10},{13,12},{... | collective-permute-start | bytes 98312 | tf_op jit(solution)/shard_map/ppermute | solution.py:21
  80.0 0.0 collective-permute-done.6.from_left
  80.0 3.3 %collective-permute-done.7.from_right = bf16[16,2,512]{2,1,0:T(2,128)(2,1)S(1)} collective-permute-done((bf16[16,2,512]{2,1,0:T(2,128)(2,1)S(1)}, bf16[16,2,512]{2,1,0:T(2,128)(2,1)S(1)}, u32[]{:S(2)}, u32[]{:S(2)}) %collective-permute-start.7) | collective-permute-done | bytes 32800 | tf_op jit(solution)/shard_map/ppermute | solution.py:21
  83.3 0.0 copy-start.2
  83.3 0.9 %copy-done.2 = bf16[2,64,512]{2,1,0:T(8,128)(2,1)S(1)} copy-done((bf16[2,64,512]{2,1,0:T(8,128)(2,1)S(1)}, bf16[2,64,512]{2,1,0:T(8,128)(2,1)}, u32[]{:S(2)}) %copy-start.2) | copy-done | bytes 131096
  84.2 4.0 %join.1 = (bf16[16,64,512]{2,1,0:T(8,128)(2,1)}, bf16[16,64,512]{2,1,0:T(8,128)(2,1)}) custom-call(s32[12]{0:T(128)S(1)} %get-tuple-element.56.slots, bf16[16,64,512]{2,1,0:T(8,128)(2,1)} %get-tuple-element.63.grads, bf16[4,8,8,512]{3,2,1,0:T(8,128)(2,1)} %get-tuple-element.64.results, ...), custom_call_target="tpu_custom_call", output_to_operand_aliasing={{0}: (1, {})} | custom-call | tf_op jit(solution)/shard_map/join/pallas_call | solution.py:683
  88.3 0.0 all-to-all-done.1
  88.3 2.0 %sums.1 = (f32[27,64,64]{2,1,0:T(8,128)}, f32[27,64,64]{2,1,0:T(8,128)}) custom-call(bf16[1792,128]{1,0:T(8,128)(2,1)S(1)} %bitcast.6), custom_call_target="tpu_custom_call" | custom-call | tf_op jit(solution)/shard_map/sums/pallas_call | solution.py:729
  (2 shorter events, 0.0 us)
Async XLA Ops:
  0.6 21.5 %copy-start.6 = (f32[64]{0:T(128)S(1)}, f32[64]{0:T(128)}, u32[]{:S(2)}) copy-start(f32[64]{0:T(128)} %param.19) | copy-start | bytes 772
  0.6 21.5 %copy-start.5 = (f32[64]{0:T(128)S(1)}, f32[64]{0:T(128)}, u32[]{:S(2)}) copy-start(f32[64]{0:T(128)} %param.18) | copy-start | bytes 772
  0.7 21.4 %copy-start.4 = (f32[64]{0:T(128)S(1)}, f32[64]{0:T(128)}, u32[]{:S(2)}) copy-start(f32[64]{0:T(128)} %param.17) | copy-start | bytes 772
  0.7 21.4 %copy-start.3 = (f32[64]{0:T(128)S(1)}, f32[64]{0:T(128)}, u32[]{:S(2)}) copy-start(f32[64]{0:T(128)} %param.16) | copy-start | bytes 772
  0.7 21.4 %copy-start = (bf16[16,64,512]{2,1,0:T(8,128)(2,1)S(1)}, bf16[16,64,512]{2,1,0:T(8,128)(2,1)}, u32[]{:S(2)}) copy-start(bf16[16,64,512]{2,1,0:T(8,128)(2,1)} %cotangent.1) | copy-start | bytes 3145732
  2.0 35.0 %copy-start.1 = (bf16[2,64,512]{2,1,0:T(8,128)(2,1)}, bf16[2,64,512]{2,1,0:T(8,128)(2,1)S(1)}, u32[]{:S(2)}) copy-start(bf16[2,64,512]{2,1,0:T(8,128)(2,1)S(1)} %get-tuple-element.47.bottom) | copy-start | bytes 393220
  2.0 10.4 %collective-permute-start = (bf16[2,64,512]{2,1,0:T(8,128)(2,1)S(1)}, bf16[2,64,512]{2,1,0:T(8,128)(2,1)S(1)}, u32[]{:S(2)}, u32[]{:S(2)}) collective-permute-start(bf16[2,64,512]{2,1,0:T(8,128)(2,1)S(1)} %get-tuple-element.47.bottom), channel_id=1, source_target_pairs={{0,4},{4,8},{8,12},{12,16},{16,20},{20,24},{24,28},{1,5},{5,9},{9,... | collective-permute-start | bytes 393224 | tf_op jit(solution)/shard_map/ppermute | solution.py:21
  5.1 7.3 %collective-permute-start.1 = (bf16[2,64,512]{2,1,0:T(8,128)(2,1)S(1)}, bf16[2,64,512]{2,1,0:T(8,128)(2,1)S(1)}, u32[]{:S(2)}, u32[]{:S(2)}) collective-permute-start(bf16[2,64,512]{2,1,0:T(8,128)(2,1)S(1)} %get-tuple-element.48.top), channel_id=1, source_target_pairs={{4,0},{8,4},{12,8},{16,12},{20,16},{24,20},{28,24},{5,1},{9,5},{13... | collective-permute-start | bytes 393224 | tf_op jit(solution)/shard_map/ppermute | solution.py:21
  12.5 6.2 %collective-permute-start.2 = (bf16[20,2,512]{2,1,0:T(2,128)(2,1)S(1)}, bf16[20,2,512]{2,1,0:T(2,128)(2,1)S(1)}, u32[]{:S(2)}, u32[]{:S(2)}) collective-permute-start(bf16[20,2,512]{2,1,0:T(2,128)(2,1)S(1)} %get-tuple-element.51), channel_id=1, source_target_pairs={{0,1},{1,2},{2,3},{4,5},{5,6},{6,7},{8,9},{9,10},{10,11},{12,13},{... | collective-permute-start | bytes 122888 | tf_op jit(solution)/shard_map/ppermute | solution.py:21
  16.8 5.3 %collective-permute-start.3 = (bf16[20,2,512]{2,1,0:T(2,128)(2,1)S(1)}, bf16[20,2,512]{2,1,0:T(2,128)(2,1)S(1)}, u32[]{:S(2)}, u32[]{:S(2)}) collective-permute-start(bf16[20,2,512]{2,1,0:T(2,128)(2,1)S(1)} %get-tuple-element.52), channel_id=1, source_target_pairs={{1,0},{2,1},{3,2},{5,4},{6,5},{7,6},{9,8},{10,9},{11,10},{13,12},{... | collective-permute-start | bytes 122888 | tf_op jit(solution)/shard_map/ppermute | solution.py:21
  37.0 16.7 %all-to-all-start = ((bf16[32,56,128]{2,1,0:T(8,128)(2,1)}), bf16[32,56,128]{2,1,0:T(8,128)(2,1)S(1)}, u32[]{:S(2)}, u32[]{:S(2)}) async-start(bf16[32,56,128]{2,1,0:T(8,128)(2,1)} %bitcast.11), calls=%async_computation | async-start | bytes 917504 | tf_op jit(solution)/shard_map/all_to_all | solution.py:762
  47.9 0.7 copy-start.7
  48.6 0.7 copy-start.8
  54.5 33.7 %all-to-all-start.1 = ((bf16[32,56,128]{2,1,0:T(8,128)(2,1)}), bf16[32,56,128]{2,1,0:T(8,128)(2,1)S(1)}, u32[]{:S(2)}, u32[]{:S(2)}) async-start(bf16[32,56,128]{2,1,0:T(8,128)(2,1)} %part.1), calls=%async_computation.1 | async-start | bytes 917504 | tf_op jit(solution)/shard_map/all_to_all | solution.py:770
  58.9 15.3 %collective-permute-start.4 = (bf16[2,72,512]{2,1,0:T(8,128)(2,1)}, bf16[2,72,512]{2,1,0:T(8,128)(2,1)S(1)}, u32[]{:S(2)}, u32[]{:S(2)}) collective-permute-start(bf16[2,72,512]{2,1,0:T(8,128)(2,1)} %copy-done.8), channel_id=1, source_target_pairs={{0,4},{4,8},{8,12},{12,16},{16,20},{20,24},{24,28},{1,5},{5,9},{9,... | collective-permute-start | bytes 442376 | tf_op jit(solution)/shard_map/ppermute | solution.py:21
  62.0 12.2 %collective-permute-start.5 = (bf16[2,72,512]{2,1,0:T(8,128)(2,1)}, bf16[2,72,512]{2,1,0:T(8,128)(2,1)S(1)}, u32[]{:S(2)}, u32[]{:S(2)}) collective-permute-start(bf16[2,72,512]{2,1,0:T(8,128)(2,1)} %copy-done.7), channel_id=1, source_target_pairs={{4,0},{8,4},{12,8},{16,12},{20,16},{24,20},{28,24},{5,1},{9,5},{13... | collective-permute-start | bytes 442376 | tf_op jit(solution)/shard_map/ppermute | solution.py:21
  74.3 5.7 %collective-permute-start.6 = (bf16[16,2,512]{2,1,0:T(2,128)(2,1)S(1)}, bf16[16,2,512]{2,1,0:T(2,128)(2,1)S(1)}, u32[]{:S(2)}, u32[]{:S(2)}) collective-permute-start(bf16[16,2,512]{2,1,0:T(2,128)(2,1)S(1)} %get-tuple-element.69), channel_id=1, source_target_pairs={{0,1},{1,2},{2,3},{4,5},{5,6},{6,7},{8,9},{9,10},{10,11},{12,13},{... | collective-permute-start | bytes 98312 | tf_op jit(solution)/shard_map/ppermute | solution.py:21
  78.1 5.2 %collective-permute-start.7 = (bf16[16,2,512]{2,1,0:T(2,128)(2,1)S(1)}, bf16[16,2,512]{2,1,0:T(2,128)(2,1)S(1)}, u32[]{:S(2)}, u32[]{:S(2)}) collective-permute-start(bf16[16,2,512]{2,1,0:T(2,128)(2,1)S(1)} %get-tuple-element.70), channel_id=1, source_target_pairs={{1,0},{2,1},{3,2},{5,4},{6,5},{7,6},{9,8},{10,9},{11,10},{13,12},{... | collective-permute-start | bytes 98312 | tf_op jit(solution)/shard_map/ppermute | solution.py:21
  83.3 0.9 %copy-start.2 = (bf16[2,64,512]{2,1,0:T(8,128)(2,1)S(1)}, bf16[2,64,512]{2,1,0:T(8,128)(2,1)}, u32[]{:S(2)}) copy-start(bf16[2,64,512]{2,1,0:T(8,128)(2,1)} %copy-done.1) | copy-start | bytes 393220

commit v5 on v4

--- a/solution.py
+++ b/solution.py
@@ -715,23 +715,33 @@
     )(*near(got))
 
 
-def sums_kernel(sums, grad_one, grad_two, *, scale):
-    base = pl.program_id(0) * 9
-    for n in range(9):
-        at = pl.multiple_of(64 * (base + n), 64)
-        v = sums[pl.ds(at, 64)].astype(F32).T * scale
-        grad_one[n] = v[0:64]
-        grad_two[n] = v[64:128]
+def sums_kernel(sums, one_to, two_to, grad_one, grad_two, sems, *, scale):
+    leaving = []
+    for k in range(3):
+        taps = slice(9 * k, 9 * k + 9)
+        for n in range(9 * k, 9 * k + 9):
+            v = sums[64 * n : 64 * n + 64].astype(F32).T * scale
+            grad_one[n] = v[0:64]
+            grad_two[n] = v[64:128]
+        for side, (held_in, target) in enumerate(((grad_one, one_to), (grad_two, two_to))):
+            copy = pltpu.make_async_copy(held_in.at[taps], target.at[taps], sems.at[side, k])
+            copy.start()
+            leaving.append(copy)
+    for copy in leaving:
+        copy.wait()
 
 
 def sums_call(sums, scale):
-    taps = pl.BlockSpec((9, 64, 64), lambda i: (i, 0, 0))
     return pl.pallas_call(
         functools.partial(sums_kernel, scale=scale),
         out_shape=(shape((27, 64, 64), F32), shape((27, 64, 64), F32)),
-        grid=(3,),
         in_specs=[VMEM],
-        out_specs=(taps, taps),
+        out_specs=(ANY, ANY),
+        scratch_shapes=[
+            pltpu.VMEM((27, 64, 64), F32),
+            pltpu.VMEM((27, 64, 64), F32),
+            pltpu.SemaphoreType.DMA((2, 3)),
+        ],
         compiler_params=pltpu.CompilerParams(vmem_limit_bytes=8 << 20),
         name="sums",
     )(*near(sums))

time: 91 us -> 90.6 us (level)
  no operation moved by 1% of the time
where the time goes in v5:
time: 90.6 us; the launch traced here: 89.8 us
  Pallas kernels  33.8 us (37%)
  starting transfers between devices  32.5 us (36%)
  waiting for transfers between devices  20.3 us (22%)
  local copies, waits for them, and re-layouts  2.24 us (2%)
  between operations  1.02 us (1%)
    ppermute x8, starting transfers between devices, shifted_in(): return lax.ppermute(array, axis, pairs)  24.2 us
    ppermute x8, waiting for transfers between devices, shifted_in(): return lax.ppermute(array, axis, pairs)  15.8 us
    pallas_call x1, Pallas kernels, brick_call(): pl.pallas_call(brick_kernel, out_shape=(pltpu.HBM((n, 8, 8, width), BF16)...  14.8 us
    pallas_call x1, Pallas kernels, input_call(): pl.pallas_call(input_kernel, out_shape=(shape((lx, ly, width), BF16), hel...  7.02 us
    all_to_all x1, waiting for transfers between devices, shards(): got = lax.all_to_all(parts, ('gx', 'gy'), 0, 0, tiled=True)  4.45 us
    all_to_all x1, starting transfers between devices, shards(): back = lax.all_to_all(mine, ('gx', 'gy'), 0, 0, tiled=True)  4.39 us
    pallas_call x1, Pallas kernels, tile_call(): pl.pallas_call(tile_kernel, out_shape=(shape((3 * ACT_MAX,), jnp.int32),...  4.23 us
    pallas_call x1, Pallas kernels, join_call(): pl.pallas_call(join_kernel, out_shape=(shape(grads.shape, BF16), shape(gr...  4.03 us
  transfers between devices with their start and end apart: 10, of which 4 were waited for; matrix products, arithmetic and copies ran while one was open for 0% of the time, Pallas kernels for 17%

profile of v5, /device:TPU:17, one launch (start us, length us, event | category | flops | bytes accessed | tf_op | source)
XLA Modules:
  0.0 89.8 jit_solution(15221902490688064563)
XLA Ops:
  0.6 0.0 copy-start.6
  0.6 0.0 copy-start.5
  0.7 0.0 copy-start.4
  0.7 0.0 copy-start.3
  0.7 0.0 copy-start
  0.7 1.3 %strips.1 = (bf16[2,64,512]{2,1,0:T(8,128)(2,1)S(1)}, bf16[2,64,512]{2,1,0:T(8,128)(2,1)S(1)}) custom-call(bf16[16,64,512]{2,1,0:T(8,128)(2,1)} %bottom_in.1, bf16[16,64,512]{2,1,0:T(8,128)(2,1)} %bottom_in.1, s32[16,64]{1,0:T(8,128)} %low.3, s32[16,64]{1,0:T(8,128)} %high.3), custom_call_target="tpu_custom_call" | custom-call | tf_op jit(solution)/shard_map/strips/pallas_call | solution.py:97
  2.0 0.0 copy-start.1
  2.0 3.1 %collective-permute-start = (bf16[2,64,512]{2,1,0:T(8,128)(2,1)S(1)}, bf16[2,64,512]{2,1,0:T(8,128)(2,1)S(1)}, u32[]{:S(2)}, u32[]{:S(2)}) collective-permute-start(bf16[2,64,512]{2,1,0:T(8,128)(2,1)S(1)} %get-tuple-element.47.bottom), channel_id=1, source_target_pairs={{0,4},{4,8},{8,12},{12,16},{16,20},{20,24},{24,28},{1,5},{5,9},{9,... | collective-permute-start | bytes 393224 | tf_op jit(solution)/shard_map/ppermute | solution.py:21
  5.1 3.1 %collective-permute-start.1 = (bf16[2,64,512]{2,1,0:T(8,128)(2,1)S(1)}, bf16[2,64,512]{2,1,0:T(8,128)(2,1)S(1)}, u32[]{:S(2)}, u32[]{:S(2)}) collective-permute-start(bf16[2,64,512]{2,1,0:T(8,128)(2,1)S(1)} %get-tuple-element.48.top), channel_id=1, source_target_pairs={{4,0},{8,4},{12,8},{16,12},{20,16},{24,20},{28,24},{5,1},{9,5},{13... | collective-permute-start | bytes 393224 | tf_op jit(solution)/shard_map/ppermute | solution.py:21
  8.2 4.2 %tiles.1 = (s32[12]{0:T(128)S(1)}, bf16[3456,256]{1,0:T(8,128)(2,1)S(1)}, bf16[3456,256]{1,0:T(8,128)(2,1)S(1)}, bf16[3456,256]{1,0:T(8,128)(2,1)S(1)}, bf16[345...) custom-call(bf16[16,64,512]{2,1,0:T(8,128)(2,1)} %bottom_in.1, ...), custom_call_target="tpu_custom_call" | custom-call | tf_op jit(solution)/shard_map/tiles/pallas_call | solution.py:229
  12.5 0.0 collective-permute-done.above
  12.5 0.0 collective-permute-done.1.below
  12.5 4.3 %collective-permute-start.2 = (bf16[20,2,512]{2,1,0:T(2,128)(2,1)S(1)}, bf16[20,2,512]{2,1,0:T(2,128)(2,1)S(1)}, u32[]{:S(2)}, u32[]{:S(2)}) collective-permute-start(bf16[20,2,512]{2,1,0:T(2,128)(2,1)S(1)} %get-tuple-element.51), channel_id=1, source_target_pairs={{0,1},{1,2},{2,3},{4,5},{5,6},{6,7},{8,9},{9,10},{10,11},{12,13},{... | collective-permute-start | bytes 122888 | tf_op jit(solution)/shard_map/ppermute | solution.py:21
  16.8 1.9 %collective-permute-start.3 = (bf16[20,2,512]{2,1,0:T(2,128)(2,1)S(1)}, bf16[20,2,512]{2,1,0:T(2,128)(2,1)S(1)}, u32[]{:S(2)}, u32[]{:S(2)}) collective-permute-start(bf16[20,2,512]{2,1,0:T(2,128)(2,1)S(1)} %get-tuple-element.52), channel_id=1, source_target_pairs={{1,0},{2,1},{3,2},{5,4},{6,5},{7,6},{9,8},{10,9},{11,10},{13,12},{... | collective-permute-start | bytes 122888 | tf_op jit(solution)/shard_map/ppermute | solution.py:21
  18.7 0.0 collective-permute-done.2.left
  18.7 3.4 %collective-permute-done.3.right = bf16[20,2,512]{2,1,0:T(2,128)(2,1)S(1)} collective-permute-done((bf16[20,2,512]{2,1,0:T(2,128)(2,1)S(1)}, bf16[20,2,512]{2,1,0:T(2,128)(2,1)S(1)}, u32[]{:S(2)}, u32[]{:S(2)}) %collective-permute-start.3) | collective-permute-done | bytes 40992 | tf_op jit(solution)/shard_map/ppermute | solution.py:21
  22.1 0.0 copy-done.6
  22.1 0.0 copy-done.5
  22.1 0.0 copy-done.4
  22.1 0.0 copy-done.3
  22.1 0.0 copy-done
  22.1 14.8 %bricks.1 = (bf16[4,8,8,512]{3,2,1,0:T(8,128)(2,1)}, bf16[640,512]{1,0:T(8,128)(2,1)}, f32[4,8,8,512]{3,2,1,0:T(8,128)}, bf16[28,64,128]{2,1,0:T(8,128)(2,1)}, f...) custom-call(s32[12]{0:T(128)S(1)} %get-tuple-element.56.slots, ...), custom_call_target="tpu_custom_call", output_to_operand_aliasing={{4}: (4, {}), {5}: (5, {})} | custom-call | tf_op jit(solution)/shard_map/bricks/pallas_call | solution.py:448
  37.0 0.0 copy-done.1
  37.0 3.9 %all-to-all-start = ((bf16[32,56,128]{2,1,0:T(8,128)(2,1)}), bf16[32,56,128]{2,1,0:T(8,128)(2,1)S(1)}, u32[]{:S(2)}, u32[]{:S(2)}) async-start(bf16[32,56,128]{2,1,0:T(8,128)(2,1)} %bitcast.11), calls=%async_computation | async-start | bytes 917504 | tf_op jit(solution)/shard_map/all_to_all | solution.py:772
  40.9 7.0 %inputs.1 = (bf16[16,64,512]{2,1,0:T(8,128)(2,1)}, bf16[2,72,512]{2,1,0:T(8,128)(2,1)S(1)}, bf16[2,72,512]{2,1,0:T(8,128)(2,1)S(1)}, bf16[16,2,512]{2,1,0:T(2,128)(2,1)S(1)}, bf16[16,2,512]{2,1,0:T(2,128)(2,1)S(1)}) custom-call(s32[12]{0:T(128)S(1)} %get-tuple-element.56.slots, bf16[640,512]{1,0:T(8,128)(2,1)} %get-tuple-element.57.errors, ...), custom_call_target="tpu_custom_call" | custom-call | tf_op jit(solution)/shard_map/inputs/pallas_call | solution.py:561
  47.9 0.0 copy-start.7
  47.9 0.6 copy-done.7
  48.6 0.0 copy-start.8
  48.6 0.7 copy-done.8
  49.2 4.4 %all-to-all-done.got = bf16[32,56,128]{2,1,0:T(8,128)(2,1)S(1)} async-done(((bf16[32,56,128]{2,1,0:T(8,128)(2,1)}), bf16[32,56,128]{2,1,0:T(8,128)(2,1)S(1)}, u32[]{:S(2)}, u32[]{:S(2)}) %all-to-all-start) | async-done | bytes 458784 | tf_op jit(solution)/shard_map/all_to_all | solution.py:772
  53.7 0.9 part.1
  54.5 4.4 %all-to-all-start.1 = ((bf16[32,56,128]{2,1,0:T(8,128)(2,1)}), bf16[32,56,128]{2,1,0:T(8,128)(2,1)S(1)}, u32[]{:S(2)}, u32[]{:S(2)}) async-start(bf16[32,56,128]{2,1,0:T(8,128)(2,1)} %part.1), calls=%async_computation.1 | async-start | bytes 917504 | tf_op jit(solution)/shard_map/all_to_all | solution.py:780
  58.9 3.1 %collective-permute-start.4 = (bf16[2,72,512]{2,1,0:T(8,128)(2,1)}, bf16[2,72,512]{2,1,0:T(8,128)(2,1)S(1)}, u32[]{:S(2)}, u32[]{:S(2)}) collective-permute-start(bf16[2,72,512]{2,1,0:T(8,128)(2,1)} %copy-done.8), channel_id=1, source_target_pairs={{0,4},{4,8},{8,12},{12,16},{16,20},{20,24},{24,28},{1,5},{5,9},{9,... | collective-permute-start | bytes 442376 | tf_op jit(solution)/shard_map/ppermute | solution.py:21
  62.0 3.1 %collective-permute-start.5 = (bf16[2,72,512]{2,1,0:T(8,128)(2,1)}, bf16[2,72,512]{2,1,0:T(8,128)(2,1)S(1)}, u32[]{:S(2)}, u32[]{:S(2)}) collective-permute-start(bf16[2,72,512]{2,1,0:T(8,128)(2,1)} %copy-done.7), channel_id=1, source_target_pairs={{4,0},{8,4},{12,8},{16,12},{20,16},{24,20},{28,24},{5,1},{9,5},{13... | collective-permute-start | bytes 442376 | tf_op jit(solution)/shard_map/ppermute | solution.py:21
  65.1 9.1 %collective-permute-done.4.from_above = bf16[2,72,512]{2,1,0:T(8,128)(2,1)S(1)} collective-permute-done((bf16[2,72,512]{2,1,0:T(8,128)(2,1)}, bf16[2,72,512]{2,1,0:T(8,128)(2,1)S(1)}, u32[]{:S(2)}, u32[]{:S(2)}) %collective-permute-start.4) | collective-permute-done | bytes 147488 | tf_op jit(solution)/shard_map/ppermute | solution.py:21
  74.3 0.0 collective-permute-done.5.from_below
  74.3 3.8 %collective-permute-start.6 = (bf16[16,2,512]{2,1,0:T(2,128)(2,1)S(1)}, bf16[16,2,512]{2,1,0:T(2,128)(2,1)S(1)}, u32[]{:S(2)}, u32[]{:S(2)}) collective-permute-start(bf16[16,2,512]{2,1,0:T(2,128)(2,1)S(1)} %get-tuple-element.69), channel_id=1, source_target_pairs={{0,1},{1,2},{2,3},{4,5},{5,6},{6,7},{8,9},{9,10},{10,11},{12,13},{... | collective-permute-start | bytes 98312 | tf_op jit(solution)/shard_map/ppermute | solution.py:21
  78.1 1.9 %collective-permute-start.7 = (bf16[16,2,512]{2,1,0:T(2,128)(2,1)S(1)}, bf16[16,2,512]{2,1,0:T(2,128)(2,1)S(1)}, u32[]{:S(2)}, u32[]{:S(2)}) collective-permute-start(bf16[16,2,512]{2,1,0:T(2,128)(2,1)S(1)} %get-tuple-element.70), channel_id=1, source_target_pairs={{1,0},{2,1},{3,2},{5,4},{6,5},{7,6},{9,8},{10,9},{11,10},{13,12},{... | collective-permute-start | bytes 98312 | tf_op jit(solution)/shard_map/ppermute | solution.py:21
  80.0 0.0 collective-permute-done.6.from_left
  80.0 3.3 %collective-permute-done.7.from_right = bf16[16,2,512]{2,1,0:T(2,128)(2,1)S(1)} collective-permute-done((bf16[16,2,512]{2,1,0:T(2,128)(2,1)S(1)}, bf16[16,2,512]{2,1,0:T(2,128)(2,1)S(1)}, u32[]{:S(2)}, u32[]{:S(2)}) %collective-permute-start.7) | collective-permute-done | bytes 32800 | tf_op jit(solution)/shard_map/ppermute | solution.py:21
  83.3 0.0 copy-start.2
  83.3 0.9 %copy-done.2 = bf16[2,64,512]{2,1,0:T(8,128)(2,1)S(1)} copy-done((bf16[2,64,512]{2,1,0:T(8,128)(2,1)S(1)}, bf16[2,64,512]{2,1,0:T(8,128)(2,1)}, u32[]{:S(2)}) %copy-start.2) | copy-done | bytes 131096
  84.2 4.0 %join.1 = (bf16[16,64,512]{2,1,0:T(8,128)(2,1)}, bf16[16,64,512]{2,1,0:T(8,128)(2,1)}) custom-call(s32[12]{0:T(128)S(1)} %get-tuple-element.56.slots, bf16[16,64,512]{2,1,0:T(8,128)(2,1)} %get-tuple-element.63.grads, bf16[4,8,8,512]{3,2,1,0:T(8,128)(2,1)} %get-tuple-element.64.results, ...), custom_call_target="tpu_custom_call", output_to_operand_aliasing={{0}: (1, {})} | custom-call | tf_op jit(solution)/shard_map/join/pallas_call | solution.py:683
  88.3 0.0 all-to-all-done.1
  88.3 1.4 %sums.1 = (f32[27,64,64]{2,1,0:T(8,128)}, f32[27,64,64]{2,1,0:T(8,128)}) custom-call(bf16[1792,128]{1,0:T(8,128)(2,1)S(1)} %bitcast.6), custom_call_target="tpu_custom_call" | custom-call | tf_op jit(solution)/shard_map/sums/pallas_call | solution.py:735
  (2 shorter events, 0.0 us)
Async XLA Ops:
  0.6 21.5 %copy-start.6 = (f32[64]{0:T(128)S(1)}, f32[64]{0:T(128)}, u32[]{:S(2)}) copy-start(f32[64]{0:T(128)} %param.19) | copy-start | bytes 772
  0.6 21.5 %copy-start.5 = (f32[64]{0:T(128)S(1)}, f32[64]{0:T(128)}, u32[]{:S(2)}) copy-start(f32[64]{0:T(128)} %param.18) | copy-start | bytes 772
  0.7 21.4 %copy-start.4 = (f32[64]{0:T(128)S(1)}, f32[64]{0:T(128)}, u32[]{:S(2)}) copy-start(f32[64]{0:T(128)} %param.17) | copy-start | bytes 772
  0.7 21.4 %copy-start.3 = (f32[64]{0:T(128)S(1)}, f32[64]{0:T(128)}, u32[]{:S(2)}) copy-start(f32[64]{0:T(128)} %param.16) | copy-start | bytes 772
  0.7 21.4 %copy-start = (bf16[16,64,512]{2,1,0:T(8,128)(2,1)S(1)}, bf16[16,64,512]{2,1,0:T(8,128)(2,1)}, u32[]{:S(2)}) copy-start(bf16[16,64,512]{2,1,0:T(8,128)(2,1)} %cotangent.1) | copy-start | bytes 3145732
  2.0 35.0 %copy-start.1 = (bf16[2,64,512]{2,1,0:T(8,128)(2,1)}, bf16[2,64,512]{2,1,0:T(8,128)(2,1)S(1)}, u32[]{:S(2)}) copy-start(bf16[2,64,512]{2,1,0:T(8,128)(2,1)S(1)} %get-tuple-element.47.bottom) | copy-start | bytes 393220
  2.0 10.4 %collective-permute-start = (bf16[2,64,512]{2,1,0:T(8,128)(2,1)S(1)}, bf16[2,64,512]{2,1,0:T(8,128)(2,1)S(1)}, u32[]{:S(2)}, u32[]{:S(2)}) collective-permute-start(bf16[2,64,512]{2,1,0:T(8,128)(2,1)S(1)} %get-tuple-element.47.bottom), channel_id=1, source_target_pairs={{0,4},{4,8},{8,12},{12,16},{16,20},{20,24},{24,28},{1,5},{5,9},{9,... | collective-permute-start | bytes 393224 | tf_op jit(solution)/shard_map/ppermute | solution.py:21
  5.1 7.3 %collective-permute-start.1 = (bf16[2,64,512]{2,1,0:T(8,128)(2,1)S(1)}, bf16[2,64,512]{2,1,0:T(8,128)(2,1)S(1)}, u32[]{:S(2)}, u32[]{:S(2)}) collective-permute-start(bf16[2,64,512]{2,1,0:T(8,128)(2,1)S(1)} %get-tuple-element.48.top), channel_id=1, source_target_pairs={{4,0},{8,4},{12,8},{16,12},{20,16},{24,20},{28,24},{5,1},{9,5},{13... | collective-permute-start | bytes 393224 | tf_op jit(solution)/shard_map/ppermute | solution.py:21
  12.5 6.2 %collective-permute-start.2 = (bf16[20,2,512]{2,1,0:T(2,128)(2,1)S(1)}, bf16[20,2,512]{2,1,0:T(2,128)(2,1)S(1)}, u32[]{:S(2)}, u32[]{:S(2)}) collective-permute-start(bf16[20,2,512]{2,1,0:T(2,128)(2,1)S(1)} %get-tuple-element.51), channel_id=1, source_target_pairs={{0,1},{1,2},{2,3},{4,5},{5,6},{6,7},{8,9},{9,10},{10,11},{12,13},{... | collective-permute-start | bytes 122888 | tf_op jit(solution)/shard_map/ppermute | solution.py:21
  16.8 5.3 %collective-permute-start.3 = (bf16[20,2,512]{2,1,0:T(2,128)(2,1)S(1)}, bf16[20,2,512]{2,1,0:T(2,128)(2,1)S(1)}, u32[]{:S(2)}, u32[]{:S(2)}) collective-permute-start(bf16[20,2,512]{2,1,0:T(2,128)(2,1)S(1)} %get-tuple-element.52), channel_id=1, source_target_pairs={{1,0},{2,1},{3,2},{5,4},{6,5},{7,6},{9,8},{10,9},{11,10},{13,12},{... | collective-permute-start | bytes 122888 | tf_op jit(solution)/shard_map/ppermute | solution.py:21
  37.0 16.7 %all-to-all-start = ((bf16[32,56,128]{2,1,0:T(8,128)(2,1)}), bf16[32,56,128]{2,1,0:T(8,128)(2,1)S(1)}, u32[]{:S(2)}, u32[]{:S(2)}) async-start(bf16[32,56,128]{2,1,0:T(8,128)(2,1)} %bitcast.11), calls=%async_computation | async-start | bytes 917504 | tf_op jit(solution)/shard_map/all_to_all | solution.py:772
  47.9 0.7 copy-start.7
  48.6 0.7 copy-start.8
  54.5 33.7 %all-to-all-start.1 = ((bf16[32,56,128]{2,1,0:T(8,128)(2,1)}), bf16[32,56,128]{2,1,0:T(8,128)(2,1)S(1)}, u32[]{:S(2)}, u32[]{:S(2)}) async-start(bf16[32,56,128]{2,1,0:T(8,128)(2,1)} %part.1), calls=%async_computation.1 | async-start | bytes 917504 | tf_op jit(solution)/shard_map/all_to_all | solution.py:780
  58.9 15.3 %collective-permute-start.4 = (bf16[2,72,512]{2,1,0:T(8,128)(2,1)}, bf16[2,72,512]{2,1,0:T(8,128)(2,1)S(1)}, u32[]{:S(2)}, u32[]{:S(2)}) collective-permute-start(bf16[2,72,512]{2,1,0:T(8,128)(2,1)} %copy-done.8), channel_id=1, source_target_pairs={{0,4},{4,8},{8,12},{12,16},{16,20},{20,24},{24,28},{1,5},{5,9},{9,... | collective-permute-start | bytes 442376 | tf_op jit(solution)/shard_map/ppermute | solution.py:21
  62.0 12.2 %collective-permute-start.5 = (bf16[2,72,512]{2,1,0:T(8,128)(2,1)}, bf16[2,72,512]{2,1,0:T(8,128)(2,1)S(1)}, u32[]{:S(2)}, u32[]{:S(2)}) collective-permute-start(bf16[2,72,512]{2,1,0:T(8,128)(2,1)} %copy-done.7), channel_id=1, source_target_pairs={{4,0},{8,4},{12,8},{16,12},{20,16},{24,20},{28,24},{5,1},{9,5},{13... | collective-permute-start | bytes 442376 | tf_op jit(solution)/shard_map/ppermute | solution.py:21
  74.3 5.7 %collective-permute-start.6 = (bf16[16,2,512]{2,1,0:T(2,128)(2,1)S(1)}, bf16[16,2,512]{2,1,0:T(2,128)(2,1)S(1)}, u32[]{:S(2)}, u32[]{:S(2)}) collective-permute-start(bf16[16,2,512]{2,1,0:T(2,128)(2,1)S(1)} %get-tuple-element.69), channel_id=1, source_target_pairs={{0,1},{1,2},{2,3},{4,5},{5,6},{6,7},{8,9},{9,10},{10,11},{12,13},{... | collective-permute-start | bytes 98312 | tf_op jit(solution)/shard_map/ppermute | solution.py:21
  78.1 5.2 %collective-permute-start.7 = (bf16[16,2,512]{2,1,0:T(2,128)(2,1)S(1)}, bf16[16,2,512]{2,1,0:T(2,128)(2,1)S(1)}, u32[]{:S(2)}, u32[]{:S(2)}) collective-permute-start(bf16[16,2,512]{2,1,0:T(2,128)(2,1)S(1)} %get-tuple-element.70), channel_id=1, source_target_pairs={{1,0},{2,1},{3,2},{5,4},{6,5},{7,6},{9,8},{10,9},{11,10},{13,12},{... | collective-permute-start | bytes 98312 | tf_op jit(solution)/shard_map/ppermute | solution.py:21
  83.3 0.9 %copy-start.2 = (bf16[2,64,512]{2,1,0:T(8,128)(2,1)S(1)}, bf16[2,64,512]{2,1,0:T(8,128)(2,1)}, u32[]{:S(2)}) copy-start(bf16[2,64,512]{2,1,0:T(8,128)(2,1)} %copy-done.1) | copy-start | bytes 393220
